TPU v7x, 256 devices: a whole 4x4x8 slice. The times are simulated.
256 devices in a mesh: grp: 4 (over y), wide: 64 (over z, x, core).
Axes of the slice: x: 4, y: 4, z: 8, core: 2. Of those that a mesh axis runs over, the one named last changes fastest.
Arguments:
- tiles: bfloat16 [12288, 256, 256], P(('grp', 'wide')), may hold values from -0.59765625 to 0.59765625
- contraction: int32 [12288], P(('grp', 'wide')), may hold values from 0 to 15
- row_tile: int32 [12288], P(('grp', 'wide')), may hold values from 0 to 255, as said below
- owner_map: int32 [256], replicated, may hold values from 0 to 255, as said below
- panel: bfloat16 [4096, 768], P('grp'), may hold values from -0.5390625 to 0.5390625
Outputs:
- column_block: float32 [65536, 768], P('wide')
Inputs may be any that keep to these rules, and one draw needn't show every extreme that they name: `row_tile`: every row tile's owner is owner_map // 4; among the 48 contributions of one device at most 2 have row tiles of one owner, and on every device some owner gets exactly 2. `owner_map`: A permutation of the row tiles.
All inputs are finite; a program needn't handle non-finite values.
Results may differ from a plain program's by a relative error of at most 0.0003.
Values may be sent and summed in bfloat16 or wider, within the bound.
A program may use at most 192 MiB of HBM per device.

v0:
```python
import math

import jax
import jax.numpy as jnp
from jax import lax
from jax.sharding import PartitionSpec as P


def place_slots(row_ids, owner_map, out_dev):
    table_ids = jnp.arange(owner_map.shape[0], dtype=jnp.int32)
    position = jnp.sum(jnp.where(row_ids[..., None] == table_ids, owner_map, 0), axis=-1)
    target = position // out_dev
    serial = jnp.arange(row_ids.shape[-1], dtype=jnp.int32)
    earlier = (target[..., :, None] == target[..., None, :]) & (serial[:, None] > serial[None, :])
    ranking = jnp.sum(earlier.astype(jnp.int32), axis=-1)
    return (position % out_dev, target, ranking)


def add_products(summed, arrived, slot_labels, panel_tiles):
    slot_count = arrived.shape[0]
    block_rows = math.gcd(slot_count, 32)
    out_dev = summed.shape[0]
    local_ids = jnp.arange(out_dev, dtype=jnp.int32)

    def one_block(which_block, running, source_tiles, source_labels):
        part_tiles = lax.dynamic_slice_in_dim(source_tiles, which_block * block_rows, block_rows, 0)
        part_labels = lax.dynamic_slice_in_dim(
            source_labels, which_block * block_rows, block_rows, 0
        )
        chosen = jnp.take(panel_tiles, part_labels[:, 1], axis=0)
        products = jnp.einsum(
            "sab,sbc->sac", part_tiles, chosen, preferred_element_type=jnp.float32
        )
        row_hits = (part_labels[:, 0][:, None] == local_ids[None, :]).astype(jnp.float32)
        return running + jnp.einsum(
            "sr,sac->rac", row_hits, products, precision=lax.Precision.HIGHEST
        )

    return lax.fori_loop(
        0,
        slot_count // block_rows,
        lambda which_block, running: one_block(which_block, running, arrived, slot_labels),
        summed,
    )


def per_device(tiles, contraction, row_tile, owner_map, panel):
    wide_count = lax.axis_size("wide")
    tile_dev = tiles.shape[0]
    tile_side = tiles.shape[1]
    out_dev = owner_map.shape[0] // wide_count
    most_slots = tile_dev * 8 // (3 * wide_count)
    slot_total = wide_count * most_slots
    local_row, target, ranking = place_slots(row_tile, owner_map, out_dev)
    slot_index = target * most_slots + ranking
    outgoing = jnp.zeros((slot_total, tile_side, tile_side), tiles.dtype).at[slot_index].set(tiles)
    all_rows, all_contraction = (
        lax.all_gather(row_tile, "wide", axis=0, tiled=True),
        lax.all_gather(contraction, "wide", axis=0, tiled=True),
    )
    all_rows = all_rows.reshape(wide_count, tile_dev)
    all_contraction = all_contraction.reshape(wide_count, tile_dev)
    source_local, source_target, source_rank = place_slots(all_rows, owner_map, out_dev)
    source_ids = jnp.arange(wide_count, dtype=jnp.int32)
    mine = source_target == lax.axis_index("wide")
    arrive_index = jnp.where(mine, source_ids[:, None] * most_slots + source_rank, slot_total)
    label_pairs = jnp.stack([source_local, all_contraction], axis=-1).reshape(
        wide_count * tile_dev, 2
    )
    vacant_label = jnp.stack(
        [jnp.full((slot_total,), out_dev, jnp.int32), jnp.zeros((slot_total,), jnp.int32)], axis=1
    )
    arrived_labels = vacant_label.at[arrive_index.reshape(-1)].set(label_pairs, mode="drop")
    gathered = lax.all_gather(panel, "grp", axis=0, tiled=True)
    panel_tiles = gathered.reshape(gathered.shape[0] // tile_side, tile_side, gathered.shape[1])
    summed = jnp.zeros((out_dev, tile_side, gathered.shape[1]), jnp.float32)
    arrived = lax.all_to_all(outgoing, "wide", split_axis=0, concat_axis=0, tiled=True)
    summed = add_products(summed, arrived, arrived_labels, panel_tiles)
    summed = lax.psum(summed, "grp")
    return summed.reshape(out_dev * tile_side, gathered.shape[1])


def solution(mesh):
    return jax.shard_map(
        per_device,
        mesh=mesh,
        in_specs=(
            P(("grp", "wide"), None, None),
            P(("grp", "wide")),
            P(("grp", "wide")),
            P(),
            P("grp", None),
        ),
        out_specs=P("wide", None),
        check_vma=False,
    )
```

profile of v0, /device:TPU:36, one launch (start us, length us, event | category | flops | bytes accessed | tf_op | source)
XLA Modules:
  0.0 973.2 jit_solution(2914574177467141061)
XLA Ops:
  6.5 0.9 select_reduce_fusion.1
  7.4 0.2 convert_reduce_fusion.1
  7.6 5.9 broadcast_in_dim.68
  13.5 16.7 %scatter_fusion.1 = bf16[128,256,256]{2,1,0:T(8,128)(2,1)} fusion(bf16[128,256,256]{2,1,0:T(8,128)(2,1)} %broadcast_in_dim.68, s32[48]{0:T(128)S(1)} %fusion.19, bf16[48,256,256]{2,1,0:T(8,128)(2,1)} %param.7), kind=kCustom, calls=%fused_computation.2 | custom fusion | bytes 18874560 | tf_op jit(solution)/shard_map/scatter | solution.py:56
  30.3 0.0 copy-start.4
  30.3 0.0 copy-start.2
  30.3 0.0 copy-start.3
  30.3 0.0 copy-start.1
  30.3 11.9 %all-to-all-start = ((bf16[128,256,256]{2,1,0:T(8,128)(2,1)}), bf16[128,256,256]{2,1,0:T(8,128)(2,1)}, u32[]{:S(2)}, u32[]{:S(2)}) async-start(bf16[128,256,256]{2,1,0:T(8,128)(2,1)} %scatter_fusion.1), calls=%async_computation | async-start | bytes 33554432 | tf_op jit(solution)/shard_map/all_to_all | solution.py:77
  42.2 0.0 copy-start
  42.2 0.0 all-gather.2.cloned.1.call-start
  42.3 0.7 all-gather.2.cloned.1.call-update
  42.9 0.0 all-reduce.5.cloned.1.call-start
  43.0 0.0 copy-done.4
  43.0 0.6 dynamic-slice
  44.3 0.0 copy-done.2
  44.3 0.3 dynamic-update-slice
  44.6 0.0 copy-done.3
  44.6 0.3 dynamic-update-slice.1
  44.8 565.9 %all-reduce.2 = (s32[3072]{0:T(1024)S(1)}, s32[3072]{0:T(1024)S(1)}) all-reduce(s32[3072]{0:T(1024)S(1)} %dynamic-update-slice, s32[3072]{0:T(1024)S(1)} %dynamic-update-slice.1), channel_id=1, replica_groups=mesh['grp'=4,'wide'=64] {'wide'}, use_global_device_ids=true, to_apply=%add | all-reduce | flops 6144 | bytes 49152
  610.7 0.1 eq.107
  610.8 0.0 copy-done.1
  610.8 1.7 select_reduce_fusion
  612.5 0.1 reduce_sum.43
  612.7 0.1 copy.11
  612.8 0.5 convert_reduce_fusion
  613.3 0.1 copy.13
  613.3 0.1 add.152
  613.5 0.1 and_select_fusion
  613.6 1.7 copy.14
  615.3 0.0 copy-done
  615.3 8.5 scatter_fusion
  623.8 0.1 copy.15
  623.8 0.0 all-gather.2.cloned.1.call-done
  623.8 0.0 all-to-all-done
  623.8 230.9 %while.14 = (s32[]{:T(128)}, f32[4,256,768]{2,0,1:T(4,128)S(1)}, s32[128,2]{0,1:T(2,128)S(1)}, bf16[128,256,256]{2,1,0:T(8,128)(2,1)}, bf16[16,256,768]{2,1,0:T(...) while((s32[]{:T(128)}, f32[4,256,768]{2,0,1:T(4,128)S(1)}, ...), condition=%wide.region_7.8_spmd.clone, body=%wide.region_6.7_spmd.clone.sunk | while | flops 3531081216 | bytes 98572000 | solution.py:39
  624.0 0.1 constant_dynamic-slice_fusion.2
  624.1 9.1 gather_fusion
  633.2 17.7 %fusion.29 = f32[32,256,768]{2,1,0:T(8,128)} fusion(bf16[32,256,768]{2,1,0:T(8,128)(2,1)} %gather_fusion, pred[32]{0:T(512)(128)(4,1)S(1)} %and_bitcast_fusion.2, bf16[128,256,256]{2,1,0:T(8,128)(2,1)} %get-tuple-element.217, s32[]{:T(128)S(6)} %select_n.171), kind=kOutput, calls=%fused_computation.6.clone.1 | convolution fusion | flops 3227516928 | bytes 41943076 | tf_op jit(solution)/shard_map/while/body/eval_jaxpr/sab,sbc->sac/dot_general | solution.py:31
  650.9 30.7 %select_add_fusion.2 = f32[4,256,768]{2,0,1:T(4,128)S(1)} fusion(f32[4,256,768]{2,0,1:T(4,128)S(1)} %get-tuple-element.206, pred[]{:T(512)S(6)} %compare.49, f32[32,256,768]{2,1,0:T(8,128)} %fusion.29, s32[32]{0:T(128)S(1)} %get-tuple-element.195), kind=kOutput, calls=%fused_computation.11.clone.1 | convolution fusion | flops 303562880 | bytes 31457408 | tf_op jit(solution)/shard_map/while/body/eval_jaxpr/sr,sac->rac/dot_general | solution.py:35
  681.7 0.1 constant_dynamic-slice_fusion.2
  681.8 9.2 gather_fusion
  690.9 17.7 %fusion.29 = f32[32,256,768]{2,1,0:T(8,128)} fusion(bf16[32,256,768]{2,1,0:T(8,128)(2,1)} %gather_fusion, pred[32]{0:T(512)(128)(4,1)S(1)} %and_bitcast_fusion.2, bf16[128,256,256]{2,1,0:T(8,128)(2,1)} %get-tuple-element.217, s32[]{:T(128)S(6)} %select_n.171), kind=kOutput, calls=%fused_computation.6.clone.1 | convolution fusion | flops 3227516928 | bytes 41943076 | tf_op jit(solution)/shard_map/while/body/eval_jaxpr/sab,sbc->sac/dot_general | solution.py:31
  708.6 30.7 %select_add_fusion.2 = f32[4,256,768]{2,0,1:T(4,128)S(1)} fusion(f32[4,256,768]{2,0,1:T(4,128)S(1)} %get-tuple-element.206, pred[]{:T(512)S(6)} %compare.49, f32[32,256,768]{2,1,0:T(8,128)} %fusion.29, s32[32]{0:T(128)S(1)} %get-tuple-element.195), kind=kOutput, calls=%fused_computation.11.clone.1 | convolution fusion | flops 303562880 | bytes 31457408 | tf_op jit(solution)/shard_map/while/body/eval_jaxpr/sr,sac->rac/dot_general | solution.py:35
  739.4 0.1 constant_dynamic-slice_fusion.2
  739.5 9.1 gather_fusion
  748.6 17.7 %fusion.29 = f32[32,256,768]{2,1,0:T(8,128)} fusion(bf16[32,256,768]{2,1,0:T(8,128)(2,1)} %gather_fusion, pred[32]{0:T(512)(128)(4,1)S(1)} %and_bitcast_fusion.2, bf16[128,256,256]{2,1,0:T(8,128)(2,1)} %get-tuple-element.217, s32[]{:T(128)S(6)} %select_n.171), kind=kOutput, calls=%fused_computation.6.clone.1 | convolution fusion | flops 3227516928 | bytes 41943076 | tf_op jit(solution)/shard_map/while/body/eval_jaxpr/sab,sbc->sac/dot_general | solution.py:31
  766.3 30.7 %select_add_fusion.2 = f32[4,256,768]{2,0,1:T(4,128)S(1)} fusion(f32[4,256,768]{2,0,1:T(4,128)S(1)} %get-tuple-element.206, pred[]{:T(512)S(6)} %compare.49, f32[32,256,768]{2,1,0:T(8,128)} %fusion.29, s32[32]{0:T(128)S(1)} %get-tuple-element.195), kind=kOutput, calls=%fused_computation.11.clone.1 | convolution fusion | flops 303562880 | bytes 31457408 | tf_op jit(solution)/shard_map/while/body/eval_jaxpr/sr,sac->rac/dot_general | solution.py:35
  797.1 0.1 constant_dynamic-slice_fusion.2
  797.1 9.1 gather_fusion
  806.3 17.7 %fusion.29 = f32[32,256,768]{2,1,0:T(8,128)} fusion(bf16[32,256,768]{2,1,0:T(8,128)(2,1)} %gather_fusion, pred[32]{0:T(512)(128)(4,1)S(1)} %and_bitcast_fusion.2, bf16[128,256,256]{2,1,0:T(8,128)(2,1)} %get-tuple-element.217, s32[]{:T(128)S(6)} %select_n.171), kind=kOutput, calls=%fused_computation.6.clone.1 | convolution fusion | flops 3227516928 | bytes 41943076 | tf_op jit(solution)/shard_map/while/body/eval_jaxpr/sab,sbc->sac/dot_general | solution.py:31
  823.9 30.7 %select_add_fusion.2 = f32[4,256,768]{2,0,1:T(4,128)S(1)} fusion(f32[4,256,768]{2,0,1:T(4,128)S(1)} %get-tuple-element.206, pred[]{:T(512)S(6)} %compare.49, f32[32,256,768]{2,1,0:T(8,128)} %fusion.29, s32[32]{0:T(128)S(1)} %get-tuple-element.195), kind=kOutput, calls=%fused_computation.11.clone.1 | convolution fusion | flops 303562880 | bytes 31457408 | tf_op jit(solution)/shard_map/while/body/eval_jaxpr/sr,sac->rac/dot_general | solution.py:35
  854.7 2.2 copy.16
  856.9 0.0 all-reduce.5.cloned.1.call-update
  857.0 105.6 %all-reduce.5.cloned.1.call-done = f32[1024,768]{1,0:T(8,128)} async-done(((f32[1024,768]{1,0:T(8,128)}), f32[1024,768]{1,0:T(8,128)}) %all-reduce.5.cloned.1.call-update) | async-done | bytes 3145744 | tf_op jit(solution)/shard_map/psum | solution.py:79
  962.6 3.8 copy.38
  (22 shorter events, 0.2 us)
Async XLA Ops:
  30.3 12.7 %copy-start.4 = (u32[256]{0:T(256)S(1)}, u32[256]{0:T(256)}, u32[]{:S(2)}) copy-start(u32[256]{0:T(256)} %constant.118) | copy-start | bytes 3076
  30.3 14.0 %copy-start.2 = (s32[48]{0:T(128)S(1)}, s32[48]{0:T(128)}, u32[]{:S(2)}) copy-start(s32[48]{0:T(128)} %param.9) | copy-start | bytes 580
  30.3 14.3 %copy-start.3 = (s32[48]{0:T(128)S(1)}, s32[48]{0:T(128)}, u32[]{:S(2)}) copy-start(s32[48]{0:T(128)} %param.8) | copy-start | bytes 580
  30.3 580.5 %copy-start.1 = (s32[256]{0:T(256)S(1)}, s32[256]{0:T(256)}, u32[]{:S(2)}) copy-start(s32[256]{0:T(256)} %param.10) | copy-start | bytes 3076
  30.3 593.5 %all-to-all-start = ((bf16[128,256,256]{2,1,0:T(8,128)(2,1)}), bf16[128,256,256]{2,1,0:T(8,128)(2,1)}, u32[]{:S(2)}, u32[]{:S(2)}) async-start(bf16[128,256,256]{2,1,0:T(8,128)(2,1)} %scatter_fusion.1), calls=%async_computation | async-start | bytes 33554432 | tf_op jit(solution)/shard_map/all_to_all | solution.py:77
  42.2 573.1 %copy-start = (s32[128,2]{1,0:T(8,128)S(1)}, s32[128,2]{1,0:T(8,128)}, u32[]{:S(2)}) copy-start(s32[128,2]{1,0:T(8,128)} %constant.110.clone.1) | copy-start | bytes 3076
  42.2 581.6 %all-gather.2.cloned.1.call-start = ((), (), s32[]{:S(2)}) async-start(), calls=%async_computation.1 | async-start | bytes 7864320 | tf_op jit(solution)/shard_map/all_gather | solution.py:74
  42.9 919.7 %all-reduce.5.cloned.1.call-start = ((), (), s32[]{:S(2)}) async-start(), calls=%async_computation.2 | async-start | bytes 6291456 | tf_op jit(solution)/shard_map/psum | solution.py:79
Sparse Core Ops, SparseCore 0:
  44.9 69.5 all-gather.1
  857.1 105.4 all-reduce.4
where the time goes:
time: 975 us; the launch traced here: 973 us
  blocking collectives  566 us (58%)
  matrix products  194 us (20%)
  waiting for transfers between devices  106 us (11%)
  local copies, waits for them, and re-layouts  77.2 us (8%)
  between operations  14.2 us (1%)
  starting transfers between devices  12 us (1%)
    unnamed x1, blocking collectives  566 us
    dot_general x4, matrix products, one_block(): jnp.einsum('sr,sac->rac', row_hits, products, precision=lax.Precision.HIG...  123 us
    psum x1, waiting for transfers between devices, per_device(): summed = lax.psum(summed, 'grp')  106 us
    dot_general x4, matrix products, one_block(): jnp.einsum('sab,sbc->sac', part_tiles, chosen, preferred_element_type=jnp...  70.7 us
    gather x4, local copies, waits for them, and re-layouts, one_block(): chosen = jnp.take(panel_tiles, part_labels[:, 1], axis=0)  36.5 us
  transfers between devices with their start and end apart: 3, of which 1 were waited for; matrix products, arithmetic and copies ran while one was open for 1% of the time, Pallas kernels for 0%

commit v1 on v0

v1 whole, which is shorter than its diff:
```python
import jax
import jax.numpy as jnp
from jax import lax
from jax.experimental import pallas as pl
from jax.experimental.pallas import tpu as pltpu
from jax.sharding import PartitionSpec as P


def place_slots(row_ids, owner_map, out_dev):
    table_ids = jnp.arange(owner_map.shape[0], dtype=jnp.int32)
    position = jnp.sum(jnp.where(row_ids[..., None] == table_ids, owner_map, 0), axis=-1)
    target = position // out_dev
    serial = jnp.arange(row_ids.shape[-1], dtype=jnp.int32)
    earlier = (target[..., :, None] == target[..., None, :]) & (serial[:, None] > serial[None, :])
    ranking = jnp.sum(earlier.astype(jnp.int32), axis=-1)
    return (position % out_dev, target, ranking)


def products_kernel(count_ref, order_ref, rows_ref, ks_ref, arrived_hbm, panel_ref, out_ref, buf, sem):
    out_ref[...] = jnp.zeros_like(out_ref)
    count = count_ref[0]
    columns = panel_ref.shape[2]
    side = buf.shape[2]

    def fetch(i, slot):
        return pltpu.make_async_copy(arrived_hbm.at[order_ref[i]], buf.at[slot], sem.at[slot])

    @pl.when(count > 0)
    def _():
        fetch(0, 0).start()

    def body(i, carry):
        slot = i % 2

        @pl.when(i + 1 < count)
        def _():
            fetch(i + 1, 1 - slot).start()

        fetch(i, slot).wait()
        source = order_ref[i]
        row = rows_ref[source]
        k = ks_ref[source]
        tile = buf[slot]
        for c in range(columns // side):
            cols = pl.ds(c * side, side)
            out_ref[row, :, cols] += jnp.dot(
                tile, panel_ref[k, :, cols], preferred_element_type=jnp.float32
            )
        return carry

    lax.fori_loop(0, count, body, 0)


def add_products(arrived, arrived_labels, panel_tiles, out_dev):
    slot_count, side = arrived.shape[0], arrived.shape[1]
    rows = arrived_labels[:, 0]
    ks = arrived_labels[:, 1]
    vacant = (rows >= out_dev).astype(jnp.int32)
    order = jnp.argsort(vacant, stable=True).astype(jnp.int32)
    count = jnp.reshape(slot_count - jnp.sum(vacant), (1,)).astype(jnp.int32)
    smem = pl.BlockSpec(memory_space=pltpu.SMEM)
    return pl.pallas_call(
        products_kernel,
        out_shape=jax.ShapeDtypeStruct((out_dev, side, panel_tiles.shape[2]), jnp.float32),
        in_specs=[smem, smem, smem, smem,
                  pl.BlockSpec(memory_space=pl.ANY),
                  pl.BlockSpec(memory_space=pltpu.VMEM)],
        out_specs=pl.BlockSpec(memory_space=pltpu.VMEM),
        scratch_shapes=[
            pltpu.VMEM((2, side, side), arrived.dtype),
            pltpu.SemaphoreType.DMA((2,)),
        ],
        compiler_params=pltpu.CompilerParams(vmem_limit_bytes=48 * 1024 * 1024),
    )(count, order, rows, ks, arrived, panel_tiles)


def per_device(tiles, contraction, row_tile, owner_map, panel):
    wide_count = lax.axis_size("wide")
    tile_dev = tiles.shape[0]
    tile_side = tiles.shape[1]
    out_dev = owner_map.shape[0] // wide_count
    most_slots = tile_dev * 8 // (3 * wide_count)
    slot_total = wide_count * most_slots
    local_row, target, ranking = place_slots(row_tile, owner_map, out_dev)
    slot_index = target * most_slots + ranking
    outgoing = jnp.zeros((slot_total, tile_side, tile_side), tiles.dtype).at[slot_index].set(tiles)
    vacant_label = jnp.stack(
        [jnp.full((slot_total,), out_dev, jnp.int32), jnp.zeros((slot_total,), jnp.int32)], axis=1
    )
    label_out = vacant_label.at[slot_index].set(jnp.stack([local_row, contraction], axis=1))
    arrived_labels = lax.all_to_all(label_out, "wide", split_axis=0, concat_axis=0, tiled=True)
    gathered = lax.all_gather(panel, "grp", axis=0, tiled=True)
    panel_tiles = gathered.reshape(gathered.shape[0] // tile_side, tile_side, gathered.shape[1])
    arrived = lax.all_to_all(outgoing, "wide", split_axis=0, concat_axis=0, tiled=True)
    summed = add_products(arrived, arrived_labels, panel_tiles, out_dev)
    summed = lax.psum(summed, "grp")
    return summed.reshape(out_dev * tile_side, gathered.shape[1])


def solution(mesh):
    return jax.shard_map(
        per_device,
        mesh=mesh,
        in_specs=(
            P(("grp", "wide"), None, None),
            P(("grp", "wide")),
            P(("grp", "wide")),
            P(),
            P("grp", None),
        ),
        out_specs=P("wide", None),
        check_vma=False,
    )
```

time: 975 us -> 590 us (0.61)
  blocking collectives: 566 us -> 0 us
  waiting for transfers between devices: 106 us -> 491 us
  matrix products: 194 us -> 0 us
  local copies, waits for them, and re-layouts: 77.2 us -> 29.4 us
  Pallas kernels: 0 us -> 25.9 us
  starting transfers between devices: 12 us -> 22.2 us
    unnamed x1 -> x0, blocking collectives: 566 us -> none
    all_to_all x1, waiting for transfers between devices: 0.01 us -> 300 us  [per_device(): lax.all_to_all(outgoing, 'wide', split_axis=0, concat_axis=0, tiled=True)]
    dot_general x8 -> x0, matrix products: 194 us -> none  [the longest x4 123 us: one_block(): jnp.einsum('sr,sac->rac', row_hits, products, precision=lax.Precision.HIG...]
    all_gather x1, waiting for transfers between devices: 0.01 us -> 67.3 us  [per_device(): gathered = lax.all_gather(panel, 'grp', axis=0, tiled=True)]
    gather x4 -> x0, local copies, waits for them, and re-layouts: 36.5 us -> none  [one_block(): chosen = jnp.take(panel_tiles, part_labels[:, 1], axis=0)]
    pallas_call x0 -> x1, Pallas kernels: none -> 25.9 us  [add_products(): pl.pallas_call(products_kernel, out_shape=jax.ShapeDtypeStruct((out_dev,...]
    psum x1, waiting for transfers between devices: 106 us -> 122 us  [per_device(): summed = lax.psum(summed, 'grp')]
    all_to_all x0 -> x1, starting transfers between devices: none -> 11.5 us  [per_device(): lax.all_to_all(label_out, 'wide', split_axis=0, concat_axis=0, tiled=True)]
  transfers between devices with their start and end apart: 3 -> 4, of which waited for: 1 -> 3; matrix products, arithmetic and copies ran while one was open for 1% -> 4% of each run, Pallas kernels for 0% -> 0%
where the time goes in v1:
time: 590 us; the launch traced here: 587 us
  waiting for transfers between devices  491 us (83%)
  local copies, waits for them, and re-layouts  29.4 us (5%)
  Pallas kernels  25.9 us (4%)
  starting transfers between devices  22.2 us (4%)
  between operations  14.1 us (2%)
    all_to_all x1, waiting for transfers between devices, per_device(): lax.all_to_all(outgoing, 'wide', split_axis=0, concat_axis=0, tiled=True)  300 us
    psum x1, waiting for transfers between devices, per_device(): summed = lax.psum(summed, 'grp')  122 us
    all_gather x1, waiting for transfers between devices, per_device(): gathered = lax.all_gather(panel, 'grp', axis=0, tiled=True)  67.3 us
    pallas_call x1, Pallas kernels, add_products(): pl.pallas_call(products_kernel, out_shape=jax.ShapeDtypeStruct((out_dev,...  25.9 us
    scatter x1, local copies, waits for them, and re-layouts, per_device(): jnp.zeros((slot_total, tile_side, tile_side), tiles.dtype).at[slot_index]  16.8 us
  transfers between devices with their start and end apart: 4, of which 3 were waited for; matrix products, arithmetic and copies ran while one was open for 4% of the time, Pallas kernels for 0%

profile of v1, /device:TPU:36, one launch (start us, length us, event | category | flops | bytes accessed | tf_op | source)
XLA Modules:
  0.0 587.0 jit_solution(1337024768623671789)
XLA Ops:
  6.5 0.9 select_reduce_fusion
  7.4 0.2 convert_reduce_fusion
  7.6 0.7 pad_add_fusion
  8.3 0.1 copy.12
  8.4 0.8 copy.22
  9.2 0.7 scatter_fusion
  10.0 1.1 copy.14
  11.1 11.5 %all-to-all-start = ((s32[64,2,2]{1,2,0:T(2,128)}), s32[64,2,2]{1,2,0:T(2,128)S(1)}, u32[]{:S(2)}, u32[]{:S(2)}) async-start(s32[64,2,2]{1,2,0:T(2,128)} %copy.14), calls=%async_computation | async-start | bytes 131072 | tf_op jit(solution)/shard_map/all_to_all | solution.py:91
  22.6 5.9 %broadcast_in_dim.12 = bf16[128,256,256]{2,1,0:T(8,128)(2,1)} broadcast(bf16[]{:T(256)} %constant.38.clone.1), dimensions={} | broadcast | bytes 16777218 | tf_op jit(solution)/shard_map/broadcast_in_dim | solution.py:86
  28.5 16.8 %scatter_fusion.1 = bf16[128,256,256]{2,1,0:T(8,128)(2,1)} fusion(bf16[128,256,256]{2,1,0:T(8,128)(2,1)} %broadcast_in_dim.12, s32[48]{0:T(128)S(1)} %get-tuple-element.10, bf16[48,256,256]{2,1,0:T(8,128)(2,1)} %param.5), kind=kCustom, calls=%fused_computation.1 | custom fusion | bytes 18874560 | tf_op jit(solution)/shard_map/scatter | solution.py:86
  45.3 0.0 all-to-all-done
  45.3 10.5 %all-to-all-start.1 = ((bf16[128,256,256]{2,1,0:T(8,128)(2,1)}), bf16[128,256,256]{2,1,0:T(8,128)(2,1)}, u32[]{:S(2)}, u32[]{:S(2)}) async-start(bf16[128,256,256]{2,1,0:T(8,128)(2,1)} %scatter_fusion.1), calls=%async_computation.1 | async-start | bytes 33554432 | tf_op jit(solution)/shard_map/all_to_all | solution.py:94
  55.9 0.0 all-gather.2.cloned.1.call-start
  55.9 0.7 all-gather.2.cloned.1.call-update
  56.6 0.0 all-reduce.2.cloned.1.call-start
  56.7 0.1 all_to_all.13
  56.8 2.5 sort.17
  59.4 0.6 fusion.2
  60.7 67.3 %all-gather.2.cloned.1.call-done = bf16[4096,768]{1,0:T(8,128)(2,1)} async-done(((bf16[1024,768]{1,0:T(8,128)(2,1)}), bf16[4096,768]{1,0:T(8,128)(2,1)}) %all-gather.2.cloned.1.call-update) | async-done | bytes 6291472 | tf_op jit(solution)/shard_map/all_gather | solution.py:92
  128.0 300.1 %all-to-all-done.1.arrived_hbm = bf16[128,256,256]{2,1,0:T(8,128)(2,1)} async-done(((bf16[128,256,256]{2,1,0:T(8,128)(2,1)}), bf16[128,256,256]{2,1,0:T(8,128)(2,1)}, u32[]{:S(2)}, u32[]{:S(2)}) %all-to-all-start.1) | async-done | bytes 16777248 | tf_op jit(solution)/shard_map/all_to_all | solution.py:94
  428.1 25.9 %shard_map.55 = f32[4,256,768]{2,1,0:T(8,128)} custom-call(s32[1]{0:T(128)} %bitcast.6.count_ref, s32[128]{0:T(128)S(1)} %get-tuple-element.6.order_ref, s32[128]{0:T(128)S(1)} %get-tuple-element.8.rows_ref, s32[128]{0:T(128)S(1)} %get-tuple-element.7.ks_ref, bf16[128,256,256]{2,1,0:T(8,128)(2,1)} %all-to-all-done.1.arrived_hbm, bf16[16,256,768]{2,1,0:T(8,128)(2,1)} %bitcast.38), custom_call_target="tpu_custom_call" | custom-call | tf_op jit(solution)/shard_map/pallas_call | solution.py:62
  453.9 0.0 all-reduce.2.cloned.1.call-update
  454.0 122.5 %all-reduce.2.cloned.1.call-done = f32[1024,768]{1,0:T(8,128)} async-done(((f32[1024,768]{1,0:T(8,128)}), f32[1024,768]{1,0:T(8,128)}) %all-reduce.2.cloned.1.call-update) | async-done | bytes 3145744 | tf_op jit(solution)/shard_map/psum | solution.py:96
  576.5 3.8 copy.23
  (6 shorter events, 0.0 us)
Async XLA Ops:
  11.1 34.2 %all-to-all-start = ((s32[64,2,2]{1,2,0:T(2,128)}), s32[64,2,2]{1,2,0:T(2,128)S(1)}, u32[]{:S(2)}, u32[]{:S(2)}) async-start(s32[64,2,2]{1,2,0:T(2,128)} %copy.14), calls=%async_computation | async-start | bytes 131072 | tf_op jit(solution)/shard_map/all_to_all | solution.py:91
  45.3 382.7 %all-to-all-start.1 = ((bf16[128,256,256]{2,1,0:T(8,128)(2,1)}), bf16[128,256,256]{2,1,0:T(8,128)(2,1)}, u32[]{:S(2)}, u32[]{:S(2)}) async-start(bf16[128,256,256]{2,1,0:T(8,128)(2,1)} %scatter_fusion.1), calls=%async_computation.1 | async-start | bytes 33554432 | tf_op jit(solution)/shard_map/all_to_all | solution.py:94
  55.9 72.1 %all-gather.2.cloned.1.call-start = ((), (), s32[]{:S(2)}) async-start(), calls=%async_computation.2 | async-start | bytes 7864320 | tf_op jit(solution)/shard_map/all_gather | solution.py:92
  56.6 519.8 %all-reduce.2.cloned.1.call-start = ((), (), s32[]{:S(2)}) async-start(), calls=%async_computation.3 | async-start | bytes 6291456 | tf_op jit(solution)/shard_map/psum | solution.py:96
Sparse Core Ops, SparseCore 0:
  58.5 69.4 all-gather.1
  454.1 122.3 all-reduce.1

commit v2 on v1

--- a/solution.py
+++ b/solution.py
@@ -16,8 +16,8 @@
     return (position % out_dev, target, ranking)
 
 
-def products_kernel(count_ref, order_ref, rows_ref, ks_ref, arrived_hbm, panel_ref, out_ref, buf, sem):
-    out_ref[...] = jnp.zeros_like(out_ref)
+def products_kernel(count_ref, order_ref, rows_ref, ks_ref, arrived_hbm, panel_ref, init_ref, out_ref, buf, sem):
+    out_ref[...] = init_ref[...]
     count = count_ref[0]
     columns = panel_ref.shape[2]
     side = buf.shape[2]
@@ -51,8 +51,9 @@
     lax.fori_loop(0, count, body, 0)
 
 
-def add_products(arrived, arrived_labels, panel_tiles, out_dev):
+def add_products(arrived, arrived_labels, panel_tiles, running):
     slot_count, side = arrived.shape[0], arrived.shape[1]
+    out_dev = running.shape[0]
     rows = arrived_labels[:, 0]
     ks = arrived_labels[:, 1]
     vacant = (rows >= out_dev).astype(jnp.int32)
@@ -64,6 +65,7 @@
         out_shape=jax.ShapeDtypeStruct((out_dev, side, panel_tiles.shape[2]), jnp.float32),
         in_specs=[smem, smem, smem, smem,
                   pl.BlockSpec(memory_space=pl.ANY),
+                  pl.BlockSpec(memory_space=pltpu.VMEM),
                   pl.BlockSpec(memory_space=pltpu.VMEM)],
         out_specs=pl.BlockSpec(memory_space=pltpu.VMEM),
         scratch_shapes=[
@@ -71,7 +73,7 @@
             pltpu.SemaphoreType.DMA((2,)),
         ],
         compiler_params=pltpu.CompilerParams(vmem_limit_bytes=48 * 1024 * 1024),
-    )(count, order, rows, ks, arrived, panel_tiles)
+    )(count, order, rows, ks, arrived, panel_tiles, running)
 
 
 def per_device(tiles, contraction, row_tile, owner_map, panel):
@@ -83,16 +85,22 @@
     slot_total = wide_count * most_slots
     local_row, target, ranking = place_slots(row_tile, owner_map, out_dev)
     slot_index = target * most_slots + ranking
-    outgoing = jnp.zeros((slot_total, tile_side, tile_side), tiles.dtype).at[slot_index].set(tiles)
     vacant_label = jnp.stack(
         [jnp.full((slot_total,), out_dev, jnp.int32), jnp.zeros((slot_total,), jnp.int32)], axis=1
     )
     label_out = vacant_label.at[slot_index].set(jnp.stack([local_row, contraction], axis=1))
     arrived_labels = lax.all_to_all(label_out, "wide", split_axis=0, concat_axis=0, tiled=True)
+    arrived_labels = arrived_labels.reshape(wide_count, most_slots, 2)
     gathered = lax.all_gather(panel, "grp", axis=0, tiled=True)
     panel_tiles = gathered.reshape(gathered.shape[0] // tile_side, tile_side, gathered.shape[1])
-    arrived = lax.all_to_all(outgoing, "wide", split_axis=0, concat_axis=0, tiled=True)
-    summed = add_products(arrived, arrived_labels, panel_tiles, out_dev)
+    summed = jnp.zeros((out_dev, tile_side, gathered.shape[1]), jnp.float32)
+    for rank in range(most_slots):
+        chunk_index = jnp.where(ranking == rank, target, wide_count)
+        outgoing = jnp.zeros((wide_count, tile_side, tile_side), tiles.dtype).at[chunk_index].set(
+            tiles, mode="drop"
+        )
+        arrived = lax.all_to_all(outgoing, "wide", split_axis=0, concat_axis=0, tiled=True)
+        summed = add_products(arrived, arrived_labels[:, rank, :], panel_tiles, summed)
     summed = lax.psum(summed, "grp")
     return summed.reshape(out_dev * tile_side, gathered.shape[1])
 

time: 590 us -> 555 us (0.941)
  waiting for transfers between devices: 491 us -> 383 us
  Pallas kernels: 25.9 us -> 69.3 us
  local copies, waits for them, and re-layouts: 29.4 us -> 49.9 us
  starting transfers between devices: 22.2 us -> 28.7 us
    all_to_all x1 -> x2, waiting for transfers between devices: 300 us -> 236 us  [per_device(): lax.all_to_all(outgoing, 'wide', split_axis=0, concat_axis=0, tiled=True)]
    pallas_call x1 -> x2, Pallas kernels: 25.9 us -> 69.3 us  [add_products(): pl.pallas_call(products_kernel, out_shape=jax.ShapeDtypeStruct((out_dev,...]
    psum x1, waiting for transfers between devices: 122 us -> 80.6 us  [per_device(): summed = lax.psum(summed, 'grp')]
    scatter x1 -> x2, local copies, waits for them, and re-layouts: 16.8 us -> 31 us  [per_device(): jnp.zeros((wide_count, tile_side, tile_side), tiles.dtype).at[chunk_index]]
    another operation x0 -> x2, local copies, waits for them, and re-layouts: none -> 8.46 us
    all_to_all x1 -> x2, starting transfers between devices: 10.5 us -> 17.1 us  [per_device(): lax.all_to_all(outgoing, 'wide', split_axis=0, concat_axis=0, tiled=True)]
  transfers between devices with their start and end apart: 4 -> 5, of which waited for: 3 -> 4; matrix products, arithmetic and copies ran while one was open for 4% -> 8% of each run, Pallas kernels for 0% -> 7%
where the time goes in v2:
time: 555 us; the launch traced here: 552 us
  waiting for transfers between devices  383 us (69%)
  Pallas kernels  69.3 us (12%)
  local copies, waits for them, and re-layouts  49.9 us (9%)
  starting transfers between devices  28.7 us (5%)
  between operations  14.9 us (3%)
  other arithmetic  6.54 us (1%)
    all_to_all x2, waiting for transfers between devices, per_device(): lax.all_to_all(outgoing, 'wide', split_axis=0, concat_axis=0, tiled=True)  236 us
    psum x1, waiting for transfers between devices, per_device(): summed = lax.psum(summed, 'grp')  80.6 us
    pallas_call x2, Pallas kernels, add_products(): pl.pallas_call(products_kernel, out_shape=jax.ShapeDtypeStruct((out_dev,...  69.3 us
    all_gather x1, waiting for transfers between devices, per_device(): gathered = lax.all_gather(panel, 'grp', axis=0, tiled=True)  64.9 us
    scatter x2, local copies, waits for them, and re-layouts, per_device(): jnp.zeros((wide_count, tile_side, tile_side), tiles.dtype).at[chunk_index]  31 us
    all_to_all x2, starting transfers between devices, per_device(): lax.all_to_all(outgoing, 'wide', split_axis=0, concat_axis=0, tiled=True)  17.1 us
    all_to_all x1, starting transfers between devices, per_device(): lax.all_to_all(label_out, 'wide', split_axis=0, concat_axis=0, tiled=True)  11.5 us
  transfers between devices with their start and end apart: 5, of which 4 were waited for; matrix products, arithmetic and copies ran while one was open for 8% of the time, Pallas kernels for 7%

profile of v2, /device:TPU:36, one launch (start us, length us, event | category | flops | bytes accessed | tf_op | source)
XLA Modules:
  0.0 552.0 jit_solution(1747763605806543204)
XLA Ops:
  6.5 0.9 select_reduce_fusion
  7.4 0.2 convert_reduce_fusion
  7.6 0.7 pad_add_fusion
  8.3 0.1 copy.15
  8.4 0.8 copy.27
  9.2 0.7 scatter_fusion
  10.0 1.1 copy.17
  11.1 11.5 %all-to-all-start = ((s32[64,2,2]{1,2,0:T(2,128)}), s32[64,2,2]{1,2,0:T(2,128)S(1)}, u32[]{:S(2)}, u32[]{:S(2)}) async-start(s32[64,2,2]{1,2,0:T(2,128)} %copy.17), calls=%async_computation | async-start | bytes 131072 | tf_op jit(solution)/shard_map/all_to_all | solution.py:92
  22.6 4.2 broadcast.273.clone.1
  26.9 16.1 %scatter_fusion.2 = bf16[64,256,256]{2,1,0:T(8,128)(2,1)} fusion(bf16[64,256,256]{2,1,0:T(8,128)(2,1)} %broadcast.273.clone.1, s32[48]{0:T(128)S(1)} %get-tuple-element.11, bf16[48,256,256]{2,1,0:T(8,128)(2,1)} %param.5), kind=kCustom, calls=%fused_computation.2 | custom fusion | bytes 18874560 | tf_op jit(solution)/shard_map/scatter | solution.py:99
  42.9 0.0 all-to-all-done
  43.0 10.6 %all-to-all-start.2 = ((bf16[64,256,256]{2,1,0:T(8,128)(2,1)}), bf16[64,256,256]{2,1,0:T(8,128)(2,1)}, u32[]{:S(2)}, u32[]{:S(2)}) async-start(bf16[64,256,256]{2,1,0:T(8,128)(2,1)} %scatter_fusion.2), calls=%async_computation.2 | async-start | bytes 16777216 | tf_op jit(solution)/shard_map/all_to_all | solution.py:102
  53.6 4.2 broadcast.273.clone
  57.8 14.9 %scatter_fusion.1 = bf16[64,256,256]{2,1,0:T(8,128)(2,1)} fusion(bf16[64,256,256]{2,1,0:T(8,128)(2,1)} %broadcast.273.clone, s32[48]{0:T(128)S(1)} %get-tuple-element.12, bf16[48,256,256]{2,1,0:T(8,128)(2,1)} %param.5), kind=kCustom, calls=%fused_computation.1 | custom fusion | bytes 18874560 | tf_op jit(solution)/shard_map/scatter | solution.py:99
  72.7 167.1 %all-to-all-done.2.arrived_hbm = bf16[64,256,256]{2,1,0:T(8,128)(2,1)} async-done(((bf16[64,256,256]{2,1,0:T(8,128)(2,1)}), bf16[64,256,256]{2,1,0:T(8,128)(2,1)}, u32[]{:S(2)}, u32[]{:S(2)}) %all-to-all-start.2) | async-done | bytes 8388640 | tf_op jit(solution)/shard_map/all_to_all | solution.py:102
  239.8 6.5 %all-to-all-start.1 = ((bf16[64,256,256]{2,1,0:T(8,128)(2,1)}), bf16[64,256,256]{2,1,0:T(8,128)(2,1)}, u32[]{:S(2)}, u32[]{:S(2)}) async-start(bf16[64,256,256]{2,1,0:T(8,128)(2,1)} %scatter_fusion.1), calls=%async_computation.1 | async-start | bytes 16777216 | tf_op jit(solution)/shard_map/all_to_all | solution.py:102
  246.2 0.0 all-gather.2.cloned.1.call-start
  246.3 0.7 all-gather.2.cloned.1.call-update
  247.0 0.0 all-reduce.2.cloned.1.call-start
  247.0 0.1 fusion.6
  247.2 0.1 copy.19
  247.2 0.1 copy.18
  247.3 0.7 fusion.4
  249.4 2.0 sort.32
  251.5 2.0 sort.31
  253.5 64.9 %all-gather.2.cloned.1.call-done = bf16[4096,768]{1,0:T(8,128)(2,1)} async-done(((bf16[1024,768]{1,0:T(8,128)(2,1)}), bf16[4096,768]{1,0:T(8,128)(2,1)}) %all-gather.2.cloned.1.call-update) | async-done | bytes 6291472 | tf_op jit(solution)/shard_map/all_gather | solution.py:94
  318.4 1.9 broadcast_in_dim.28.init_ref
  320.3 41.0 %shard_map.55.init_ref = f32[4,256,768]{2,1,0:T(8,128)S(1)} custom-call(s32[1]{0:T(128)} %bitcast.13.count_ref, s32[64]{0:T(128)S(1)} %get-tuple-element.8.order_ref, s32[64]{0:T(128)S(1)} %get-tuple-element.15.rows_ref, s32[64]{0:T(128)S(1)} %get-tuple-element.14.ks_ref, bf16[64,256,256]{2,1,0:T(8,128)(2,1)} %all-to-all-done.2.arrived_hbm, ...), custom_call_target="tpu_custom_call" | custom-call | tf_op jit(solution)/shard_map/pallas_call | solution.py:63
  361.3 0.0 copy-start
  361.3 1.7 copy-done
  363.0 69.4 %all-to-all-done.1.arrived_hbm = bf16[64,256,256]{2,1,0:T(8,128)(2,1)} async-done(((bf16[64,256,256]{2,1,0:T(8,128)(2,1)}), bf16[64,256,256]{2,1,0:T(8,128)(2,1)}, u32[]{:S(2)}, u32[]{:S(2)}) %all-to-all-start.1) | async-done | bytes 8388640 | tf_op jit(solution)/shard_map/all_to_all | solution.py:102
  432.4 28.3 %shard_map.56 = f32[4,256,768]{2,1,0:T(8,128)} custom-call(s32[1]{0:T(128)} %bitcast.7.count_ref, s32[64]{0:T(128)S(1)} %get-tuple-element.7.order_ref, s32[64]{0:T(128)S(1)} %get-tuple-element.17.rows_ref, s32[64]{0:T(128)S(1)} %get-tuple-element.16.ks_ref, bf16[64,256,256]{2,1,0:T(8,128)(2,1)} %all-to-all-done.1.arrived_hbm, ...), custom_call_target="tpu_custom_call" | custom-call | tf_op jit(solution)/shard_map/pallas_call | solution.py:63
  460.8 0.0 all-reduce.2.cloned.1.call-update
  460.8 80.6 %all-reduce.2.cloned.1.call-done = f32[1024,768]{1,0:T(8,128)} async-done(((f32[1024,768]{1,0:T(8,128)}), f32[1024,768]{1,0:T(8,128)}) %all-reduce.2.cloned.1.call-update) | async-done | bytes 3145744 | tf_op jit(solution)/shard_map/psum | solution.py:104
  541.4 3.8 copy.28
  (8 shorter events, 0.0 us)
Async XLA Ops:
  11.1 31.9 %all-to-all-start = ((s32[64,2,2]{1,2,0:T(2,128)}), s32[64,2,2]{1,2,0:T(2,128)S(1)}, u32[]{:S(2)}, u32[]{:S(2)}) async-start(s32[64,2,2]{1,2,0:T(2,128)} %copy.17), calls=%async_computation | async-start | bytes 131072 | tf_op jit(solution)/shard_map/all_to_all | solution.py:92
  43.0 196.8 %all-to-all-start.2 = ((bf16[64,256,256]{2,1,0:T(8,128)(2,1)}), bf16[64,256,256]{2,1,0:T(8,128)(2,1)}, u32[]{:S(2)}, u32[]{:S(2)}) async-start(bf16[64,256,256]{2,1,0:T(8,128)(2,1)} %scatter_fusion.2), calls=%async_computation.2 | async-start | bytes 16777216 | tf_op jit(solution)/shard_map/all_to_all | solution.py:102
  239.8 192.6 %all-to-all-start.1 = ((bf16[64,256,256]{2,1,0:T(8,128)(2,1)}), bf16[64,256,256]{2,1,0:T(8,128)(2,1)}, u32[]{:S(2)}, u32[]{:S(2)}) async-start(bf16[64,256,256]{2,1,0:T(8,128)(2,1)} %scatter_fusion.1), calls=%async_computation.1 | async-start | bytes 16777216 | tf_op jit(solution)/shard_map/all_to_all | solution.py:102
  246.2 72.2 %all-gather.2.cloned.1.call-start = ((), (), s32[]{:S(2)}) async-start(), calls=%async_computation.3 | async-start | bytes 7864320 | tf_op jit(solution)/shard_map/all_gather | solution.py:94
  247.0 294.4 %all-reduce.2.cloned.1.call-start = ((), (), s32[]{:S(2)}) async-start(), calls=%async_computation.4 | async-start | bytes 6291456 | tf_op jit(solution)/shard_map/psum | solution.py:104
  361.3 1.7 copy-start
Sparse Core Ops, SparseCore 0:
  248.9 69.4 all-gather.1
  460.9 80.4 all-reduce.1

commit v3 on v2

--- a/solution.py
+++ b/solution.py
@@ -16,31 +16,16 @@
     return (position % out_dev, target, ranking)
 
 
-def products_kernel(count_ref, order_ref, rows_ref, ks_ref, arrived_hbm, panel_ref, init_ref, out_ref, buf, sem):
+def products_kernel(count_ref, order_ref, rows_ref, ks_ref, arrived_ref, panel_ref, init_ref, out_ref):
     out_ref[...] = init_ref[...]
-    count = count_ref[0]
     columns = panel_ref.shape[2]
-    side = buf.shape[2]
-
-    def fetch(i, slot):
-        return pltpu.make_async_copy(arrived_hbm.at[order_ref[i]], buf.at[slot], sem.at[slot])
-
-    @pl.when(count > 0)
-    def _():
-        fetch(0, 0).start()
+    side = arrived_ref.shape[2]
 
     def body(i, carry):
-        slot = i % 2
-
-        @pl.when(i + 1 < count)
-        def _():
-            fetch(i + 1, 1 - slot).start()
-
-        fetch(i, slot).wait()
         source = order_ref[i]
         row = rows_ref[source]
         k = ks_ref[source]
-        tile = buf[slot]
+        tile = arrived_ref[source]
         for c in range(columns // side):
             cols = pl.ds(c * side, side)
             out_ref[row, :, cols] += jnp.dot(
@@ -48,7 +33,7 @@
             )
         return carry
 
-    lax.fori_loop(0, count, body, 0)
+    lax.fori_loop(0, count_ref[0], body, 0)
 
 
 def add_products(arrived, arrived_labels, panel_tiles, running):
@@ -64,14 +49,10 @@
         products_kernel,
         out_shape=jax.ShapeDtypeStruct((out_dev, side, panel_tiles.shape[2]), jnp.float32),
         in_specs=[smem, smem, smem, smem,
-                  pl.BlockSpec(memory_space=pl.ANY),
+                  pl.BlockSpec(memory_space=pltpu.VMEM),
                   pl.BlockSpec(memory_space=pltpu.VMEM),
                   pl.BlockSpec(memory_space=pltpu.VMEM)],
         out_specs=pl.BlockSpec(memory_space=pltpu.VMEM),
-        scratch_shapes=[
-            pltpu.VMEM((2, side, side), arrived.dtype),
-            pltpu.SemaphoreType.DMA((2,)),
-        ],
         compiler_params=pltpu.CompilerParams(vmem_limit_bytes=48 * 1024 * 1024),
     )(count, order, rows, ks, arrived, panel_tiles, running)
 
@@ -96,9 +77,10 @@
     summed = jnp.zeros((out_dev, tile_side, gathered.shape[1]), jnp.float32)
     for rank in range(most_slots):
         chunk_index = jnp.where(ranking == rank, target, wide_count)
-        outgoing = jnp.zeros((wide_count, tile_side, tile_side), tiles.dtype).at[chunk_index].set(
-            tiles, mode="drop"
+        picks = jnp.full((wide_count,), tile_dev, jnp.int32).at[chunk_index].set(
+            jnp.arange(tile_dev, dtype=jnp.int32), mode="drop"
         )
+        outgoing = jnp.take(tiles, picks, axis=0, mode="fill", fill_value=0)
         arrived = lax.all_to_all(outgoing, "wide", split_axis=0, concat_axis=0, tiled=True)
         summed = add_products(arrived, arrived_labels[:, rank, :], panel_tiles, summed)
     summed = lax.psum(summed, "grp")

time: 555 us -> 540 us (0.973)
  Pallas kernels: 69.3 us -> 30.5 us
  waiting for transfers between devices: 383 us -> 415 us
  local copies, waits for them, and re-layouts: 49.9 us -> 28.3 us
  other arithmetic: 6.54 us -> 21 us
    pallas_call x2, Pallas kernels: 69.3 us -> 30.5 us  [add_products(): pl.pallas_call(products_kernel, out_shape=jax.ShapeDtypeStruct((out_dev,...]
    scatter x2, local copies, waits for them, and re-layouts: 31 us -> 1.45 us  [per_device(): jnp.full((wide_count,), tile_dev, jnp.int32).at[chunk_index]]
    all_to_all x2, waiting for transfers between devices: 236 us -> 261 us  [per_device(): lax.all_to_all(outgoing, 'wide', split_axis=0, concat_axis=0, tiled=True)]
    gather x0 -> x2, local copies, waits for them, and re-layouts: none -> 16.4 us  [per_device(): outgoing = jnp.take(tiles, picks, axis=0, mode='fill', fill_value=0)]
    select_n x1 -> x5, other arithmetic: 0.02 us -> 14.5 us  [the longest x4 14.4 us: per_device(): outgoing = jnp.take(tiles, picks, axis=0, mode='fill', fill_value=0)]
    another operation x2 -> x0, local copies, waits for them, and re-layouts: 8.46 us -> none
    psum x1, waiting for transfers between devices: 80.6 us -> 87.8 us  [per_device(): summed = lax.psum(summed, 'grp')]
  transfers between devices with their start and end apart: 5 -> 5, of which waited for: 4 -> 4; matrix products, arithmetic and copies ran while one was open for 8% -> 7% of each run, Pallas kernels for 7% -> 4%
where the time goes in v3:
time: 540 us; the launch traced here: 538 us
  waiting for transfers between devices  415 us (77%)
  Pallas kernels  30.5 us (6%)
  starting transfers between devices  28.6 us (5%)
  local copies, waits for them, and re-layouts  28.3 us (5%)
  other arithmetic  21 us (4%)
  between operations  14.9 us (3%)
    all_to_all x2, waiting for transfers between devices, per_device(): lax.all_to_all(outgoing, 'wide', split_axis=0, concat_axis=0, tiled=True)  261 us
    psum x1, waiting for transfers between devices, per_device(): summed = lax.psum(summed, 'grp')  87.8 us
    all_gather x1, waiting for transfers between devices, per_device(): gathered = lax.all_gather(panel, 'grp', axis=0, tiled=True)  65 us
    pallas_call x2, Pallas kernels, add_products(): pl.pallas_call(products_kernel, out_shape=jax.ShapeDtypeStruct((out_dev,...  30.5 us
    all_to_all x2, starting transfers between devices, per_device(): lax.all_to_all(outgoing, 'wide', split_axis=0, concat_axis=0, tiled=True)  16.9 us
    gather x2, local copies, waits for them, and re-layouts, per_device(): outgoing = jnp.take(tiles, picks, axis=0, mode='fill', fill_value=0)  16.4 us
    select_n x4, other arithmetic, per_device(): outgoing = jnp.take(tiles, picks, axis=0, mode='fill', fill_value=0)  14.4 us
    all_to_all x1, starting transfers between devices, per_device(): lax.all_to_all(label_out, 'wide', split_axis=0, concat_axis=0, tiled=True)  11.5 us
  transfers between devices with their start and end apart: 5, of which 4 were waited for; matrix products, arithmetic and copies ran while one was open for 7% of the time, Pallas kernels for 4%

profile of v3, /device:TPU:36, one launch (start us, length us, event | category | flops | bytes accessed | tf_op | source)
XLA Modules:
  0.0 538.1 jit_solution(5334006721777031868)
XLA Ops:
  6.5 0.9 select_reduce_fusion
  7.4 0.2 convert_reduce_fusion
  7.6 0.7 pad_add_fusion
  8.3 0.1 copy.15
  8.4 0.8 copy.25
  9.2 0.7 scatter_fusion
  10.0 1.1 copy.17
  11.1 11.5 %all-to-all-start = ((s32[64,2,2]{1,2,0:T(2,128)}), s32[64,2,2]{1,2,0:T(2,128)S(1)}, u32[]{:S(2)}, u32[]{:S(2)}) async-start(s32[64,2,2]{1,2,0:T(2,128)} %copy.17), calls=%async_computation | async-start | bytes 131072 | tf_op jit(solution)/shard_map/all_to_all | solution.py:73
  22.6 0.7 scatter_custom_fusion.2
  23.4 8.2 %gather_fusion.1 = bf16[64,256,256]{2,1,0:T(8,128)(2,1)} fusion(bf16[48,256,256]{2,1,0:T(8,128)(2,1)} %param.7, s32[1024]{0:T(1024)S(1)} %pad_clamp_fusion), kind=kCustom, calls=%fused_computation.1.clone | custom fusion | bytes 16777472 | tf_op jit(solution)/shard_map/jit(_take)/gather | solution.py:83
  31.6 7.2 %broadcast_select_fusion = bf16[64,256,256]{2,1,0:T(8,128)(2,1)} fusion(bf16[64,256,256]{2,1,0:T(8,128)(2,1)} %gather_fusion.1, pred[64]{0:T(512)(128)(4,1)S(1)} %compare_and_fusion), kind=kLoop, calls=%fused_computation.5 | loop fusion | flops 4194304 | bytes 16777280 | tf_op jit(solution)/shard_map/jit(_take)/select_n | solution.py:83
  38.8 0.0 all-to-all-done
  38.8 10.5 %all-to-all-start.2 = ((bf16[64,256,256]{2,1,0:T(8,128)(2,1)}), bf16[64,256,256]{2,1,0:T(8,128)(2,1)}, u32[]{:S(2)}, u32[]{:S(2)}) async-start(bf16[64,256,256]{2,1,0:T(8,128)(2,1)} %broadcast_select_fusion), calls=%async_computation.2 | async-start | bytes 16777216 | tf_op jit(solution)/shard_map/all_to_all | solution.py:84
  49.4 0.7 scatter_custom_fusion.1
  50.1 8.2 %gather_fusion = bf16[64,256,256]{2,1,0:T(8,128)(2,1)} fusion(bf16[48,256,256]{2,1,0:T(8,128)(2,1)} %param.7, s32[1024]{0:T(1024)S(1)} %pad_clamp_fusion.1), kind=kCustom, calls=%fused_computation.clone | custom fusion | bytes 16777472 | tf_op jit(solution)/shard_map/jit(_take)/gather | solution.py:83
  58.3 7.2 %broadcast_select_fusion.1 = bf16[64,256,256]{2,1,0:T(8,128)(2,1)} fusion(bf16[64,256,256]{2,1,0:T(8,128)(2,1)} %gather_fusion, pred[64]{0:T(512)(128)(4,1)S(1)} %compare_and_fusion.1), kind=kLoop, calls=%fused_computation.6 | loop fusion | flops 4194304 | bytes 16777280 | tf_op jit(solution)/shard_map/jit(_take)/select_n | solution.py:83
  65.5 170.0 %all-to-all-done.2.arrived_ref = bf16[64,256,256]{2,1,0:T(8,128)(2,1)} async-done(((bf16[64,256,256]{2,1,0:T(8,128)(2,1)}), bf16[64,256,256]{2,1,0:T(8,128)(2,1)}, u32[]{:S(2)}, u32[]{:S(2)}) %all-to-all-start.2) | async-done | bytes 8388640 | tf_op jit(solution)/shard_map/all_to_all | solution.py:84
  235.5 6.5 %all-to-all-start.1 = ((bf16[64,256,256]{2,1,0:T(8,128)(2,1)}), bf16[64,256,256]{2,1,0:T(8,128)(2,1)}, u32[]{:S(2)}, u32[]{:S(2)}) async-start(bf16[64,256,256]{2,1,0:T(8,128)(2,1)} %broadcast_select_fusion.1), calls=%async_computation.1 | async-start | bytes 16777216 | tf_op jit(solution)/shard_map/all_to_all | solution.py:84
  242.0 0.0 all-gather.2.cloned.1.call-start
  242.0 0.7 all-gather.2.cloned.1.call-update
  242.7 0.0 all-reduce.2.cloned.1.call-start
  242.8 0.1 fusion.10
  242.9 0.1 copy.19
  243.0 0.1 copy.18
  243.1 0.7 fusion.8
  245.2 2.0 sort.32
  247.2 2.0 sort.31
  249.3 65.0 %all-gather.2.cloned.1.call-done = bf16[4096,768]{1,0:T(8,128)(2,1)} async-done(((bf16[1024,768]{1,0:T(8,128)(2,1)}), bf16[4096,768]{1,0:T(8,128)(2,1)}) %all-gather.2.cloned.1.call-update) | async-done | bytes 6291472 | tf_op jit(solution)/shard_map/all_gather | solution.py:75
  314.3 1.9 broadcast_in_dim.37.init_ref
  316.2 19.0 %shard_map.55.init_ref = f32[4,256,768]{2,1,0:T(8,128)S(1)} custom-call(s32[1]{0:T(128)} %bitcast.13.count_ref, s32[64]{0:T(128)S(1)} %get-tuple-element.9.order_ref, s32[64]{0:T(128)S(1)} %get-tuple-element.16.rows_ref, s32[64]{0:T(128)S(1)} %get-tuple-element.15.ks_ref, bf16[64,256,256]{2,1,0:T(8,128)(2,1)} %all-to-all-done.2.arrived_ref, ...), custom_call_target="tpu_custom_call" | custom-call | tf_op jit(solution)/shard_map/pallas_call | solution.py:48
  335.3 0.0 copy-start
  335.3 1.7 copy-done
  337.0 91.2 %all-to-all-done.1.arrived_ref = bf16[64,256,256]{2,1,0:T(8,128)(2,1)} async-done(((bf16[64,256,256]{2,1,0:T(8,128)(2,1)}), bf16[64,256,256]{2,1,0:T(8,128)(2,1)}, u32[]{:S(2)}, u32[]{:S(2)}) %all-to-all-start.1) | async-done | bytes 8388640 | tf_op jit(solution)/shard_map/all_to_all | solution.py:84
  428.2 11.5 %shard_map.56 = f32[4,256,768]{2,1,0:T(8,128)} custom-call(s32[1]{0:T(128)} %bitcast.7.count_ref, s32[64]{0:T(128)S(1)} %get-tuple-element.8.order_ref, s32[64]{0:T(128)S(1)} %get-tuple-element.18.rows_ref, s32[64]{0:T(128)S(1)} %get-tuple-element.17.ks_ref, bf16[64,256,256]{2,1,0:T(8,128)(2,1)} %all-to-all-done.1.arrived_ref, ...), custom_call_target="tpu_custom_call" | custom-call | tf_op jit(solution)/shard_map/pallas_call | solution.py:48
  439.7 0.0 all-reduce.2.cloned.1.call-update
  439.7 87.8 %all-reduce.2.cloned.1.call-done = f32[1024,768]{1,0:T(8,128)} async-done(((f32[1024,768]{1,0:T(8,128)}), f32[1024,768]{1,0:T(8,128)}) %all-reduce.2.cloned.1.call-update) | async-done | bytes 3145744 | tf_op jit(solution)/shard_map/psum | solution.py:86
  527.5 3.8 copy.26
  (16 shorter events, 0.1 us)
Async XLA Ops:
  11.1 27.8 %all-to-all-start = ((s32[64,2,2]{1,2,0:T(2,128)}), s32[64,2,2]{1,2,0:T(2,128)S(1)}, u32[]{:S(2)}, u32[]{:S(2)}) async-start(s32[64,2,2]{1,2,0:T(2,128)} %copy.17), calls=%async_computation | async-start | bytes 131072 | tf_op jit(solution)/shard_map/all_to_all | solution.py:73
  38.8 196.7 %all-to-all-start.2 = ((bf16[64,256,256]{2,1,0:T(8,128)(2,1)}), bf16[64,256,256]{2,1,0:T(8,128)(2,1)}, u32[]{:S(2)}, u32[]{:S(2)}) async-start(bf16[64,256,256]{2,1,0:T(8,128)(2,1)} %broadcast_select_fusion), calls=%async_computation.2 | async-start | bytes 16777216 | tf_op jit(solution)/shard_map/all_to_all | solution.py:84
  235.5 192.6 %all-to-all-start.1 = ((bf16[64,256,256]{2,1,0:T(8,128)(2,1)}), bf16[64,256,256]{2,1,0:T(8,128)(2,1)}, u32[]{:S(2)}, u32[]{:S(2)}) async-start(bf16[64,256,256]{2,1,0:T(8,128)(2,1)} %broadcast_select_fusion.1), calls=%async_computation.1 | async-start | bytes 16777216 | tf_op jit(solution)/shard_map/all_to_all | solution.py:84
  242.0 72.3 %all-gather.2.cloned.1.call-start = ((), (), s32[]{:S(2)}) async-start(), calls=%async_computation.3 | async-start | bytes 7864320 | tf_op jit(solution)/shard_map/all_gather | solution.py:75
  242.7 284.8 %all-reduce.2.cloned.1.call-start = ((), (), s32[]{:S(2)}) async-start(), calls=%async_computation.4 | async-start | bytes 6291456 | tf_op jit(solution)/shard_map/psum | solution.py:86
  335.3 1.7 copy-start
Sparse Core Ops, SparseCore 0:
  244.6 69.6 all-gather.1
  439.8 87.6 all-reduce.1

commit v4 on v3

--- a/solution.py
+++ b/solution.py
@@ -80,7 +80,7 @@
         picks = jnp.full((wide_count,), tile_dev, jnp.int32).at[chunk_index].set(
             jnp.arange(tile_dev, dtype=jnp.int32), mode="drop"
         )
-        outgoing = jnp.take(tiles, picks, axis=0, mode="fill", fill_value=0)
+        outgoing = jnp.take(tiles, picks, axis=0, mode="clip")
         arrived = lax.all_to_all(outgoing, "wide", split_axis=0, concat_axis=0, tiled=True)
         summed = add_products(arrived, arrived_labels[:, rank, :], panel_tiles, summed)
     summed = lax.psum(summed, "grp")

time: 540 us -> 528 us (0.978)
  other arithmetic: 21 us -> 6.55 us
    select_n x4 -> x0, other arithmetic: 14.4 us -> none  [per_device(): outgoing = jnp.take(tiles, picks, axis=0, mode='fill', fill_value=0)]
    all_to_all x2, waiting for transfers between devices: 261 us -> 267 us  [per_device(): lax.all_to_all(outgoing, 'wide', split_axis=0, concat_axis=0, tiled=True)]
    psum x1, waiting for transfers between devices: 87.8 us -> 82.1 us  [per_device(): summed = lax.psum(summed, 'grp')]
  transfers between devices with their start and end apart: 5 -> 5, of which waited for: 4 -> 4; matrix products, arithmetic and copies ran while one was open for 7% -> 5% of each run, Pallas kernels for 4% -> 4%
where the time goes in v4:
time: 528 us; the launch traced here: 527 us
  waiting for transfers between devices  415 us (79%)
  Pallas kernels  33.1 us (6%)
  starting transfers between devices  28.5 us (5%)
  local copies, waits for them, and re-layouts  28.3 us (5%)
  between operations  14.9 us (3%)
  other arithmetic  6.55 us (1%)
    all_to_all x2, waiting for transfers between devices, per_device(): lax.all_to_all(outgoing, 'wide', split_axis=0, concat_axis=0, tiled=True)  267 us
    psum x1, waiting for transfers between devices, per_device(): summed = lax.psum(summed, 'grp')  82.1 us
    all_gather x1, waiting for transfers between devices, per_device(): gathered = lax.all_gather(panel, 'grp', axis=0, tiled=True)  65 us
    pallas_call x2, Pallas kernels, add_products(): pl.pallas_call(products_kernel, out_shape=jax.ShapeDtypeStruct((out_dev,...  33.1 us
    all_to_all x2, starting transfers between devices, per_device(): lax.all_to_all(outgoing, 'wide', split_axis=0, concat_axis=0, tiled=True)  16.9 us
    gather x2, local copies, waits for them, and re-layouts, per_device(): outgoing = jnp.take(tiles, picks, axis=0, mode='clip')  16.4 us
    all_to_all x1, starting transfers between devices, per_device(): lax.all_to_all(label_out, 'wide', split_axis=0, concat_axis=0, tiled=True)  11.5 us
  transfers between devices with their start and end apart: 5, of which 4 were waited for; matrix products, arithmetic and copies ran while one was open for 5% of the time, Pallas kernels for 4%

profile of v4, /device:TPU:36, one launch (start us, length us, event | category | flops | bytes accessed | tf_op | source)
XLA Modules:
  0.0 526.7 jit_solution(8268033800074806789)
XLA Ops:
  6.5 0.9 select_reduce_fusion
  7.4 0.2 convert_reduce_fusion
  7.6 0.7 pad_add_fusion
  8.3 0.1 copy.15
  8.4 0.8 copy.25
  9.2 0.7 scatter_fusion
  10.0 1.1 copy.17
  11.1 11.5 %all-to-all-start = ((s32[64,2,2]{1,2,0:T(2,128)}), s32[64,2,2]{1,2,0:T(2,128)S(1)}, u32[]{:S(2)}, u32[]{:S(2)}) async-start(s32[64,2,2]{1,2,0:T(2,128)} %copy.17), calls=%async_computation | async-start | bytes 131072 | tf_op jit(solution)/shard_map/all_to_all | solution.py:73
  22.6 0.7 scatter_custom_fusion.2
  23.4 8.3 %gather_fusion.1 = bf16[64,256,256]{2,1,0:T(8,128)(2,1)} fusion(bf16[48,256,256]{2,1,0:T(8,128)(2,1)} %param.5, s32[1024]{0:T(1024)S(1)} %pad_clamp_fusion), kind=kCustom, calls=%fused_computation.1 | custom fusion | bytes 16777472 | tf_op jit(solution)/shard_map/jit(_take)/gather | solution.py:83
  31.7 0.0 all-to-all-done
  31.7 10.5 %all-to-all-start.2 = ((bf16[64,256,256]{2,1,0:T(8,128)(2,1)}), bf16[64,256,256]{2,1,0:T(8,128)(2,1)}, u32[]{:S(2)}, u32[]{:S(2)}) async-start(bf16[64,256,256]{2,1,0:T(8,128)(2,1)} %gather_fusion.1), calls=%async_computation.2 | async-start | bytes 16777216 | tf_op jit(solution)/shard_map/all_to_all | solution.py:84
  42.2 0.7 scatter_custom_fusion.1
  42.9 8.1 %gather_fusion = bf16[64,256,256]{2,1,0:T(8,128)(2,1)} fusion(bf16[48,256,256]{2,1,0:T(8,128)(2,1)} %param.5, s32[1024]{0:T(1024)S(1)} %pad_clamp_fusion.1), kind=kCustom, calls=%fused_computation | custom fusion | bytes 16777472 | tf_op jit(solution)/shard_map/jit(_take)/gather | solution.py:83
  51.0 177.3 %all-to-all-done.2.arrived_ref = bf16[64,256,256]{2,1,0:T(8,128)(2,1)} async-done(((bf16[64,256,256]{2,1,0:T(8,128)(2,1)}), bf16[64,256,256]{2,1,0:T(8,128)(2,1)}, u32[]{:S(2)}, u32[]{:S(2)}) %all-to-all-start.2) | async-done | bytes 8388640 | tf_op jit(solution)/shard_map/all_to_all | solution.py:84
  228.3 6.5 %all-to-all-start.1 = ((bf16[64,256,256]{2,1,0:T(8,128)(2,1)}), bf16[64,256,256]{2,1,0:T(8,128)(2,1)}, u32[]{:S(2)}, u32[]{:S(2)}) async-start(bf16[64,256,256]{2,1,0:T(8,128)(2,1)} %gather_fusion), calls=%async_computation.1 | async-start | bytes 16777216 | tf_op jit(solution)/shard_map/all_to_all | solution.py:84
  234.8 0.0 all-gather.2.cloned.1.call-start
  234.8 0.7 all-gather.2.cloned.1.call-update
  235.5 0.0 all-reduce.2.cloned.1.call-start
  235.6 0.1 fusion.10
  235.7 0.1 copy.19
  235.8 0.1 copy.18
  235.9 0.7 fusion.8
  238.0 2.0 sort.32
  240.0 2.0 sort.31
  242.1 65.0 %all-gather.2.cloned.1.call-done = bf16[4096,768]{1,0:T(8,128)(2,1)} async-done(((bf16[1024,768]{1,0:T(8,128)(2,1)}), bf16[4096,768]{1,0:T(8,128)(2,1)}) %all-gather.2.cloned.1.call-update) | async-done | bytes 6291472 | tf_op jit(solution)/shard_map/all_gather | solution.py:75
  307.1 1.9 broadcast_in_dim.37.init_ref
  309.0 20.1 %shard_map.55.init_ref = f32[4,256,768]{2,1,0:T(8,128)S(1)} custom-call(s32[1]{0:T(128)} %bitcast.13.count_ref, s32[64]{0:T(128)S(1)} %get-tuple-element.8.order_ref, s32[64]{0:T(128)S(1)} %get-tuple-element.15.rows_ref, s32[64]{0:T(128)S(1)} %get-tuple-element.14.ks_ref, bf16[64,256,256]{2,1,0:T(8,128)(2,1)} %all-to-all-done.2.arrived_ref, ...), custom_call_target="tpu_custom_call" | custom-call | tf_op jit(solution)/shard_map/pallas_call | solution.py:48
  329.1 0.0 copy-start
  329.2 1.7 copy-done
  330.8 90.1 %all-to-all-done.1.arrived_ref = bf16[64,256,256]{2,1,0:T(8,128)(2,1)} async-done(((bf16[64,256,256]{2,1,0:T(8,128)(2,1)}), bf16[64,256,256]{2,1,0:T(8,128)(2,1)}, u32[]{:S(2)}, u32[]{:S(2)}) %all-to-all-start.1) | async-done | bytes 8388640 | tf_op jit(solution)/shard_map/all_to_all | solution.py:84
  421.0 12.9 %shard_map.56 = f32[4,256,768]{2,1,0:T(8,128)} custom-call(s32[1]{0:T(128)} %bitcast.7.count_ref, s32[64]{0:T(128)S(1)} %get-tuple-element.7.order_ref, s32[64]{0:T(128)S(1)} %get-tuple-element.17.rows_ref, s32[64]{0:T(128)S(1)} %get-tuple-element.16.ks_ref, bf16[64,256,256]{2,1,0:T(8,128)(2,1)} %all-to-all-done.1.arrived_ref, ...), custom_call_target="tpu_custom_call" | custom-call | tf_op jit(solution)/shard_map/pallas_call | solution.py:48
  433.9 0.0 all-reduce.2.cloned.1.call-update
  433.9 82.1 %all-reduce.2.cloned.1.call-done = f32[1024,768]{1,0:T(8,128)} async-done(((f32[1024,768]{1,0:T(8,128)}), f32[1024,768]{1,0:T(8,128)}) %all-reduce.2.cloned.1.call-update) | async-done | bytes 3145744 | tf_op jit(solution)/shard_map/psum | solution.py:86
  516.1 3.8 copy.26
  (12 shorter events, 0.1 us)
Async XLA Ops:
  11.1 20.6 %all-to-all-start = ((s32[64,2,2]{1,2,0:T(2,128)}), s32[64,2,2]{1,2,0:T(2,128)S(1)}, u32[]{:S(2)}, u32[]{:S(2)}) async-start(s32[64,2,2]{1,2,0:T(2,128)} %copy.17), calls=%async_computation | async-start | bytes 131072 | tf_op jit(solution)/shard_map/all_to_all | solution.py:73
  31.7 196.6 %all-to-all-start.2 = ((bf16[64,256,256]{2,1,0:T(8,128)(2,1)}), bf16[64,256,256]{2,1,0:T(8,128)(2,1)}, u32[]{:S(2)}, u32[]{:S(2)}) async-start(bf16[64,256,256]{2,1,0:T(8,128)(2,1)} %gather_fusion.1), calls=%async_computation.2 | async-start | bytes 16777216 | tf_op jit(solution)/shard_map/all_to_all | solution.py:84
  228.3 192.6 %all-to-all-start.1 = ((bf16[64,256,256]{2,1,0:T(8,128)(2,1)}), bf16[64,256,256]{2,1,0:T(8,128)(2,1)}, u32[]{:S(2)}, u32[]{:S(2)}) async-start(bf16[64,256,256]{2,1,0:T(8,128)(2,1)} %gather_fusion), calls=%async_computation.1 | async-start | bytes 16777216 | tf_op jit(solution)/shard_map/all_to_all | solution.py:84
  234.8 72.3 %all-gather.2.cloned.1.call-start = ((), (), s32[]{:S(2)}) async-start(), calls=%async_computation.3 | async-start | bytes 7864320 | tf_op jit(solution)/shard_map/all_gather | solution.py:75
  235.5 280.5 %all-reduce.2.cloned.1.call-start = ((), (), s32[]{:S(2)}) async-start(), calls=%async_computation.4 | async-start | bytes 6291456 | tf_op jit(solution)/shard_map/psum | solution.py:86
  329.1 1.7 copy-start
Sparse Core Ops, SparseCore 0:
  237.4 69.6 all-gather.1
  434.0 81.9 all-reduce.1

commit v5 on v4

--- a/solution.py
+++ b/solution.py
@@ -1,9 +1,88 @@
+import functools
+
 import jax
 import jax.numpy as jnp
 from jax import lax
 from jax.experimental import pallas as pl
 from jax.experimental.pallas import tpu as pltpu
 from jax.sharding import PartitionSpec as P
+
+
+MESH = pl.DeviceIdType.MESH
+
+
+def ring_sum_kernel(n, x_ref, out_ref, sbuf, rbuf, send_sem, recv_sem):
+    me = lax.axis_index("grp")
+    column = lax.axis_index("wide")
+    right = lax.rem(me + 1, n)
+    left = lax.rem(me + n - 1, n)
+    half = x_ref.shape[1] // 2
+    neighbours = (right, left)
+
+    barrier = pltpu.get_barrier_semaphore()
+    for neighbour in (left, right):
+        pl.semaphore_signal(barrier, inc=1, device_id=(neighbour, column), device_id_type=MESH)
+    pl.semaphore_wait(barrier, 2)
+
+    def send(way, step, src, dst):
+        copy = pltpu.make_async_remote_copy(
+            src_ref=src,
+            dst_ref=dst,
+            send_sem=send_sem.at[way, step],
+            recv_sem=recv_sem.at[way, step],
+            device_id=(neighbours[way], column),
+            device_id_type=MESH,
+        )
+        copy.start()
+        return copy
+
+    for step in range(n - 1):
+        copies = []
+        for way in range(2):
+            sign = 1 - 2 * way
+            rows = pl.ds(way * half, half)
+            chunk = lax.rem(me - sign * (step + 1) + 2 * n, n)
+            if step == 0:
+                src = x_ref.at[chunk, rows]
+            else:
+                sbuf[way, step] = rbuf[way, step - 1] + x_ref[chunk, rows]
+                src = sbuf.at[way, step]
+            copies.append(send(way, step, src, rbuf.at[way, step]))
+        for copy in copies:
+            copy.wait()
+
+    for way in range(2):
+        rows = pl.ds(way * half, half)
+        out_ref[me, rows] = rbuf[way, n - 2] + x_ref[me, rows]
+
+    for step in range(n - 1):
+        copies = []
+        for way in range(2):
+            sign = 1 - 2 * way
+            rows = pl.ds(way * half, half)
+            chunk = lax.rem(me - sign * step + 2 * n, n)
+            copies.append(send(way, n - 1 + step, out_ref.at[chunk, rows], out_ref.at[chunk, rows]))
+        for copy in copies:
+            copy.wait()
+
+
+def ring_sum(x, n):
+    half = x.shape[1] // 2
+    return pl.pallas_call(
+        functools.partial(ring_sum_kernel, n),
+        out_shape=jax.ShapeDtypeStruct(x.shape, x.dtype),
+        in_specs=[pl.BlockSpec(memory_space=pltpu.VMEM)],
+        out_specs=pl.BlockSpec(memory_space=pltpu.VMEM),
+        scratch_shapes=[
+            pltpu.VMEM((2, n - 1, half, x.shape[2]), x.dtype),
+            pltpu.VMEM((2, n - 1, half, x.shape[2]), x.dtype),
+            pltpu.SemaphoreType.DMA((2, 2 * (n - 1))),
+            pltpu.SemaphoreType.DMA((2, 2 * (n - 1))),
+        ],
+        compiler_params=pltpu.CompilerParams(
+            collective_id=0, has_side_effects=True, vmem_limit_bytes=48 * 1024 * 1024
+        ),
+    )(x)
 
 
 def place_slots(row_ids, owner_map, out_dev):
@@ -83,7 +162,7 @@
         outgoing = jnp.take(tiles, picks, axis=0, mode="clip")
         arrived = lax.all_to_all(outgoing, "wide", split_axis=0, concat_axis=0, tiled=True)
         summed = add_products(arrived, arrived_labels[:, rank, :], panel_tiles, summed)
-    summed = lax.psum(summed, "grp")
+    summed = ring_sum(summed, lax.axis_size("grp"))
     return summed.reshape(out_dev * tile_side, gathered.shape[1])
 
 

time: 528 us -> 510 us (0.966)
  waiting for transfers between devices: 415 us -> 334 us
  Pallas kernels: 33.1 us -> 95.9 us
    psum x1 -> x0, waiting for transfers between devices: 82.1 us -> none  [per_device(): summed = lax.psum(summed, 'grp')]
    pallas_call x0 -> x1, Pallas kernels: none -> 64.9 us  [ring_sum(): pl.pallas_call(functools.partial(ring_sum_kernel, n), out_shape=jax.Shape...]
  transfers between devices with their start and end apart: 5 -> 4, of which waited for: 4 -> 3; matrix products, arithmetic and copies ran while one was open for 5% -> 5% of each run, Pallas kernels for 4% -> 4%
where the time goes in v5:
time: 510 us; the launch traced here: 508 us
  waiting for transfers between devices  334 us (65%)
  Pallas kernels  95.9 us (19%)
  starting transfers between devices  28.5 us (6%)
  local copies, waits for them, and re-layouts  27.9 us (5%)
  between operations  14.9 us (3%)
  other arithmetic  6.55 us (1%)
    all_to_all x2, waiting for transfers between devices, per_device(): lax.all_to_all(outgoing, 'wide', split_axis=0, concat_axis=0, tiled=True)  268 us
    all_gather x1, waiting for transfers between devices, per_device(): gathered = lax.all_gather(panel, 'grp', axis=0, tiled=True)  65 us
    pallas_call x1, Pallas kernels, ring_sum(): pl.pallas_call(functools.partial(ring_sum_kernel, n), out_shape=jax.Shape...  64.9 us
    pallas_call x2, Pallas kernels, add_products(): pl.pallas_call(products_kernel, out_shape=jax.ShapeDtypeStruct((out_dev,...  31 us
    all_to_all x2, starting transfers between devices, per_device(): lax.all_to_all(outgoing, 'wide', split_axis=0, concat_axis=0, tiled=True)  16.9 us
    gather x2, local copies, waits for them, and re-layouts, per_device(): outgoing = jnp.take(tiles, picks, axis=0, mode='clip')  16.4 us
    all_to_all x1, starting transfers between devices, per_device(): lax.all_to_all(label_out, 'wide', split_axis=0, concat_axis=0, tiled=True)  11.5 us
  transfers between devices with their start and end apart: 4, of which 3 were waited for; matrix products, arithmetic and copies ran while one was open for 5% of the time, Pallas kernels for 4%

profile of v5, /device:TPU:36, one launch (start us, length us, event | category | flops | bytes accessed | tf_op | source)
XLA Modules:
  0.0 507.7 jit_solution(1945803417266498377)
XLA Ops:
  6.5 0.9 select_reduce_fusion
  7.4 0.2 convert_reduce_fusion
  7.6 0.7 pad_add_fusion
  8.3 0.1 copy.15
  8.4 0.8 copy.25
  9.2 0.7 scatter_fusion
  10.0 1.1 copy.17
  11.1 11.5 %all-to-all-start = ((s32[64,2,2]{1,2,0:T(2,128)}), s32[64,2,2]{1,2,0:T(2,128)S(1)}, u32[]{:S(2)}, u32[]{:S(2)}) async-start(s32[64,2,2]{1,2,0:T(2,128)} %copy.17), calls=%async_computation | async-start | bytes 131072 | tf_op jit(solution)/shard_map/all_to_all | solution.py:152
  22.6 0.7 scatter_custom_fusion.2
  23.4 8.2 %gather_fusion.1 = bf16[64,256,256]{2,1,0:T(8,128)(2,1)} fusion(bf16[48,256,256]{2,1,0:T(8,128)(2,1)} %param.5, s32[1024]{0:T(1024)S(1)} %pad_clamp_fusion), kind=kCustom, calls=%fused_computation.1 | custom fusion | bytes 16777472 | tf_op jit(solution)/shard_map/jit(_take)/gather | solution.py:162
  31.6 0.0 all-to-all-done
  31.6 10.5 %all-to-all-start.2 = ((bf16[64,256,256]{2,1,0:T(8,128)(2,1)}), bf16[64,256,256]{2,1,0:T(8,128)(2,1)}, u32[]{:S(2)}, u32[]{:S(2)}) async-start(bf16[64,256,256]{2,1,0:T(8,128)(2,1)} %gather_fusion.1), calls=%async_computation.2 | async-start | bytes 16777216 | tf_op jit(solution)/shard_map/all_to_all | solution.py:163
  42.1 0.7 scatter_custom_fusion.1
  42.9 8.1 %gather_fusion = bf16[64,256,256]{2,1,0:T(8,128)(2,1)} fusion(bf16[48,256,256]{2,1,0:T(8,128)(2,1)} %param.5, s32[1024]{0:T(1024)S(1)} %pad_clamp_fusion.1), kind=kCustom, calls=%fused_computation | custom fusion | bytes 16777472 | tf_op jit(solution)/shard_map/jit(_take)/gather | solution.py:162
  51.0 177.3 %all-to-all-done.2.arrived_ref = bf16[64,256,256]{2,1,0:T(8,128)(2,1)} async-done(((bf16[64,256,256]{2,1,0:T(8,128)(2,1)}), bf16[64,256,256]{2,1,0:T(8,128)(2,1)}, u32[]{:S(2)}, u32[]{:S(2)}) %all-to-all-start.2) | async-done | bytes 8388640 | tf_op jit(solution)/shard_map/all_to_all | solution.py:163
  228.3 6.5 %all-to-all-start.1 = ((bf16[64,256,256]{2,1,0:T(8,128)(2,1)}), bf16[64,256,256]{2,1,0:T(8,128)(2,1)}, u32[]{:S(2)}, u32[]{:S(2)}) async-start(bf16[64,256,256]{2,1,0:T(8,128)(2,1)} %gather_fusion), calls=%async_computation.1 | async-start | bytes 16777216 | tf_op jit(solution)/shard_map/all_to_all | solution.py:163
  234.8 0.0 all-gather.2.cloned.1.call-start
  234.8 0.7 all-gather.2.cloned.1.call-update
  235.5 0.1 fusion.10
  235.6 0.1 copy.19
  235.7 0.1 copy.18
  235.8 0.7 fusion.8
  237.9 2.0 sort.32
  240.0 2.0 sort.31
  242.0 65.0 %all-gather.2.cloned.1.call-done = bf16[4096,768]{1,0:T(8,128)(2,1)} async-done(((bf16[1024,768]{1,0:T(8,128)(2,1)}), bf16[4096,768]{1,0:T(8,128)(2,1)}) %all-gather.2.cloned.1.call-update) | async-done | bytes 6291472 | tf_op jit(solution)/shard_map/all_gather | solution.py:154
  307.0 1.9 broadcast_in_dim.37.init_ref
  309.0 19.3 %shard_map.55.init_ref = f32[4,256,768]{2,1,0:T(8,128)S(1)} custom-call(s32[1]{0:T(128)} %bitcast.13.count_ref, s32[64]{0:T(128)S(1)} %get-tuple-element.8.order_ref, s32[64]{0:T(128)S(1)} %get-tuple-element.15.rows_ref, s32[64]{0:T(128)S(1)} %get-tuple-element.14.ks_ref, bf16[64,256,256]{2,1,0:T(8,128)(2,1)} %all-to-all-done.2.arrived_ref, ...), custom_call_target="tpu_custom_call" | custom-call | tf_op jit(solution)/shard_map/pallas_call | solution.py:127
  328.3 0.0 copy-start.1
  328.3 1.7 copy-done.1
  330.0 91.0 %all-to-all-done.1.arrived_ref = bf16[64,256,256]{2,1,0:T(8,128)(2,1)} async-done(((bf16[64,256,256]{2,1,0:T(8,128)(2,1)}), bf16[64,256,256]{2,1,0:T(8,128)(2,1)}, u32[]{:S(2)}, u32[]{:S(2)}) %all-to-all-start.1) | async-done | bytes 8388640 | tf_op jit(solution)/shard_map/all_to_all | solution.py:163
  420.9 11.7 %shard_map.56.x_ref = f32[4,256,768]{2,1,0:T(8,128)S(1)} custom-call(s32[1]{0:T(128)} %bitcast.7.count_ref, s32[64]{0:T(128)S(1)} %get-tuple-element.7.order_ref, s32[64]{0:T(128)S(1)} %get-tuple-element.17.rows_ref, s32[64]{0:T(128)S(1)} %get-tuple-element.16.ks_ref, bf16[64,256,256]{2,1,0:T(8,128)(2,1)} %all-to-all-done.1.arrived_ref, ...), custom_call_target="tpu_custom_call" | custom-call | tf_op jit(solution)/shard_map/pallas_call | solution.py:127
  432.7 0.0 copy-start
  432.7 1.7 copy-done
  434.3 64.9 %shard_map.57 = f32[4,256,768]{2,1,0:T(8,128)S(1)} custom-call(f32[4,256,768]{2,1,0:T(8,128)} %copy-done), custom_call_target="tpu_custom_call" | custom-call | tf_op jit(solution)/shard_map/pallas_call | solution.py:71
  499.2 1.7 copy.26
  (12 shorter events, 0.1 us)
Async XLA Ops:
  11.1 20.6 %all-to-all-start = ((s32[64,2,2]{1,2,0:T(2,128)}), s32[64,2,2]{1,2,0:T(2,128)S(1)}, u32[]{:S(2)}, u32[]{:S(2)}) async-start(s32[64,2,2]{1,2,0:T(2,128)} %copy.17), calls=%async_computation | async-start | bytes 131072 | tf_op jit(solution)/shard_map/all_to_all | solution.py:152
  31.6 196.7 %all-to-all-start.2 = ((bf16[64,256,256]{2,1,0:T(8,128)(2,1)}), bf16[64,256,256]{2,1,0:T(8,128)(2,1)}, u32[]{:S(2)}, u32[]{:S(2)}) async-start(bf16[64,256,256]{2,1,0:T(8,128)(2,1)} %gather_fusion.1), calls=%async_computation.2 | async-start | bytes 16777216 | tf_op jit(solution)/shard_map/all_to_all | solution.py:163
  228.3 192.6 %all-to-all-start.1 = ((bf16[64,256,256]{2,1,0:T(8,128)(2,1)}), bf16[64,256,256]{2,1,0:T(8,128)(2,1)}, u32[]{:S(2)}, u32[]{:S(2)}) async-start(bf16[64,256,256]{2,1,0:T(8,128)(2,1)} %gather_fusion), calls=%async_computation.1 | async-start | bytes 16777216 | tf_op jit(solution)/shard_map/all_to_all | solution.py:163
  234.8 72.3 %all-gather.2.cloned.1.call-start = ((), (), s32[]{:S(2)}) async-start(), calls=%async_computation.3 | async-start | bytes 7864320 | tf_op jit(solution)/shard_map/all_gather | solution.py:154
  328.3 1.7 copy-start.1
  432.7 1.7 copy-start
Sparse Core Ops, SparseCore 0:
  237.4 69.5 all-gather.1

commit v6 on v5

--- a/solution.py
+++ b/solution.py
@@ -66,7 +66,7 @@
             copy.wait()
 
 
-def ring_sum(x, n):
+def ring_sum(x, n, ident):
     half = x.shape[1] // 2
     return pl.pallas_call(
         functools.partial(ring_sum_kernel, n),
@@ -80,7 +80,7 @@
             pltpu.SemaphoreType.DMA((2, 2 * (n - 1))),
         ],
         compiler_params=pltpu.CompilerParams(
-            collective_id=0, has_side_effects=True, vmem_limit_bytes=48 * 1024 * 1024
+            collective_id=ident, has_side_effects=True, vmem_limit_bytes=48 * 1024 * 1024
         ),
     )(x)
 
@@ -115,25 +115,25 @@
     lax.fori_loop(0, count_ref[0], body, 0)
 
 
-def add_products(arrived, arrived_labels, panel_tiles, running):
-    slot_count, side = arrived.shape[0], arrived.shape[1]
-    out_dev = running.shape[0]
+def slot_order(arrived_labels, out_dev):
     rows = arrived_labels[:, 0]
     ks = arrived_labels[:, 1]
     vacant = (rows >= out_dev).astype(jnp.int32)
     order = jnp.argsort(vacant, stable=True).astype(jnp.int32)
-    count = jnp.reshape(slot_count - jnp.sum(vacant), (1,)).astype(jnp.int32)
+    count = jnp.reshape(rows.shape[0] - jnp.sum(vacant), (1,)).astype(jnp.int32)
+    return count, order, rows, ks
+
+
+def add_products(arrived, schedule, panel_tiles, running):
+    vmem = pl.BlockSpec(memory_space=pltpu.VMEM)
     smem = pl.BlockSpec(memory_space=pltpu.SMEM)
     return pl.pallas_call(
         products_kernel,
-        out_shape=jax.ShapeDtypeStruct((out_dev, side, panel_tiles.shape[2]), jnp.float32),
-        in_specs=[smem, smem, smem, smem,
-                  pl.BlockSpec(memory_space=pltpu.VMEM),
-                  pl.BlockSpec(memory_space=pltpu.VMEM),
-                  pl.BlockSpec(memory_space=pltpu.VMEM)],
-        out_specs=pl.BlockSpec(memory_space=pltpu.VMEM),
+        out_shape=jax.ShapeDtypeStruct(running.shape, jnp.float32),
+        in_specs=[smem, smem, smem, smem, vmem, vmem, vmem],
+        out_specs=vmem,
         compiler_params=pltpu.CompilerParams(vmem_limit_bytes=48 * 1024 * 1024),
-    )(count, order, rows, ks, arrived, panel_tiles, running)
+    )(*schedule, arrived, panel_tiles, running)
 
 
 def per_device(tiles, contraction, row_tile, owner_map, panel):
@@ -153,16 +153,33 @@
     arrived_labels = arrived_labels.reshape(wide_count, most_slots, 2)
     gathered = lax.all_gather(panel, "grp", axis=0, tiled=True)
     panel_tiles = gathered.reshape(gathered.shape[0] // tile_side, tile_side, gathered.shape[1])
-    summed = jnp.zeros((out_dev, tile_side, gathered.shape[1]), jnp.float32)
+    band = tile_side // 2
+    arrived_labels = arrived_labels.reshape(wide_count, most_slots, 2)
+    schedules = [slot_order(arrived_labels[:, rank, :], out_dev) for rank in range(most_slots)]
+    outgoing = {}
     for rank in range(most_slots):
         chunk_index = jnp.where(ranking == rank, target, wide_count)
         picks = jnp.full((wide_count,), tile_dev, jnp.int32).at[chunk_index].set(
             jnp.arange(tile_dev, dtype=jnp.int32), mode="drop"
         )
-        outgoing = jnp.take(tiles, picks, axis=0, mode="clip")
-        arrived = lax.all_to_all(outgoing, "wide", split_axis=0, concat_axis=0, tiled=True)
-        summed = add_products(arrived, arrived_labels[:, rank, :], panel_tiles, summed)
-    summed = ring_sum(summed, lax.axis_size("grp"))
+        for half in range(2):
+            rows = tiles[:, half * band:(half + 1) * band, :]
+            outgoing[rank, half] = jnp.take(rows, picks, axis=0, mode="clip")
+
+    def exchange(block):
+        return lax.all_to_all(block, "wide", split_axis=0, concat_axis=0, tiled=True)
+
+    zero = jnp.zeros((out_dev, band, gathered.shape[1]), jnp.float32)
+    upper = add_products(exchange(outgoing[0, 0]), schedules[0], panel_tiles, zero)
+    lower = add_products(exchange(outgoing[0, 1]), schedules[0], panel_tiles, zero)
+    late, upper = lax.optimization_barrier((outgoing[1, 0], upper))
+    upper = add_products(exchange(late), schedules[1], panel_tiles, upper)
+    late, lower = lax.optimization_barrier((outgoing[1, 1], lower))
+    arrived = exchange(late)
+    upper = ring_sum(upper, lax.axis_size("grp"), 0)
+    lower = add_products(arrived, schedules[1], panel_tiles, lower)
+    lower = ring_sum(lower, lax.axis_size("grp"), 1)
+    summed = jnp.concatenate([upper, lower], axis=1)
     return summed.reshape(out_dev * tile_side, gathered.shape[1])
 
 

time: 510 us -> 506 us (level)
  waiting for transfers between devices: 334 us -> 306 us
  starting transfers between devices: 28.5 us -> 42 us
  Pallas kernels: 95.9 us -> 102 us
    all_gather x1, waiting for transfers between devices: 65 us -> 0.01 us  [per_device(): gathered = lax.all_gather(panel, 'grp', axis=0, tiled=True)]
    all_to_all x2 -> x4, waiting for transfers between devices: 268 us -> 305 us  [exchange(): lax.all_to_all(block, 'wide', split_axis=0, concat_axis=0, tiled=True)]
    pallas_call x1 -> x2, Pallas kernels: 64.9 us -> 83.8 us  [ring_sum(): pl.pallas_call(functools.partial(ring_sum_kernel, n), out_shape=jax.Shape...]
    all_to_all x2 -> x4, starting transfers between devices: 16.9 us -> 30.4 us  [exchange(): lax.all_to_all(block, 'wide', split_axis=0, concat_axis=0, tiled=True)]
    pallas_call x2 -> x4, Pallas kernels: 31 us -> 18.5 us  [add_products(): pl.pallas_call(products_kernel, out_shape=jax.ShapeDtypeStruct(running.sh...]
    slice x0 -> x1, local copies, waits for them, and re-layouts: none -> 5.14 us  [per_device(): rows = tiles[:, half * band:(half + 1) * band, :]]
    gather x2 -> x4, local copies, waits for them, and re-layouts: 16.4 us -> 15.4 us  [per_device(): outgoing[rank, half] = jnp.take(rows, picks, axis=0, mode='clip')]
  transfers between devices with their start and end apart: 4 -> 6, of which waited for: 3 -> 4; matrix products, arithmetic and copies ran while one was open for 5% -> 5% of each run, Pallas kernels for 4% -> 11%
where the time goes in v6:
time: 506 us; the launch traced here: 500 us
  waiting for transfers between devices  306 us (60%)
  Pallas kernels  102 us (20%)
  starting transfers between devices  42 us (8%)
  local copies, waits for them, and re-layouts  26.4 us (5%)
  between operations  15 us (3%)
  other arithmetic  8.55 us (2%)
    all_to_all x4, waiting for transfers between devices, exchange(): lax.all_to_all(block, 'wide', split_axis=0, concat_axis=0, tiled=True)  305 us
    pallas_call x2, Pallas kernels, ring_sum(): pl.pallas_call(functools.partial(ring_sum_kernel, n), out_shape=jax.Shape...  83.8 us
    all_to_all x4, starting transfers between devices, exchange(): lax.all_to_all(block, 'wide', split_axis=0, concat_axis=0, tiled=True)  30.4 us
    pallas_call x4, Pallas kernels, add_products(): pl.pallas_call(products_kernel, out_shape=jax.ShapeDtypeStruct(running.sh...  18.5 us
    gather x4, local copies, waits for them, and re-layouts, per_device(): outgoing[rank, half] = jnp.take(rows, picks, axis=0, mode='clip')  15.4 us
    all_to_all x1, starting transfers between devices, per_device(): lax.all_to_all(label_out, 'wide', split_axis=0, concat_axis=0, tiled=True)  11.5 us
  transfers between devices with their start and end apart: 6, of which 4 were waited for; matrix products, arithmetic and copies ran while one was open for 5% of the time, Pallas kernels for 11%

profile of v6, /device:TPU:36, one launch (start us, length us, event | category | flops | bytes accessed | tf_op | source)
XLA Modules:
  0.0 500.2 jit_solution(10388537205873200149)
XLA Ops:
  6.5 0.9 select_reduce_fusion
  7.4 0.2 convert_reduce_fusion
  7.6 0.7 pad_add_fusion
  8.3 0.1 copy.15
  8.4 0.8 copy.24
  9.2 0.7 scatter_fusion
  10.0 1.1 copy.17
  11.1 11.5 %all-to-all-start = ((s32[64,2,2]{1,2,0:T(2,128)}), s32[64,2,2]{1,2,0:T(2,128)S(1)}, u32[]{:S(2)}, u32[]{:S(2)}) async-start(s32[64,2,2]{1,2,0:T(2,128)} %copy.17), calls=%async_computation | async-start | bytes 131072 | tf_op jit(solution)/shard_map/all_to_all | solution.py:152
  22.6 5.1 %fusion.10 = (bf16[48,128,256]{2,1,0:T(8,128)(2,1)}, bf16[48,128,256]{2,1,0:T(8,128)(2,1)S(1)}) fusion(bf16[48,256,256]{2,1,0:T(8,128)(2,1)} %param.5), kind=kLoop, calls=%fused_computation.47 | loop fusion | bytes 12582912 | tf_op jit(solution)/shard_map/slice | solution.py:166
  27.8 0.0 copy-start.2
  27.8 0.7 scatter_custom_fusion.2
  28.5 5.1 %gather_fusion.1 = bf16[64,128,256]{2,1,0:T(8,128)(2,1)} fusion(bf16[48,128,256]{2,1,0:T(8,128)(2,1)} %get-tuple-element.17, s32[1024]{0:T(1024)S(1)} %pad_clamp_fusion), kind=kCustom, calls=%fused_computation.1 | custom fusion | bytes 8388864 | tf_op jit(solution)/shard_map/jit(_take)/gather | solution.py:167
  33.6 0.0 all-to-all-done
  33.6 10.5 %all-to-all-start.1 = ((bf16[64,128,256]{2,1,0:T(8,128)(2,1)}), bf16[64,128,256]{2,1,0:T(8,128)(2,1)}, u32[]{:S(2)}, u32[]{:S(2)}) async-start(bf16[64,128,256]{2,1,0:T(8,128)(2,1)} %gather_fusion.1), calls=%async_computation.1 | async-start | bytes 8388608 | tf_op jit(solution)/shard_map/all_to_all | solution.py:170
  44.1 0.0 all-gather.2.cloned.1.call-start
  44.2 0.7 all-gather.2.cloned.1.call-update
  44.9 0.0 copy-done.2
  44.9 2.8 gather_fusion.3
  47.7 0.0 copy-start.3
  47.7 91.5 %all-to-all-done.1.arrived_ref = bf16[64,128,256]{2,1,0:T(8,128)(2,1)} async-done(((bf16[64,128,256]{2,1,0:T(8,128)(2,1)}), bf16[64,128,256]{2,1,0:T(8,128)(2,1)}, u32[]{:S(2)}, u32[]{:S(2)}) %all-to-all-start.1) | async-done | bytes 4194336 | tf_op jit(solution)/shard_map/all_to_all | solution.py:170
  139.2 6.8 %all-to-all-start.3 = ((bf16[64,128,256]{2,1,0:T(8,128)(2,1)}), bf16[64,128,256]{2,1,0:T(8,128)(2,1)}, u32[]{:S(2)}, u32[]{:S(2)}) async-start(bf16[64,128,256]{2,1,0:T(8,128)(2,1)} %gather_fusion.3), calls=%async_computation.3 | async-start | bytes 8388608 | tf_op jit(solution)/shard_map/all_to_all | solution.py:170
  146.0 0.7 scatter_custom_fusion.1
  146.7 0.0 copy-done.3
  146.7 2.8 gather_fusion
  149.6 0.1 fusion.11
  149.7 0.1 copy.19
  149.8 0.1 copy.18
  149.9 0.7 fusion.8
  151.3 2.1 sort.32
  153.4 0.0 all-gather.2.cloned.1.call-done
  153.4 0.1 broadcast_in_dim.39.init_ref
  153.5 4.6 shard_map.55.init_ref
  158.2 83.2 %all-to-all-done.3.arrived_ref = bf16[64,128,256]{2,1,0:T(8,128)(2,1)} async-done(((bf16[64,128,256]{2,1,0:T(8,128)(2,1)}), bf16[64,128,256]{2,1,0:T(8,128)(2,1)}, u32[]{:S(2)}, u32[]{:S(2)}) %all-to-all-start.3) | async-done | bytes 4194336 | tf_op jit(solution)/shard_map/all_to_all | solution.py:170
  241.3 6.6 %all-to-all-start.2 = ((bf16[64,128,256]{2,1,0:T(8,128)(2,1)}), bf16[64,128,256]{2,1,0:T(8,128)(2,1)}, u32[]{:S(2)}, u32[]{:S(2)}) async-start(bf16[64,128,256]{2,1,0:T(8,128)(2,1)} %gather_fusion), calls=%async_computation.2 | async-start | bytes 8388608 | tf_op jit(solution)/shard_map/all_to_all | solution.py:170
  247.9 4.7 gather_fusion.2
  252.6 4.6 shard_map.58.init_ref
  257.2 0.0 copy-start
  257.2 1.1 copy-done
  258.3 84.9 %all-to-all-done.2.arrived_ref = bf16[64,128,256]{2,1,0:T(8,128)(2,1)} async-done(((bf16[64,128,256]{2,1,0:T(8,128)(2,1)}), bf16[64,128,256]{2,1,0:T(8,128)(2,1)}, u32[]{:S(2)}, u32[]{:S(2)}) %all-to-all-start.2) | async-done | bytes 4194336 | tf_op jit(solution)/shard_map/all_to_all | solution.py:170
  343.2 6.6 %all-to-all-start.4 = ((bf16[64,128,256]{2,1,0:T(8,128)(2,1)}), bf16[64,128,256]{2,1,0:T(8,128)(2,1)}, u32[]{:S(2)}, u32[]{:S(2)}) async-start(bf16[64,128,256]{2,1,0:T(8,128)(2,1)} %gather_fusion.2), calls=%async_computation.4 | async-start | bytes 8388608 | tf_op jit(solution)/shard_map/all_to_all | solution.py:170
  350.5 2.0 sort.31
  352.5 4.6 shard_map.56.x_ref
  357.2 0.0 copy-start.1
  357.2 42.1 %shard_map.57 = f32[4,128,768]{2,1,0:T(8,128)S(1)} custom-call(f32[4,128,768]{2,1,0:T(8,128)S(1)} %shard_map.56.x_ref), custom_call_target="tpu_custom_call" | custom-call | tf_op jit(solution)/shard_map/pallas_call | solution.py:71
  399.3 45.8 %all-to-all-done.4.arrived_ref = bf16[64,128,256]{2,1,0:T(8,128)(2,1)} async-done(((bf16[64,128,256]{2,1,0:T(8,128)(2,1)}), bf16[64,128,256]{2,1,0:T(8,128)(2,1)}, u32[]{:S(2)}, u32[]{:S(2)}) %all-to-all-start.4) | async-done | bytes 4194336 | tf_op jit(solution)/shard_map/all_to_all | solution.py:170
  445.1 0.0 copy-done.1
  445.1 4.6 shard_map.59.x_ref
  449.7 41.7 %shard_map.60 = f32[4,128,768]{2,1,0:T(8,128)S(1)} custom-call(f32[4,128,768]{2,1,0:T(8,128)S(1)} %shard_map.59.x_ref), custom_call_target="tpu_custom_call" | custom-call | tf_op jit(solution)/shard_map/pallas_call | solution.py:71
  491.4 1.9 pad_maximum_fusion
  (12 shorter events, 0.1 us)
Async XLA Ops:
  11.1 22.6 %all-to-all-start = ((s32[64,2,2]{1,2,0:T(2,128)}), s32[64,2,2]{1,2,0:T(2,128)S(1)}, u32[]{:S(2)}, u32[]{:S(2)}) async-start(s32[64,2,2]{1,2,0:T(2,128)} %copy.17), calls=%async_computation | async-start | bytes 131072 | tf_op jit(solution)/shard_map/all_to_all | solution.py:152
  27.8 17.1 %copy-start.2 = (bf16[48,128,256]{2,1,0:T(8,128)(2,1)}, bf16[48,128,256]{2,1,0:T(8,128)(2,1)S(1)}, u32[]{:S(2)}) copy-start(bf16[48,128,256]{2,1,0:T(8,128)(2,1)S(1)} %get-tuple-element.18) | copy-start | bytes 9437188
  33.6 105.5 %all-to-all-start.1 = ((bf16[64,128,256]{2,1,0:T(8,128)(2,1)}), bf16[64,128,256]{2,1,0:T(8,128)(2,1)}, u32[]{:S(2)}, u32[]{:S(2)}) async-start(bf16[64,128,256]{2,1,0:T(8,128)(2,1)} %gather_fusion.1), calls=%async_computation.1 | async-start | bytes 8388608 | tf_op jit(solution)/shard_map/all_to_all | solution.py:170
  44.1 109.3 %all-gather.2.cloned.1.call-start = ((), (), s32[]{:S(2)}) async-start(), calls=%async_computation.5 | async-start | bytes 7864320 | tf_op jit(solution)/shard_map/all_gather | solution.py:154
  47.7 99.1 %copy-start.3 = (bf16[48,128,256]{2,1,0:T(8,128)(2,1)S(1)}, bf16[48,128,256]{2,1,0:T(8,128)(2,1)}, u32[]{:S(2)}) copy-start(bf16[48,128,256]{2,1,0:T(8,128)(2,1)} %get-tuple-element.17) | copy-start | bytes 9437188
  139.2 102.1 %all-to-all-start.3 = ((bf16[64,128,256]{2,1,0:T(8,128)(2,1)}), bf16[64,128,256]{2,1,0:T(8,128)(2,1)}, u32[]{:S(2)}, u32[]{:S(2)}) async-start(bf16[64,128,256]{2,1,0:T(8,128)(2,1)} %gather_fusion.3), calls=%async_computation.3 | async-start | bytes 8388608 | tf_op jit(solution)/shard_map/all_to_all | solution.py:170
  241.3 101.9 %all-to-all-start.2 = ((bf16[64,128,256]{2,1,0:T(8,128)(2,1)}), bf16[64,128,256]{2,1,0:T(8,128)(2,1)}, u32[]{:S(2)}, u32[]{:S(2)}) async-start(bf16[64,128,256]{2,1,0:T(8,128)(2,1)} %gather_fusion), calls=%async_computation.2 | async-start | bytes 8388608 | tf_op jit(solution)/shard_map/all_to_all | solution.py:170
  257.2 1.1 copy-start
  343.2 101.9 %all-to-all-start.4 = ((bf16[64,128,256]{2,1,0:T(8,128)(2,1)}), bf16[64,128,256]{2,1,0:T(8,128)(2,1)}, u32[]{:S(2)}, u32[]{:S(2)}) async-start(bf16[64,128,256]{2,1,0:T(8,128)(2,1)} %gather_fusion.2), calls=%async_computation.4 | async-start | bytes 8388608 | tf_op jit(solution)/shard_map/all_to_all | solution.py:170
  357.2 88.0 %copy-start.1 = (f32[4,128,768]{2,1,0:T(8,128)S(1)}, f32[4,128,768]{2,1,0:T(8,128)}, u32[]{:S(2)}) copy-start(f32[4,128,768]{2,1,0:T(8,128)} %copy-done) | copy-start | bytes 4718596
Sparse Core Ops, SparseCore 0:
  46.8 69.5 all-gather.1

commit v7 on v6

--- a/solution.py
+++ b/solution.py
@@ -153,31 +153,29 @@
     arrived_labels = arrived_labels.reshape(wide_count, most_slots, 2)
     gathered = lax.all_gather(panel, "grp", axis=0, tiled=True)
     panel_tiles = gathered.reshape(gathered.shape[0] // tile_side, tile_side, gathered.shape[1])
-    band = tile_side // 2
+    band = tile_side * 3 // 4
     arrived_labels = arrived_labels.reshape(wide_count, most_slots, 2)
     schedules = [slot_order(arrived_labels[:, rank, :], out_dev) for rank in range(most_slots)]
-    outgoing = {}
+    picks = []
     for rank in range(most_slots):
         chunk_index = jnp.where(ranking == rank, target, wide_count)
-        picks = jnp.full((wide_count,), tile_dev, jnp.int32).at[chunk_index].set(
+        picks.append(jnp.full((wide_count,), tile_dev, jnp.int32).at[chunk_index].set(
             jnp.arange(tile_dev, dtype=jnp.int32), mode="drop"
-        )
-        for half in range(2):
-            rows = tiles[:, half * band:(half + 1) * band, :]
-            outgoing[rank, half] = jnp.take(rows, picks, axis=0, mode="clip")
+        ))
+    first = jnp.take(tiles, picks[0], axis=0, mode="clip")
+    upper_out = jnp.take(tiles[:, :band, :], picks[1], axis=0, mode="clip")
+    lower_out = jnp.take(tiles[:, band:, :], picks[1], axis=0, mode="clip")
 
     def exchange(block):
         return lax.all_to_all(block, "wide", split_axis=0, concat_axis=0, tiled=True)
 
-    zero = jnp.zeros((out_dev, band, gathered.shape[1]), jnp.float32)
-    upper = add_products(exchange(outgoing[0, 0]), schedules[0], panel_tiles, zero)
-    lower = add_products(exchange(outgoing[0, 1]), schedules[0], panel_tiles, zero)
-    late, upper = lax.optimization_barrier((outgoing[1, 0], upper))
-    upper = add_products(exchange(late), schedules[1], panel_tiles, upper)
-    late, lower = lax.optimization_barrier((outgoing[1, 1], lower))
-    arrived = exchange(late)
+    zero = jnp.zeros((out_dev, tile_side, gathered.shape[1]), jnp.float32)
+    whole = add_products(exchange(first), schedules[0], panel_tiles, zero)
+    upper = add_products(exchange(upper_out), schedules[1], panel_tiles, whole[:, :band, :])
+    lower_out, whole = lax.optimization_barrier((lower_out, whole))
+    arrived = exchange(lower_out)
     upper = ring_sum(upper, lax.axis_size("grp"), 0)
-    lower = add_products(arrived, schedules[1], panel_tiles, lower)
+    lower = add_products(arrived, schedules[1], panel_tiles, whole[:, band:, :])
     lower = ring_sum(lower, lax.axis_size("grp"), 1)
     summed = jnp.concatenate([upper, lower], axis=1)
     return summed.reshape(out_dev * tile_side, gathered.shape[1])

time: 506 us -> 501 us (level)
  waiting for transfers between devices: 306 us -> 288 us
  Pallas kernels: 102 us -> 115 us
  starting transfers between devices: 42 us -> 35 us
    all_to_all x4 -> x3, waiting for transfers between devices: 305 us -> 223 us  [exchange(): lax.all_to_all(block, 'wide', split_axis=0, concat_axis=0, tiled=True)]
    all_gather x1, waiting for transfers between devices: 0.01 us -> 65.1 us  [per_device(): gathered = lax.all_gather(panel, 'grp', axis=0, tiled=True)]
    pallas_call x4 -> x3, Pallas kernels: 18.5 us -> 32.4 us  [add_products(): pl.pallas_call(products_kernel, out_shape=jax.ShapeDtypeStruct(running.sh...]
    all_to_all x4 -> x3, starting transfers between devices: 30.4 us -> 23.4 us  [exchange(): lax.all_to_all(block, 'wide', split_axis=0, concat_axis=0, tiled=True)]
    gather x4 -> x3, local copies, waits for them, and re-layouts: 15.4 us -> 16.1 us  [the longest x1 8.2 us: per_device(): first = jnp.take(tiles, picks[0], axis=0, mode='clip')]
  transfers between devices with their start and end apart: 6 -> 5, of which waited for: 4 -> 3; matrix products, arithmetic and copies ran while one was open for 5% -> 6% of each run, Pallas kernels for 11% -> 17%
where the time goes in v7:
time: 501 us; the launch traced here: 491 us
  waiting for transfers between devices  288 us (57%)
  Pallas kernels  115 us (23%)
  starting transfers between devices  35 us (7%)
  local copies, waits for them, and re-layouts  29.5 us (6%)
  between operations  14.9 us (3%)
  other arithmetic  8.46 us (2%)
    all_to_all x3, waiting for transfers between devices, exchange(): lax.all_to_all(block, 'wide', split_axis=0, concat_axis=0, tiled=True)  223 us
    pallas_call x2, Pallas kernels, ring_sum(): pl.pallas_call(functools.partial(ring_sum_kernel, n), out_shape=jax.Shape...  82.6 us
    all_gather x1, waiting for transfers between devices, per_device(): gathered = lax.all_gather(panel, 'grp', axis=0, tiled=True)  65.1 us
    pallas_call x3, Pallas kernels, add_products(): pl.pallas_call(products_kernel, out_shape=jax.ShapeDtypeStruct(running.sh...  32.4 us
    all_to_all x3, starting transfers between devices, exchange(): lax.all_to_all(block, 'wide', split_axis=0, concat_axis=0, tiled=True)  23.4 us
    all_to_all x1, starting transfers between devices, per_device(): lax.all_to_all(label_out, 'wide', split_axis=0, concat_axis=0, tiled=True)  11.5 us
  transfers between devices with their start and end apart: 5, of which 3 were waited for; matrix products, arithmetic and copies ran while one was open for 6% of the time, Pallas kernels for 17%

profile of v7, /device:TPU:36, one launch (start us, length us, event | category | flops | bytes accessed | tf_op | source)
XLA Modules:
  0.0 491.1 jit_solution(2213420282584525457)
XLA Ops:
  6.5 0.8 copy.24
  7.4 0.9 select_reduce_fusion
  8.2 0.2 convert_reduce_fusion
  8.5 0.7 pad_add_fusion
  9.1 0.1 copy.15
  9.2 0.8 scatter_fusion
  10.0 1.1 copy.17
  11.1 11.5 %all-to-all-start = ((s32[64,2,2]{1,2,0:T(2,128)}), s32[64,2,2]{1,2,0:T(2,128)S(1)}, u32[]{:S(2)}, u32[]{:S(2)}) async-start(s32[64,2,2]{1,2,0:T(2,128)} %copy.17), calls=%async_computation | async-start | bytes 131072 | tf_op jit(solution)/shard_map/all_to_all | solution.py:152
  22.6 0.7 scatter_custom_fusion.2
  23.4 8.2 %gather_fusion.1 = bf16[64,256,256]{2,1,0:T(8,128)(2,1)} fusion(bf16[48,256,256]{2,1,0:T(8,128)(2,1)} %param.5, s32[1024]{0:T(1024)S(1)} %pad_clamp_fusion), kind=kCustom, calls=%fused_computation.1 | custom fusion | bytes 16777472 | tf_op jit(solution)/shard_map/jit(_take)/gather | solution.py:165
  31.6 0.0 all-to-all-done
  31.6 10.5 %all-to-all-start.2 = ((bf16[64,256,256]{2,1,0:T(8,128)(2,1)}), bf16[64,256,256]{2,1,0:T(8,128)(2,1)}, u32[]{:S(2)}, u32[]{:S(2)}) async-start(bf16[64,256,256]{2,1,0:T(8,128)(2,1)} %gather_fusion.1), calls=%async_computation.2 | async-start | bytes 16777216 | tf_op jit(solution)/shard_map/all_to_all | solution.py:170
  42.1 5.1 %slice.33 = bf16[48,192,256]{2,1,0:T(8,128)(2,1)} slice(bf16[48,256,256]{2,1,0:T(8,128)(2,1)} %param.5), slice={[0:48], [0:192], [0:256]} | slice | bytes 9437184 | tf_op jit(solution)/shard_map/slice | solution.py:166
  47.2 0.7 scatter_custom_fusion.1
  48.0 5.9 %gather_fusion = bf16[64,192,256]{2,1,0:T(8,128)(2,1)} fusion(bf16[48,192,256]{2,1,0:T(8,128)(2,1)} %slice.33, s32[1024]{0:T(1024)S(1)} %pad_clamp_fusion.1), kind=kCustom, calls=%fused_computation | custom fusion | bytes 12583168 | tf_op jit(solution)/shard_map/jit(_take)/gather | solution.py:166
  53.9 174.4 %all-to-all-done.2.arrived_ref = bf16[64,256,256]{2,1,0:T(8,128)(2,1)} async-done(((bf16[64,256,256]{2,1,0:T(8,128)(2,1)}), bf16[64,256,256]{2,1,0:T(8,128)(2,1)}, u32[]{:S(2)}, u32[]{:S(2)}) %all-to-all-start.2) | async-done | bytes 8388640 | tf_op jit(solution)/shard_map/all_to_all | solution.py:170
  228.3 6.4 %all-to-all-start.1 = ((bf16[64,192,256]{2,1,0:T(8,128)(2,1)}), bf16[64,192,256]{2,1,0:T(8,128)(2,1)}, u32[]{:S(2)}, u32[]{:S(2)}) async-start(bf16[64,192,256]{2,1,0:T(8,128)(2,1)} %gather_fusion), calls=%async_computation.1 | async-start | bytes 12582912 | tf_op jit(solution)/shard_map/all_to_all | solution.py:170
  234.7 0.0 slice-start
  234.8 0.0 all-gather.2.cloned.1.call-start
  234.8 0.7 all-gather.2.cloned.1.call-update
  235.5 0.7 slice-done
  236.2 2.0 gather_fusion.2
  238.1 0.1 fusion.10
  238.3 0.1 copy.18
  238.4 0.1 copy.19
  238.4 0.7 fusion.8
  239.8 2.0 sort.32
  241.9 65.1 %all-gather.2.cloned.1.call-done = bf16[4096,768]{1,0:T(8,128)(2,1)} async-done(((bf16[1024,768]{1,0:T(8,128)(2,1)}), bf16[4096,768]{1,0:T(8,128)(2,1)}) %all-gather.2.cloned.1.call-update) | async-done | bytes 6291472 | tf_op jit(solution)/shard_map/all_gather | solution.py:154
  307.0 1.9 broadcast_in_dim.40.init_ref
  308.9 18.2 %shard_map.55 = f32[4,256,768]{2,1,0:T(8,128)S(1)} custom-call(s32[1]{0:T(128)} %bitcast.13.count_ref, s32[64]{0:T(128)S(1)} %get-tuple-element.10.order_ref, s32[64]{0:T(128)S(1)} %get-tuple-element.19.rows_ref, s32[64]{0:T(128)S(1)} %get-tuple-element.18.ks_ref, bf16[64,256,256]{2,1,0:T(8,128)(2,1)} %all-to-all-done.2.arrived_ref, ...), custom_call_target="tpu_custom_call" | custom-call | tf_op jit(solution)/shard_map/pallas_call | solution.py:130
  327.2 48.1 %all-to-all-done.1.arrived_ref = bf16[64,192,256]{2,1,0:T(8,128)(2,1)} async-done(((bf16[64,192,256]{2,1,0:T(8,128)(2,1)}), bf16[64,192,256]{2,1,0:T(8,128)(2,1)}, u32[]{:S(2)}, u32[]{:S(2)}) %all-to-all-start.1) | async-done | bytes 6291488 | tf_op jit(solution)/shard_map/all_to_all | solution.py:170
  375.3 6.5 %all-to-all-start.3 = ((bf16[64,64,256]{2,1,0:T(8,128)(2,1)}), bf16[64,64,256]{2,1,0:T(8,128)(2,1)}, u32[]{:S(2)}, u32[]{:S(2)}) async-start(bf16[64,64,256]{2,1,0:T(8,128)(2,1)} %gather_fusion.2), calls=%async_computation.3 | async-start | bytes 4194304 | tf_op jit(solution)/shard_map/all_to_all | solution.py:170
  382.5 2.0 sort.31
  384.5 0.2 slice.48.init_ref
  384.7 0.9 slice.39.init_ref
  385.6 8.0 %shard_map.56.x_ref = f32[4,192,768]{2,1,0:T(8,128)S(1)} custom-call(s32[1]{0:T(128)} %bitcast.7.count_ref, s32[64]{0:T(128)S(1)} %get-tuple-element.9.order_ref, s32[64]{0:T(128)S(1)} %get-tuple-element.21.rows_ref, s32[64]{0:T(128)S(1)} %get-tuple-element.20.ks_ref, bf16[64,192,256]{2,1,0:T(8,128)(2,1)} %all-to-all-done.1.arrived_ref, ...), custom_call_target="tpu_custom_call" | custom-call | tf_op jit(solution)/shard_map/pallas_call | solution.py:130
  393.6 0.0 copy-start
  393.6 55.7 %shard_map.57 = f32[4,192,768]{2,1,0:T(8,128)S(1)} custom-call(f32[4,192,768]{2,1,0:T(8,128)S(1)} %shard_map.56.x_ref), custom_call_target="tpu_custom_call" | custom-call | tf_op jit(solution)/shard_map/pallas_call | solution.py:71
  449.3 0.0 all-to-all-done.3.arrived_ref
  449.3 0.0 copy-done
  449.3 6.1 %shard_map.58.x_ref = f32[4,64,768]{2,1,0:T(8,128)S(1)} custom-call(s32[1]{0:T(128)} %bitcast.7.count_ref, s32[64]{0:T(128)S(1)} %get-tuple-element.9.order_ref, s32[64]{0:T(128)S(1)} %get-tuple-element.21.rows_ref, s32[64]{0:T(128)S(1)} %get-tuple-element.20.ks_ref, bf16[64,64,256]{2,1,0:T(8,128)(2,1)} %all-to-all-done.3.arrived_ref, ...), custom_call_target="tpu_custom_call" | custom-call | tf_op jit(solution)/shard_map/pallas_call | solution.py:130
  455.5 26.9 %shard_map.59 = f32[4,64,768]{2,1,0:T(8,128)S(1)} custom-call(f32[4,64,768]{2,1,0:T(8,128)S(1)} %shard_map.58.x_ref), custom_call_target="tpu_custom_call" | custom-call | tf_op jit(solution)/shard_map/pallas_call | solution.py:71
  482.4 1.9 pad_maximum_fusion
  (12 shorter events, 0.1 us)
Async XLA Ops:
  11.1 20.5 %all-to-all-start = ((s32[64,2,2]{1,2,0:T(2,128)}), s32[64,2,2]{1,2,0:T(2,128)S(1)}, u32[]{:S(2)}, u32[]{:S(2)}) async-start(s32[64,2,2]{1,2,0:T(2,128)} %copy.17), calls=%async_computation | async-start | bytes 131072 | tf_op jit(solution)/shard_map/all_to_all | solution.py:152
  31.6 196.7 %all-to-all-start.2 = ((bf16[64,256,256]{2,1,0:T(8,128)(2,1)}), bf16[64,256,256]{2,1,0:T(8,128)(2,1)}, u32[]{:S(2)}, u32[]{:S(2)}) async-start(bf16[64,256,256]{2,1,0:T(8,128)(2,1)} %gather_fusion.1), calls=%async_computation.2 | async-start | bytes 16777216 | tf_op jit(solution)/shard_map/all_to_all | solution.py:170
  228.3 147.0 %all-to-all-start.1 = ((bf16[64,192,256]{2,1,0:T(8,128)(2,1)}), bf16[64,192,256]{2,1,0:T(8,128)(2,1)}, u32[]{:S(2)}, u32[]{:S(2)}) async-start(bf16[64,192,256]{2,1,0:T(8,128)(2,1)} %gather_fusion), calls=%async_computation.1 | async-start | bytes 12582912 | tf_op jit(solution)/shard_map/all_to_all | solution.py:170
  234.7 1.4 slice-start
  234.8 72.3 %all-gather.2.cloned.1.call-start = ((), (), s32[]{:S(2)}) async-start(), calls=%async_computation.4 | async-start | bytes 7864320 | tf_op jit(solution)/shard_map/all_gather | solution.py:154
  375.3 74.0 %all-to-all-start.3 = ((bf16[64,64,256]{2,1,0:T(8,128)(2,1)}), bf16[64,64,256]{2,1,0:T(8,128)(2,1)}, u32[]{:S(2)}, u32[]{:S(2)}) async-start(bf16[64,64,256]{2,1,0:T(8,128)(2,1)} %gather_fusion.2), calls=%async_computation.3 | async-start | bytes 4194304 | tf_op jit(solution)/shard_map/all_to_all | solution.py:170
  393.6 55.7 %copy-start = (f32[4,64,768]{2,1,0:T(8,128)S(1)}, f32[4,64,768]{2,1,0:T(8,128)}, u32[]{:S(2)}) copy-start(f32[4,64,768]{2,1,0:T(8,128)} %slice.39.init_ref) | copy-start | bytes 2359300
Sparse Core Ops, SparseCore 0:
  237.4 69.5 all-gather.1

commit v8 on v7

--- a/solution.py
+++ b/solution.py
@@ -153,7 +153,7 @@
     arrived_labels = arrived_labels.reshape(wide_count, most_slots, 2)
     gathered = lax.all_gather(panel, "grp", axis=0, tiled=True)
     panel_tiles = gathered.reshape(gathered.shape[0] // tile_side, tile_side, gathered.shape[1])
-    band = tile_side * 3 // 4
+    band = tile_side * 5 // 8
     arrived_labels = arrived_labels.reshape(wide_count, most_slots, 2)
     schedules = [slot_order(arrived_labels[:, rank, :], out_dev) for rank in range(most_slots)]
     picks = []

time: 501 us -> 489 us (0.976)
  waiting for transfers between devices: 288 us -> 277 us
  local copies, waits for them, and re-layouts: 29.5 us -> 36 us
    all_to_all x3, waiting for transfers between devices: 223 us -> 212 us  [exchange(): lax.all_to_all(block, 'wide', split_axis=0, concat_axis=0, tiled=True)]
    pallas_call x2, Pallas kernels: 82.6 us -> 75 us  [ring_sum(): pl.pallas_call(functools.partial(ring_sum_kernel, n), out_shape=jax.Shape...]
  transfers between devices with their start and end apart: 5 -> 5, of which waited for: 3 -> 4; matrix products, arithmetic and copies ran while one was open for 6% -> 7% of each run, Pallas kernels for 17% -> 15%
where the time goes in v8:
time: 489 us; the launch traced here: 482 us
  waiting for transfers between devices  277 us (57%)
  Pallas kernels  111 us (23%)
  local copies, waits for them, and re-layouts  36 us (7%)
  starting transfers between devices  35.3 us (7%)
  between operations  14.9 us (3%)
  other arithmetic  8.53 us (2%)
    all_to_all x3, waiting for transfers between devices, exchange(): lax.all_to_all(block, 'wide', split_axis=0, concat_axis=0, tiled=True)  212 us
    pallas_call x2, Pallas kernels, ring_sum(): pl.pallas_call(functools.partial(ring_sum_kernel, n), out_shape=jax.Shape...  75 us
    all_gather x1, waiting for transfers between devices, per_device(): gathered = lax.all_gather(panel, 'grp', axis=0, tiled=True)  64.5 us
    pallas_call x3, Pallas kernels, add_products(): pl.pallas_call(products_kernel, out_shape=jax.ShapeDtypeStruct(running.sh...  35.7 us
    all_to_all x3, starting transfers between devices, exchange(): lax.all_to_all(block, 'wide', split_axis=0, concat_axis=0, tiled=True)  23.7 us
    all_to_all x1, starting transfers between devices, per_device(): lax.all_to_all(label_out, 'wide', split_axis=0, concat_axis=0, tiled=True)  11.5 us
  transfers between devices with their start and end apart: 5, of which 4 were waited for; matrix products, arithmetic and copies ran while one was open for 7% of the time, Pallas kernels for 15%

profile of v8, /device:TPU:36, one launch (start us, length us, event | category | flops | bytes accessed | tf_op | source)
XLA Modules:
  0.0 482.4 jit_solution(2791459635933406026)
XLA Ops:
  6.5 0.9 select_reduce_fusion
  7.4 0.2 convert_reduce_fusion
  7.6 0.7 pad_add_fusion
  8.3 0.1 copy.15
  8.4 0.8 copy.24
  9.2 0.7 scatter_fusion
  10.0 1.1 copy.17
  11.1 11.5 %all-to-all-start = ((s32[64,2,2]{1,2,0:T(2,128)}), s32[64,2,2]{1,2,0:T(2,128)S(1)}, u32[]{:S(2)}, u32[]{:S(2)}) async-start(s32[64,2,2]{1,2,0:T(2,128)} %copy.17), calls=%async_computation | async-start | bytes 131072 | tf_op jit(solution)/shard_map/all_to_all | solution.py:152
  22.6 0.7 scatter_custom_fusion.2
  23.4 8.2 %gather_fusion.1 = bf16[64,256,256]{2,1,0:T(8,128)(2,1)} fusion(bf16[48,256,256]{2,1,0:T(8,128)(2,1)} %param.5, s32[1024]{0:T(1024)S(1)} %pad_clamp_fusion), kind=kCustom, calls=%fused_computation.1 | custom fusion | bytes 16777472 | tf_op jit(solution)/shard_map/jit(_take)/gather | solution.py:165
  31.6 0.0 all-to-all-done
  31.6 10.5 %all-to-all-start.2 = ((bf16[64,256,256]{2,1,0:T(8,128)(2,1)}), bf16[64,256,256]{2,1,0:T(8,128)(2,1)}, u32[]{:S(2)}, u32[]{:S(2)}) async-start(bf16[64,256,256]{2,1,0:T(8,128)(2,1)} %gather_fusion.1), calls=%async_computation.2 | async-start | bytes 16777216 | tf_op jit(solution)/shard_map/all_to_all | solution.py:170
  42.1 4.3 slice.33
  46.4 0.7 scatter_custom_fusion.1
  47.1 5.3 %gather_fusion = bf16[64,160,256]{2,1,0:T(8,128)(2,1)} fusion(bf16[48,160,256]{2,1,0:T(8,128)(2,1)} %slice.33, s32[1024]{0:T(1024)S(1)} %pad_clamp_fusion.1), kind=kCustom, calls=%fused_computation | custom fusion | bytes 10486016 | tf_op jit(solution)/shard_map/jit(_take)/gather | solution.py:166
  52.4 175.9 %all-to-all-done.2.arrived_ref = bf16[64,256,256]{2,1,0:T(8,128)(2,1)} async-done(((bf16[64,256,256]{2,1,0:T(8,128)(2,1)}), bf16[64,256,256]{2,1,0:T(8,128)(2,1)}, u32[]{:S(2)}, u32[]{:S(2)}) %all-to-all-start.2) | async-done | bytes 8388640 | tf_op jit(solution)/shard_map/all_to_all | solution.py:170
  228.3 6.4 %all-to-all-start.1 = ((bf16[64,160,256]{2,1,0:T(8,128)(2,1)}), bf16[64,160,256]{2,1,0:T(8,128)(2,1)}, u32[]{:S(2)}, u32[]{:S(2)}) async-start(bf16[64,160,256]{2,1,0:T(8,128)(2,1)} %gather_fusion), calls=%async_computation.1 | async-start | bytes 10485760 | tf_op jit(solution)/shard_map/all_to_all | solution.py:170
  234.7 0.0 slice-start
  234.7 0.0 all-gather.2.cloned.1.call-start
  234.8 0.7 all-gather.2.cloned.1.call-update
  235.5 0.9 slice-done
  236.4 2.4 gather_fusion.2
  238.8 0.1 fusion.10
  238.9 0.1 copy.19
  239.0 0.1 copy.18
  239.1 0.7 fusion.8
  240.5 2.0 sort.32
  242.5 64.5 %all-gather.2.cloned.1.call-done = bf16[4096,768]{1,0:T(8,128)(2,1)} async-done(((bf16[1024,768]{1,0:T(8,128)(2,1)}), bf16[4096,768]{1,0:T(8,128)(2,1)}) %all-gather.2.cloned.1.call-update) | async-done | bytes 6291472 | tf_op jit(solution)/shard_map/all_gather | solution.py:154
  307.0 2.0 broadcast_in_dim.40.init_ref
  309.0 19.9 %shard_map.55 = f32[4,256,768]{2,1,0:T(8,128)S(1)} custom-call(s32[1]{0:T(128)} %bitcast.13.count_ref, s32[64]{0:T(128)S(1)} %get-tuple-element.10.order_ref, s32[64]{0:T(128)S(1)} %get-tuple-element.19.rows_ref, s32[64]{0:T(128)S(1)} %get-tuple-element.18.ks_ref, bf16[64,256,256]{2,1,0:T(8,128)(2,1)} %all-to-all-done.2.arrived_ref, ...), custom_call_target="tpu_custom_call" | custom-call | tf_op jit(solution)/shard_map/pallas_call | solution.py:130
  328.9 0.0 copy-start
  328.9 1.7 copy-done
  330.6 21.5 %all-to-all-done.1.arrived_ref = bf16[64,160,256]{2,1,0:T(8,128)(2,1)} async-done(((bf16[64,160,256]{2,1,0:T(8,128)(2,1)}), bf16[64,160,256]{2,1,0:T(8,128)(2,1)}, u32[]{:S(2)}, u32[]{:S(2)}) %all-to-all-start.1) | async-done | bytes 5242912 | tf_op jit(solution)/shard_map/all_to_all | solution.py:170
  352.1 6.8 %all-to-all-start.3 = ((bf16[64,96,256]{2,1,0:T(8,128)(2,1)}), bf16[64,96,256]{2,1,0:T(8,128)(2,1)S(1)}, u32[]{:S(2)}, u32[]{:S(2)}) async-start(bf16[64,96,256]{2,1,0:T(8,128)(2,1)} %gather_fusion.2), calls=%async_computation.3 | async-start | bytes 6291456 | tf_op jit(solution)/shard_map/all_to_all | solution.py:170
  359.5 2.1 sort.31
  361.6 1.7 slice.48.init_ref
  363.3 8.9 %shard_map.56.x_ref = f32[4,160,768]{2,1,0:T(8,128)S(1)} custom-call(s32[1]{0:T(128)} %bitcast.7.count_ref, s32[64]{0:T(128)S(1)} %get-tuple-element.9.order_ref, s32[64]{0:T(128)S(1)} %get-tuple-element.21.rows_ref, s32[64]{0:T(128)S(1)} %get-tuple-element.20.ks_ref, bf16[64,160,256]{2,1,0:T(8,128)(2,1)} %all-to-all-done.1.arrived_ref, ...), custom_call_target="tpu_custom_call" | custom-call | tf_op jit(solution)/shard_map/pallas_call | solution.py:130
  372.3 41.3 %shard_map.57 = f32[4,160,768]{2,1,0:T(8,128)S(1)} custom-call(f32[4,160,768]{2,1,0:T(8,128)S(1)} %shard_map.56.x_ref), custom_call_target="tpu_custom_call" | custom-call | tf_op jit(solution)/shard_map/pallas_call | solution.py:71
  413.6 0.0 copy-start.1
  413.6 1.3 copy-done.1
  414.9 2.4 slice.39.init_ref
  417.3 14.5 %all-to-all-done.3.arrived_ref = bf16[64,96,256]{2,1,0:T(8,128)(2,1)S(1)} async-done(((bf16[64,96,256]{2,1,0:T(8,128)(2,1)}), bf16[64,96,256]{2,1,0:T(8,128)(2,1)S(1)}, u32[]{:S(2)}, u32[]{:S(2)}) %all-to-all-start.3) | async-done | bytes 3145760 | tf_op jit(solution)/shard_map/all_to_all | solution.py:170
  431.7 0.0 copy-start.3
  431.7 1.3 copy-done.3
  433.0 6.9 %shard_map.58.x_ref = f32[4,96,768]{2,1,0:T(8,128)S(1)} custom-call(s32[1]{0:T(128)} %bitcast.7.count_ref, s32[64]{0:T(128)S(1)} %get-tuple-element.9.order_ref, s32[64]{0:T(128)S(1)} %get-tuple-element.21.rows_ref, s32[64]{0:T(128)S(1)} %get-tuple-element.20.ks_ref, bf16[64,96,256]{2,1,0:T(8,128)(2,1)S(1)} %all-to-all-done.3.arrived_ref, ...), custom_call_target="tpu_custom_call" | custom-call | tf_op jit(solution)/shard_map/pallas_call | solution.py:130
  439.9 0.0 copy-start.2
  439.9 33.7 %shard_map.59 = f32[4,96,768]{2,1,0:T(8,128)S(1)} custom-call(f32[4,96,768]{2,1,0:T(8,128)S(1)} %shard_map.58.x_ref), custom_call_target="tpu_custom_call" | custom-call | tf_op jit(solution)/shard_map/pallas_call | solution.py:71
  473.6 0.0 copy-done.2
  473.6 2.0 pad_maximum_fusion
  (12 shorter events, 0.1 us)
Async XLA Ops:
  11.1 20.5 %all-to-all-start = ((s32[64,2,2]{1,2,0:T(2,128)}), s32[64,2,2]{1,2,0:T(2,128)S(1)}, u32[]{:S(2)}, u32[]{:S(2)}) async-start(s32[64,2,2]{1,2,0:T(2,128)} %copy.17), calls=%async_computation | async-start | bytes 131072 | tf_op jit(solution)/shard_map/all_to_all | solution.py:152
  31.6 196.7 %all-to-all-start.2 = ((bf16[64,256,256]{2,1,0:T(8,128)(2,1)}), bf16[64,256,256]{2,1,0:T(8,128)(2,1)}, u32[]{:S(2)}, u32[]{:S(2)}) async-start(bf16[64,256,256]{2,1,0:T(8,128)(2,1)} %gather_fusion.1), calls=%async_computation.2 | async-start | bytes 16777216 | tf_op jit(solution)/shard_map/all_to_all | solution.py:170
  228.3 123.8 %all-to-all-start.1 = ((bf16[64,160,256]{2,1,0:T(8,128)(2,1)}), bf16[64,160,256]{2,1,0:T(8,128)(2,1)}, u32[]{:S(2)}, u32[]{:S(2)}) async-start(bf16[64,160,256]{2,1,0:T(8,128)(2,1)} %gather_fusion), calls=%async_computation.1 | async-start | bytes 10485760 | tf_op jit(solution)/shard_map/all_to_all | solution.py:170
  234.7 1.7 slice-start
  234.7 72.3 %all-gather.2.cloned.1.call-start = ((), (), s32[]{:S(2)}) async-start(), calls=%async_computation.4 | async-start | bytes 7864320 | tf_op jit(solution)/shard_map/all_gather | solution.py:154
  328.9 1.7 copy-start
  352.1 79.7 %all-to-all-start.3 = ((bf16[64,96,256]{2,1,0:T(8,128)(2,1)}), bf16[64,96,256]{2,1,0:T(8,128)(2,1)S(1)}, u32[]{:S(2)}, u32[]{:S(2)}) async-start(bf16[64,96,256]{2,1,0:T(8,128)(2,1)} %gather_fusion.2), calls=%async_computation.3 | async-start | bytes 6291456 | tf_op jit(solution)/shard_map/all_to_all | solution.py:170
  413.6 1.3 copy-start.1
  431.7 1.3 copy-start.3
  439.9 33.7 %copy-start.2 = (f32[4,160,768]{2,1,0:T(8,128)S(1)}, f32[4,160,768]{2,1,0:T(8,128)}, u32[]{:S(2)}) copy-start(f32[4,160,768]{2,1,0:T(8,128)} %copy-done.1) | copy-start | bytes 5898244
Sparse Core Ops, SparseCore 0:
  237.4 69.5 all-gather.1

commit v9 on v8

--- a/solution.py
+++ b/solution.py
@@ -151,8 +151,17 @@
     label_out = vacant_label.at[slot_index].set(jnp.stack([local_row, contraction], axis=1))
     arrived_labels = lax.all_to_all(label_out, "wide", split_axis=0, concat_axis=0, tiled=True)
     arrived_labels = arrived_labels.reshape(wide_count, most_slots, 2)
-    gathered = lax.all_gather(panel, "grp", axis=0, tiled=True)
+    grp_count = lax.axis_size("grp")
+    pieces = [panel] + [
+        lax.ppermute(panel, "grp", [(j, (j + shift) % grp_count) for j in range(grp_count)])
+        for shift in range(1, grp_count)
+    ]
+    gathered = jnp.concatenate(pieces, axis=0)
     panel_tiles = gathered.reshape(gathered.shape[0] // tile_side, tile_side, gathered.shape[1])
+    held = panel.shape[0] // tile_side
+    owner = arrived_labels[..., 1] // held
+    shift = lax.rem(lax.axis_index("grp") - owner + grp_count, grp_count)
+    arrived_labels = arrived_labels.at[..., 1].set(shift * held + arrived_labels[..., 1] % held)
     band = tile_side * 5 // 8
     arrived_labels = arrived_labels.reshape(wide_count, most_slots, 2)
     schedules = [slot_order(arrived_labels[:, rank, :], out_dev) for rank in range(most_slots)]

time: 489 us -> 475 us (0.971)
  Pallas kernels: 111 us -> 91.6 us
  between operations: 14.9 us -> 1.39 us
  other arithmetic: 8.53 us -> 15.3 us
  starting transfers between devices: 35.3 us -> 41.1 us
  waiting for transfers between devices: 277 us -> 282 us
    all_gather x1 -> x0, waiting for transfers between devices: 64.5 us -> none  [per_device(): gathered = lax.all_gather(panel, 'grp', axis=0, tiled=True)]
    ppermute x0 -> x3, waiting for transfers between devices: none -> 60.6 us  [per_device(): lax.ppermute(panel, 'grp', [(j, (j + shift) % grp_count) for j in range(g...]
    pallas_call x3, Pallas kernels: 35.7 us -> 13.7 us  [add_products(): pl.pallas_call(products_kernel, out_shape=jax.ShapeDtypeStruct(running.sh...]
    all_to_all x3, waiting for transfers between devices: 212 us -> 222 us  [exchange(): lax.all_to_all(block, 'wide', split_axis=0, concat_axis=0, tiled=True)]
    concatenate x0 -> x1, other arithmetic: none -> 6.55 us  [per_device(): gathered = jnp.concatenate(pieces, axis=0)]
    ppermute x0 -> x3, starting transfers between devices: none -> 5.87 us  [per_device(): lax.ppermute(panel, 'grp', [(j, (j + shift) % grp_count) for j in range(g...]
  transfers between devices with their start and end apart: 5 -> 7, of which waited for: 4 -> 5; matrix products, arithmetic and copies ran while one was open for 7% -> 9% of each run, Pallas kernels for 15% -> 11%
where the time goes in v9:
time: 475 us; the launch traced here: 467 us
  waiting for transfers between devices  282 us (59%)
  Pallas kernels  91.6 us (19%)
  starting transfers between devices  41.1 us (9%)
  local copies, waits for them, and re-layouts  35.3 us (7%)
  other arithmetic  15.3 us (3%)
    all_to_all x3, waiting for transfers between devices, exchange(): lax.all_to_all(block, 'wide', split_axis=0, concat_axis=0, tiled=True)  222 us
    pallas_call x2, Pallas kernels, ring_sum(): pl.pallas_call(functools.partial(ring_sum_kernel, n), out_shape=jax.Shape...  78 us
    ppermute x3, waiting for transfers between devices, per_device(): lax.ppermute(panel, 'grp', [(j, (j + shift) % grp_count) for j in range(g...  60.6 us
    all_to_all x3, starting transfers between devices, exchange(): lax.all_to_all(block, 'wide', split_axis=0, concat_axis=0, tiled=True)  23.7 us
    pallas_call x3, Pallas kernels, add_products(): pl.pallas_call(products_kernel, out_shape=jax.ShapeDtypeStruct(running.sh...  13.7 us
    all_to_all x1, starting transfers between devices, per_device(): lax.all_to_all(label_out, 'wide', split_axis=0, concat_axis=0, tiled=True)  11.5 us
  transfers between devices with their start and end apart: 7, of which 5 were waited for; matrix products, arithmetic and copies ran while one was open for 9% of the time, Pallas kernels for 11%

profile of v9, /device:TPU:36, one launch (start us, length us, event | category | flops | bytes accessed | tf_op | source)
XLA Modules:
  0.0 467.1 jit_solution(929264896144795305)
XLA Ops:
  0.0 0.9 select_reduce_fusion
  0.9 0.2 convert_reduce_fusion
  1.1 0.7 pad_add_fusion
  1.8 0.1 copy.15
  1.8 0.8 copy.25
  2.7 0.7 scatter_fusion
  3.4 1.1 copy.17
  4.5 11.5 %all-to-all-start = ((s32[64,2,2]{1,2,0:T(2,128)}), s32[64,2,2]{1,2,0:T(2,128)S(1)}, u32[]{:S(2)}, u32[]{:S(2)}) async-start(s32[64,2,2]{1,2,0:T(2,128)} %copy.17), calls=%async_computation | async-start | bytes 131072 | tf_op jit(solution)/shard_map/all_to_all | solution.py:152
  16.1 0.7 scatter_custom_fusion.2
  16.8 8.2 %gather_fusion.1 = bf16[64,256,256]{2,1,0:T(8,128)(2,1)} fusion(bf16[48,256,256]{2,1,0:T(8,128)(2,1)} %param.7, s32[1024]{0:T(1024)S(1)} %pad_clamp_fusion), kind=kCustom, calls=%fused_computation.1 | custom fusion | bytes 16777472 | tf_op jit(solution)/shard_map/jit(_take)/gather | solution.py:174
  25.1 0.0 all-to-all-done
  25.1 10.5 %all-to-all-start.2 = ((bf16[64,256,256]{2,1,0:T(8,128)(2,1)}), bf16[64,256,256]{2,1,0:T(8,128)(2,1)}, u32[]{:S(2)}, u32[]{:S(2)}) async-start(bf16[64,256,256]{2,1,0:T(8,128)(2,1)} %gather_fusion.1), calls=%async_computation.2 | async-start | bytes 16777216 | tf_op jit(solution)/shard_map/all_to_all | solution.py:179
  35.6 4.3 slice.58
  39.9 0.7 scatter_custom_fusion.1
  40.6 5.3 %gather_fusion = bf16[64,160,256]{2,1,0:T(8,128)(2,1)} fusion(bf16[48,160,256]{2,1,0:T(8,128)(2,1)} %slice.58, s32[1024]{0:T(1024)S(1)} %pad_clamp_fusion.1), kind=kCustom, calls=%fused_computation | custom fusion | bytes 10486016 | tf_op jit(solution)/shard_map/jit(_take)/gather | solution.py:175
  45.9 175.9 %all-to-all-done.2.arrived_ref = bf16[64,256,256]{2,1,0:T(8,128)(2,1)} async-done(((bf16[64,256,256]{2,1,0:T(8,128)(2,1)}), bf16[64,256,256]{2,1,0:T(8,128)(2,1)}, u32[]{:S(2)}, u32[]{:S(2)}) %all-to-all-start.2) | async-done | bytes 8388640 | tf_op jit(solution)/shard_map/all_to_all | solution.py:179
  221.8 6.4 %all-to-all-start.1 = ((bf16[64,160,256]{2,1,0:T(8,128)(2,1)}), bf16[64,160,256]{2,1,0:T(8,128)(2,1)}, u32[]{:S(2)}, u32[]{:S(2)}) async-start(bf16[64,160,256]{2,1,0:T(8,128)(2,1)} %gather_fusion), calls=%async_computation.1 | async-start | bytes 10485760 | tf_op jit(solution)/shard_map/all_to_all | solution.py:179
  228.2 0.0 slice-start
  228.2 1.6 collective-permute-start
  229.8 2.9 collective-permute-start.1
  232.8 1.3 collective-permute-start.2
  234.1 0.0 slice-done
  234.1 2.4 gather_fusion.2
  236.5 0.3 fusion
  236.9 0.2 scatter.27
  237.0 0.1 fusion.13
  237.2 0.1 copy.19
  237.2 0.1 copy.18
  237.3 0.7 fusion.11
  238.6 2.0 sort.32
  240.6 25.7 %collective-permute-done = bf16[1024,768]{1,0:T(8,128)(2,1)} collective-permute-done((bf16[1024,768]{1,0:T(8,128)(2,1)}, bf16[1024,768]{1,0:T(8,128)(2,1)}, u32[]{:S(2)}, u32[]{:S(2)}) %collective-permute-start) | collective-permute-done | bytes 1572896 | tf_op jit(solution)/shard_map/ppermute | solution.py:156
  266.3 34.9 %collective-permute-done.1 = bf16[1024,768]{1,0:T(8,128)(2,1)} collective-permute-done((bf16[1024,768]{1,0:T(8,128)(2,1)}, bf16[1024,768]{1,0:T(8,128)(2,1)}, u32[]{:S(2)}, u32[]{:S(2)}) %collective-permute-start.1) | collective-permute-done | bytes 1572896 | tf_op jit(solution)/shard_map/ppermute | solution.py:156
  301.2 0.0 collective-permute-done.2
  301.2 6.6 %pad_maximum_fusion = bf16[4096,768]{1,0:T(8,128)(2,1)} fusion(bf16[1024,768]{1,0:T(8,128)(2,1)} %collective-permute-done.2, bf16[1024,768]{1,0:T(8,128)(2,1)} %collective-permute-done.1, bf16[1024,768]{1,0:T(8,128)(2,1)} %collective-permute-done, bf16[1024,768]{1,0:T(8,128)(2,1)} %param.11), kind=kLoop, calls=%fused_computation.6 | loop fusion | flops 25165824 | bytes 12582912 | tf_op jit(solution)/shard_map/concatenate | solution.py:159
  307.8 2.0 broadcast_in_dim.40.init_ref
  309.8 6.3 %shard_map.55 = f32[4,256,768]{2,1,0:T(8,128)S(1)} custom-call(s32[1]{0:T(128)} %bitcast.13.count_ref, s32[64]{0:T(128)S(1)} %get-tuple-element.22.order_ref, s32[64]{0:T(128)S(1)} %get-tuple-element.31.rows_ref, s32[64]{0:T(128)S(1)} %get-tuple-element.30.ks_ref, bf16[64,256,256]{2,1,0:T(8,128)(2,1)} %all-to-all-done.2.arrived_ref, ...), custom_call_target="tpu_custom_call" | custom-call | tf_op jit(solution)/shard_map/pallas_call | solution.py:130
  316.1 0.0 copy-start
  316.1 1.7 copy-done
  317.8 27.8 %all-to-all-done.1.arrived_ref = bf16[64,160,256]{2,1,0:T(8,128)(2,1)} async-done(((bf16[64,160,256]{2,1,0:T(8,128)(2,1)}), bf16[64,160,256]{2,1,0:T(8,128)(2,1)}, u32[]{:S(2)}, u32[]{:S(2)}) %all-to-all-start.1) | async-done | bytes 5242912 | tf_op jit(solution)/shard_map/all_to_all | solution.py:179
  345.6 6.8 %all-to-all-start.3 = ((bf16[64,96,256]{2,1,0:T(8,128)(2,1)}), bf16[64,96,256]{2,1,0:T(8,128)(2,1)S(1)}, u32[]{:S(2)}, u32[]{:S(2)}) async-start(bf16[64,96,256]{2,1,0:T(8,128)(2,1)} %gather_fusion.2), calls=%async_computation.3 | async-start | bytes 6291456 | tf_op jit(solution)/shard_map/all_to_all | solution.py:179
  352.9 2.1 sort.31
  355.0 1.7 slice.74.init_ref
  356.7 4.5 shard_map.56.x_ref
  361.3 42.2 %shard_map.57 = f32[4,160,768]{2,1,0:T(8,128)S(1)} custom-call(f32[4,160,768]{2,1,0:T(8,128)S(1)} %shard_map.56.x_ref), custom_call_target="tpu_custom_call" | custom-call | tf_op jit(solution)/shard_map/pallas_call | solution.py:71
  403.5 0.0 copy-start.1
  403.5 1.3 copy-done.1
  404.8 2.4 slice.64.init_ref
  407.2 18.1 %all-to-all-done.3.arrived_ref = bf16[64,96,256]{2,1,0:T(8,128)(2,1)S(1)} async-done(((bf16[64,96,256]{2,1,0:T(8,128)(2,1)}), bf16[64,96,256]{2,1,0:T(8,128)(2,1)S(1)}, u32[]{:S(2)}, u32[]{:S(2)}) %all-to-all-start.3) | async-done | bytes 3145760 | tf_op jit(solution)/shard_map/all_to_all | solution.py:179
  425.3 0.0 copy-start.3
  425.3 1.3 copy-done.3
  426.5 2.9 shard_map.58.x_ref
  429.4 0.0 copy-start.2
  429.4 35.7 %shard_map.59 = f32[4,96,768]{2,1,0:T(8,128)S(1)} custom-call(f32[4,96,768]{2,1,0:T(8,128)S(1)} %shard_map.58.x_ref), custom_call_target="tpu_custom_call" | custom-call | tf_op jit(solution)/shard_map/pallas_call | solution.py:71
  465.2 0.0 copy-done.2
  465.2 2.0 pad_maximum_fusion.1
  (12 shorter events, 0.1 us)
Async XLA Ops:
  4.5 20.5 %all-to-all-start = ((s32[64,2,2]{1,2,0:T(2,128)}), s32[64,2,2]{1,2,0:T(2,128)S(1)}, u32[]{:S(2)}, u32[]{:S(2)}) async-start(s32[64,2,2]{1,2,0:T(2,128)} %copy.17), calls=%async_computation | async-start | bytes 131072 | tf_op jit(solution)/shard_map/all_to_all | solution.py:152
  25.1 196.7 %all-to-all-start.2 = ((bf16[64,256,256]{2,1,0:T(8,128)(2,1)}), bf16[64,256,256]{2,1,0:T(8,128)(2,1)}, u32[]{:S(2)}, u32[]{:S(2)}) async-start(bf16[64,256,256]{2,1,0:T(8,128)(2,1)} %gather_fusion.1), calls=%async_computation.2 | async-start | bytes 16777216 | tf_op jit(solution)/shard_map/all_to_all | solution.py:179
  221.8 123.8 %all-to-all-start.1 = ((bf16[64,160,256]{2,1,0:T(8,128)(2,1)}), bf16[64,160,256]{2,1,0:T(8,128)(2,1)}, u32[]{:S(2)}, u32[]{:S(2)}) async-start(bf16[64,160,256]{2,1,0:T(8,128)(2,1)} %gather_fusion), calls=%async_computation.1 | async-start | bytes 10485760 | tf_op jit(solution)/shard_map/all_to_all | solution.py:179
  228.2 5.9 %slice-start = ((bf16[48,256,256]{2,1,0:T(8,128)(2,1)}), bf16[48,96,256]{2,1,0:T(8,128)(2,1)S(1)}, s32[]{:S(2)}) async-start(bf16[48,256,256]{2,1,0:T(8,128)(2,1)} %param.7), calls=%async_computation.4 | async-start | bytes 4718592 | tf_op jit(solution)/shard_map/slice | solution.py:176
  228.2 38.1 %collective-permute-start = (bf16[1024,768]{1,0:T(8,128)(2,1)}, bf16[1024,768]{1,0:T(8,128)(2,1)}, u32[]{:S(2)}, u32[]{:S(2)}) collective-permute-start(bf16[1024,768]{1,0:T(8,128)(2,1)} %param.11), channel_id=1, source_target_pairs={{0,64},{64,128},{128,192},{192,0},{1,65},{65,129},{129,193},{193,1... | collective-permute-start | bytes 4718600 | tf_op jit(solution)/shard_map/ppermute | solution.py:156
  229.8 71.4 %collective-permute-start.1 = (bf16[1024,768]{1,0:T(8,128)(2,1)}, bf16[1024,768]{1,0:T(8,128)(2,1)}, u32[]{:S(2)}, u32[]{:S(2)}) collective-permute-start(bf16[1024,768]{1,0:T(8,128)(2,1)} %param.11), channel_id=1, source_target_pairs={{0,128},{64,192},{128,0},{192,64},{1,129},{65,193},{129,1},{193,65... | collective-permute-start | bytes 4718600 | tf_op jit(solution)/shard_map/ppermute | solution.py:156
  232.8 68.4 %collective-permute-start.2 = (bf16[1024,768]{1,0:T(8,128)(2,1)}, bf16[1024,768]{1,0:T(8,128)(2,1)}, u32[]{:S(2)}, u32[]{:S(2)}) collective-permute-start(bf16[1024,768]{1,0:T(8,128)(2,1)} %param.11), channel_id=1, source_target_pairs={{0,192},{64,0},{128,64},{192,128},{1,193},{65,1},{129,65},{193,129... | collective-permute-start | bytes 4718600 | tf_op jit(solution)/shard_map/ppermute | solution.py:156
  316.1 1.7 copy-start
  345.6 79.7 %all-to-all-start.3 = ((bf16[64,96,256]{2,1,0:T(8,128)(2,1)}), bf16[64,96,256]{2,1,0:T(8,128)(2,1)S(1)}, u32[]{:S(2)}, u32[]{:S(2)}) async-start(bf16[64,96,256]{2,1,0:T(8,128)(2,1)} %gather_fusion.2), calls=%async_computation.3 | async-start | bytes 6291456 | tf_op jit(solution)/shard_map/all_to_all | solution.py:179
  403.5 1.3 copy-start.1
  425.3 1.3 copy-start.3
  429.4 35.8 %copy-start.2 = (f32[4,160,768]{2,1,0:T(8,128)S(1)}, f32[4,160,768]{2,1,0:T(8,128)}, u32[]{:S(2)}) copy-start(f32[4,160,768]{2,1,0:T(8,128)} %copy-done.1) | copy-start | bytes 5898244

commit v10 on v9

--- a/solution.py
+++ b/solution.py
@@ -85,6 +85,58 @@
     )(x)
 
 
+def label_kernel(n, lab_ref, out_ref, send_sem, recv_sem):
+    me = lax.axis_index("wide")
+    row = lax.axis_index("grp")
+    barrier = pltpu.get_barrier_semaphore()
+
+    def greet(shift, carry):
+        peer = lax.rem(me + shift, n)
+        pl.semaphore_signal(barrier, inc=1, device_id=(row, peer), device_id_type=MESH)
+        return carry
+
+    lax.fori_loop(1, n, greet, 0)
+    pl.semaphore_wait(barrier, n - 1)
+    out_ref[me] = lab_ref[me]
+
+    def link(source, target, peer):
+        return pltpu.make_async_remote_copy(
+            src_ref=lab_ref.at[target],
+            dst_ref=out_ref.at[source],
+            send_sem=send_sem.at[target],
+            recv_sem=recv_sem.at[source],
+            device_id=(row, peer),
+            device_id_type=MESH,
+        )
+
+    def start(shift, carry):
+        peer = lax.rem(me + shift, n)
+        link(me, peer, peer).start()
+        return carry
+
+    lax.fori_loop(1, n, start, 0)
+
+    def finish(shift, carry):
+        peer = lax.rem(me + shift, n)
+        link(me, peer, peer).wait_send()
+        source = lax.rem(me + n - shift, n)
+        link(source, source, source).wait_recv()
+        return carry
+
+    lax.fori_loop(1, n, finish, 0)
+
+
+def swap_labels(lab, n):
+    return pl.pallas_call(
+        functools.partial(label_kernel, n),
+        out_shape=jax.ShapeDtypeStruct(lab.shape, lab.dtype),
+        in_specs=[pl.BlockSpec(memory_space=pltpu.VMEM)],
+        out_specs=pl.BlockSpec(memory_space=pltpu.VMEM),
+        scratch_shapes=[pltpu.SemaphoreType.DMA((n,)), pltpu.SemaphoreType.DMA((n,))],
+        compiler_params=pltpu.CompilerParams(collective_id=2, has_side_effects=True),
+    )(lab)
+
+
 def place_slots(row_ids, owner_map, out_dev):
     table_ids = jnp.arange(owner_map.shape[0], dtype=jnp.int32)
     position = jnp.sum(jnp.where(row_ids[..., None] == table_ids, owner_map, 0), axis=-1)
@@ -149,8 +201,11 @@
         [jnp.full((slot_total,), out_dev, jnp.int32), jnp.zeros((slot_total,), jnp.int32)], axis=1
     )
     label_out = vacant_label.at[slot_index].set(jnp.stack([local_row, contraction], axis=1))
-    arrived_labels = lax.all_to_all(label_out, "wide", split_axis=0, concat_axis=0, tiled=True)
-    arrived_labels = arrived_labels.reshape(wide_count, most_slots, 2)
+    packed = jnp.zeros((wide_count, 8, 128), jnp.int32).at[:, 0, :2 * most_slots].set(
+        label_out.reshape(wide_count, 2 * most_slots)
+    )
+    packed = swap_labels(packed, wide_count)
+    arrived_labels = packed[:, 0, :2 * most_slots].reshape(wide_count, most_slots, 2)
     grp_count = lax.axis_size("grp")
     pieces = [panel] + [
         lax.ppermute(panel, "grp", [(j, (j + shift) % grp_count) for j in range(grp_count)])
@@ -173,6 +228,8 @@
         ))
     first = jnp.take(tiles, picks[0], axis=0, mode="clip")
     upper_out = jnp.take(tiles[:, :band, :], picks[1], axis=0, mode="clip")
+    upper_out, packed = lax.optimization_barrier((upper_out, packed))
+    arrived_labels = packed[:, 0, :2 * most_slots].reshape(wide_count, most_slots, 2)
     lower_out = jnp.take(tiles[:, band:, :], picks[1], axis=0, mode="clip")
 
     def exchange(block):

time: 475 us -> 474 us (level); the launches traced: 467 us -> 471 us
  Pallas kernels: 91.6 us -> 301 us
  waiting for transfers between devices: 282 us -> 86.5 us
  starting transfers between devices: 41.1 us -> 32.7 us
    all_to_all x3, waiting for transfers between devices: 222 us -> 26.3 us  [exchange(): lax.all_to_all(block, 'wide', split_axis=0, concat_axis=0, tiled=True)]
    pallas_call x0 -> x1, Pallas kernels: none -> 187 us  [swap_labels(): pl.pallas_call(functools.partial(label_kernel, n), out_shape=jax.ShapeDty...]
    pallas_call x3, Pallas kernels: 13.7 us -> 36.9 us  [add_products(): pl.pallas_call(products_kernel, out_shape=jax.ShapeDtypeStruct(running.sh...]
    all_to_all x1 -> x0, starting transfers between devices: 11.5 us -> none  [per_device(): lax.all_to_all(label_out, 'wide', split_axis=0, concat_axis=0, tiled=True)]
  transfers between devices with their start and end apart: 7 -> 6, of which waited for: 5 -> 4; matrix products, arithmetic and copies ran while one was open for 9% -> 7% of each run, Pallas kernels for 11% -> 55%
where the time goes in v10:
time: 474 us; the launch traced here: 471 us
  Pallas kernels  301 us (64%)
  waiting for transfers between devices  86.5 us (18%)
  local copies, waits for them, and re-layouts  35.1 us (7%)
  starting transfers between devices  32.7 us (7%)
  other arithmetic  14.4 us (3%)
    pallas_call x1, Pallas kernels, swap_labels(): pl.pallas_call(functools.partial(label_kernel, n), out_shape=jax.ShapeDty...  187 us
    pallas_call x2, Pallas kernels, ring_sum(): pl.pallas_call(functools.partial(ring_sum_kernel, n), out_shape=jax.Shape...  77 us
    ppermute x3, waiting for transfers between devices, per_device(): lax.ppermute(panel, 'grp', [(j, (j + shift) % grp_count) for j in range(g...  60.2 us
    pallas_call x3, Pallas kernels, add_products(): pl.pallas_call(products_kernel, out_shape=jax.ShapeDtypeStruct(running.sh...  36.9 us
    all_to_all x3, starting transfers between devices, exchange(): lax.all_to_all(block, 'wide', split_axis=0, concat_axis=0, tiled=True)  26.8 us
    all_to_all x3, waiting for transfers between devices, exchange(): lax.all_to_all(block, 'wide', split_axis=0, concat_axis=0, tiled=True)  26.3 us
  transfers between devices with their start and end apart: 6, of which 4 were waited for; matrix products, arithmetic and copies ran while one was open for 7% of the time, Pallas kernels for 55%

profile of v10, /device:TPU:36, one launch (start us, length us, event | category | flops | bytes accessed | tf_op | source)
XLA Modules:
  0.0 471.3 jit_solution(13328297527431267457)
XLA Ops:
  0.0 0.9 select_reduce_fusion
  0.9 0.2 convert_reduce_fusion
  1.1 0.7 scatter_custom_fusion.2
  1.8 8.4 %gather_fusion.1 = bf16[64,256,256]{2,1,0:T(8,128)(2,1)} fusion(bf16[48,256,256]{2,1,0:T(8,128)(2,1)} %param.9, s32[1024]{0:T(1024)S(1)} %pad_clamp_fusion), kind=kCustom, calls=%fused_computation.1 | custom fusion | bytes 16777472 | tf_op jit(solution)/shard_map/jit(_take)/gather | solution.py:229
  10.2 11.7 %all-to-all-start.1 = ((bf16[64,256,256]{2,1,0:T(8,128)(2,1)}), bf16[64,256,256]{2,1,0:T(8,128)(2,1)}, u32[]{:S(2)}, u32[]{:S(2)}) async-start(bf16[64,256,256]{2,1,0:T(8,128)(2,1)} %gather_fusion.1), calls=%async_computation.1 | async-start | bytes 16777216 | tf_op jit(solution)/shard_map/all_to_all | solution.py:236
  21.9 0.0 copy-start.5
  22.0 0.0 copy-start.4
  22.0 4.3 slice.85
  26.3 0.0 copy-done.5
  26.3 0.1 copy.11
  26.4 0.0 copy-done.4
  26.4 0.8 scatter_fusion
  27.1 0.1 reshape.238
  27.2 0.7 scatter.32.lab_ref
  27.9 187.2 %shard_map.55 = s32[64,8,128]{2,1,0:T(8,128)} custom-call(s32[64,8,128]{2,1,0:T(8,128)} %scatter.32.lab_ref), custom_call_target="tpu_custom_call" | custom-call | tf_op jit(solution)/shard_map/pallas_call | solution.py:130
  215.1 0.7 scatter_custom_fusion.1
  215.9 5.3 %gather_fusion = bf16[64,160,256]{2,1,0:T(8,128)(2,1)} fusion(bf16[48,160,256]{2,1,0:T(8,128)(2,1)} %slice.85, s32[1024]{0:T(1024)S(1)} %pad_clamp_fusion.1), kind=kCustom, calls=%fused_computation | custom fusion | bytes 10486016 | tf_op jit(solution)/shard_map/jit(_take)/gather | solution.py:230
  221.2 0.0 all-to-all-done.1.arrived_ref
  221.2 8.8 %all-to-all-start = ((bf16[64,160,256]{2,1,0:T(8,128)(2,1)}), bf16[64,160,256]{2,1,0:T(8,128)(2,1)}, u32[]{:S(2)}, u32[]{:S(2)}) async-start(bf16[64,160,256]{2,1,0:T(8,128)(2,1)} %gather_fusion), calls=%async_computation | async-start | bytes 10485760 | tf_op jit(solution)/shard_map/all_to_all | solution.py:236
  230.1 0.0 slice-start
  230.1 1.6 collective-permute-start
  231.7 2.9 collective-permute-start.1
  234.7 1.3 collective-permute-start.2
  236.0 1.0 slice.80
  236.9 0.1 copy.13
  237.0 0.0 slice-done
  237.0 2.4 gather_fusion.2
  239.5 2.1 sort.32
  241.6 0.7 fusion.11
  242.9 25.3 %collective-permute-done = bf16[1024,768]{1,0:T(8,128)(2,1)} collective-permute-done((bf16[1024,768]{1,0:T(8,128)(2,1)}, bf16[1024,768]{1,0:T(8,128)(2,1)}, u32[]{:S(2)}, u32[]{:S(2)}) %collective-permute-start) | collective-permute-done | bytes 1572896 | tf_op jit(solution)/shard_map/ppermute | solution.py:211
  268.2 34.9 %collective-permute-done.1 = bf16[1024,768]{1,0:T(8,128)(2,1)} collective-permute-done((bf16[1024,768]{1,0:T(8,128)(2,1)}, bf16[1024,768]{1,0:T(8,128)(2,1)}, u32[]{:S(2)}, u32[]{:S(2)}) %collective-permute-start.1) | collective-permute-done | bytes 1572896 | tf_op jit(solution)/shard_map/ppermute | solution.py:211
  303.1 0.0 collective-permute-done.2
  303.1 6.4 %pad_maximum_fusion = bf16[4096,768]{1,0:T(8,128)(2,1)} fusion(bf16[1024,768]{1,0:T(8,128)(2,1)} %collective-permute-done.2, bf16[1024,768]{1,0:T(8,128)(2,1)} %collective-permute-done.1, bf16[1024,768]{1,0:T(8,128)(2,1)} %collective-permute-done, bf16[1024,768]{1,0:T(8,128)(2,1)} %param.13), kind=kLoop, calls=%fused_computation.6 | loop fusion | flops 25165824 | bytes 12582912 | tf_op jit(solution)/shard_map/concatenate | solution.py:214
  309.6 2.0 broadcast_in_dim.41.init_ref
  311.6 19.3 %shard_map.56 = f32[4,256,768]{2,1,0:T(8,128)S(1)} custom-call(s32[1]{0:T(128)} %bitcast.14.count_ref, s32[64]{0:T(128)S(1)} %get-tuple-element.36.order_ref, s32[64]{0:T(128)S(1)} %get-tuple-element.45.rows_ref, s32[64]{0:T(128)S(1)} %get-tuple-element.44.ks_ref, bf16[64,256,256]{2,1,0:T(8,128)(2,1)} %all-to-all-done.1.arrived_ref, ...), custom_call_target="tpu_custom_call" | custom-call | tf_op jit(solution)/shard_map/pallas_call | solution.py:182
  330.9 0.0 copy-start
  330.9 1.7 copy-done
  332.7 15.3 %all-to-all-done.arrived_ref = bf16[64,160,256]{2,1,0:T(8,128)(2,1)} async-done(((bf16[64,160,256]{2,1,0:T(8,128)(2,1)}), bf16[64,160,256]{2,1,0:T(8,128)(2,1)}, u32[]{:S(2)}, u32[]{:S(2)}) %all-to-all-start) | async-done | bytes 5242912 | tf_op jit(solution)/shard_map/all_to_all | solution.py:236
  348.0 6.3 %all-to-all-start.2 = ((bf16[64,96,256]{2,1,0:T(8,128)(2,1)}), bf16[64,96,256]{2,1,0:T(8,128)(2,1)S(1)}, u32[]{:S(2)}, u32[]{:S(2)}) async-start(bf16[64,96,256]{2,1,0:T(8,128)(2,1)} %gather_fusion.2), calls=%async_computation.2 | async-start | bytes 6291456 | tf_op jit(solution)/shard_map/all_to_all | solution.py:236
  354.9 2.1 sort.31
  357.0 1.7 slice.101.init_ref
  358.7 9.9 %shard_map.57.x_ref = f32[4,160,768]{2,1,0:T(8,128)S(1)} custom-call(s32[1]{0:T(128)} %bitcast.8.count_ref, s32[64]{0:T(128)S(1)} %get-tuple-element.34.order_ref, s32[64]{0:T(128)S(1)} %get-tuple-element.47.rows_ref, s32[64]{0:T(128)S(1)} %get-tuple-element.46.ks_ref, bf16[64,160,256]{2,1,0:T(8,128)(2,1)} %all-to-all-done.arrived_ref, ...), custom_call_target="tpu_custom_call" | custom-call | tf_op jit(solution)/shard_map/pallas_call | solution.py:182
  368.6 43.8 %shard_map.58 = f32[4,160,768]{2,1,0:T(8,128)S(1)} custom-call(f32[4,160,768]{2,1,0:T(8,128)S(1)} %shard_map.57.x_ref), custom_call_target="tpu_custom_call" | custom-call | tf_op jit(solution)/shard_map/pallas_call | solution.py:71
  412.5 0.0 copy-start.1
  412.5 1.3 copy-done.1
  413.8 2.4 slice.91.init_ref
  416.2 11.0 %all-to-all-done.2.arrived_ref = bf16[64,96,256]{2,1,0:T(8,128)(2,1)S(1)} async-done(((bf16[64,96,256]{2,1,0:T(8,128)(2,1)}), bf16[64,96,256]{2,1,0:T(8,128)(2,1)S(1)}, u32[]{:S(2)}, u32[]{:S(2)}) %all-to-all-start.2) | async-done | bytes 3145760 | tf_op jit(solution)/shard_map/all_to_all | solution.py:236
  427.2 0.0 copy-start.3
  427.2 1.3 copy-done.3
  428.4 7.7 %shard_map.59.x_ref = f32[4,96,768]{2,1,0:T(8,128)S(1)} custom-call(s32[1]{0:T(128)} %bitcast.8.count_ref, s32[64]{0:T(128)S(1)} %get-tuple-element.34.order_ref, s32[64]{0:T(128)S(1)} %get-tuple-element.47.rows_ref, s32[64]{0:T(128)S(1)} %get-tuple-element.46.ks_ref, bf16[64,96,256]{2,1,0:T(8,128)(2,1)S(1)} %all-to-all-done.2.arrived_ref, ...), custom_call_target="tpu_custom_call" | custom-call | tf_op jit(solution)/shard_map/pallas_call | solution.py:182
  436.2 0.0 copy-start.2
  436.2 33.1 %shard_map.60 = f32[4,96,768]{2,1,0:T(8,128)S(1)} custom-call(f32[4,96,768]{2,1,0:T(8,128)S(1)} %shard_map.59.x_ref), custom_call_target="tpu_custom_call" | custom-call | tf_op jit(solution)/shard_map/pallas_call | solution.py:71
  469.3 0.0 copy-done.2
  469.3 2.0 pad_maximum_fusion.1
  (15 shorter events, 0.1 us)
Async XLA Ops:
  10.2 211.0 %all-to-all-start.1 = ((bf16[64,256,256]{2,1,0:T(8,128)(2,1)}), bf16[64,256,256]{2,1,0:T(8,128)(2,1)}, u32[]{:S(2)}, u32[]{:S(2)}) async-start(bf16[64,256,256]{2,1,0:T(8,128)(2,1)} %gather_fusion.1), calls=%async_computation.1 | async-start | bytes 16777216 | tf_op jit(solution)/shard_map/all_to_all | solution.py:236
  21.9 4.3 copy-start.5
  22.0 4.4 copy-start.4
  221.2 126.7 %all-to-all-start = ((bf16[64,160,256]{2,1,0:T(8,128)(2,1)}), bf16[64,160,256]{2,1,0:T(8,128)(2,1)}, u32[]{:S(2)}, u32[]{:S(2)}) async-start(bf16[64,160,256]{2,1,0:T(8,128)(2,1)} %gather_fusion), calls=%async_computation | async-start | bytes 10485760 | tf_op jit(solution)/shard_map/all_to_all | solution.py:236
  230.1 6.9 %slice-start = ((bf16[48,256,256]{2,1,0:T(8,128)(2,1)}), bf16[48,96,256]{2,1,0:T(8,128)(2,1)S(1)}, s32[]{:S(2)}) async-start(bf16[48,256,256]{2,1,0:T(8,128)(2,1)} %param.9), calls=%async_computation.3 | async-start | bytes 4718592 | tf_op jit(solution)/shard_map/slice | solution.py:233
  230.1 38.1 %collective-permute-start = (bf16[1024,768]{1,0:T(8,128)(2,1)}, bf16[1024,768]{1,0:T(8,128)(2,1)}, u32[]{:S(2)}, u32[]{:S(2)}) collective-permute-start(bf16[1024,768]{1,0:T(8,128)(2,1)} %param.13), channel_id=1, source_target_pairs={{0,64},{64,128},{128,192},{192,0},{1,65},{65,129},{129,193},{193,1... | collective-permute-start | bytes 4718600 | tf_op jit(solution)/shard_map/ppermute | solution.py:211
  231.7 71.4 %collective-permute-start.1 = (bf16[1024,768]{1,0:T(8,128)(2,1)}, bf16[1024,768]{1,0:T(8,128)(2,1)}, u32[]{:S(2)}, u32[]{:S(2)}) collective-permute-start(bf16[1024,768]{1,0:T(8,128)(2,1)} %param.13), channel_id=1, source_target_pairs={{0,128},{64,192},{128,0},{192,64},{1,129},{65,193},{129,1},{193,65... | collective-permute-start | bytes 4718600 | tf_op jit(solution)/shard_map/ppermute | solution.py:211
  234.7 68.4 %collective-permute-start.2 = (bf16[1024,768]{1,0:T(8,128)(2,1)}, bf16[1024,768]{1,0:T(8,128)(2,1)}, u32[]{:S(2)}, u32[]{:S(2)}) collective-permute-start(bf16[1024,768]{1,0:T(8,128)(2,1)} %param.13), channel_id=1, source_target_pairs={{0,192},{64,0},{128,64},{192,128},{1,193},{65,1},{129,65},{193,129... | collective-permute-start | bytes 4718600 | tf_op jit(solution)/shard_map/ppermute | solution.py:211
  330.9 1.8 copy-start
  348.0 79.2 %all-to-all-start.2 = ((bf16[64,96,256]{2,1,0:T(8,128)(2,1)}), bf16[64,96,256]{2,1,0:T(8,128)(2,1)S(1)}, u32[]{:S(2)}, u32[]{:S(2)}) async-start(bf16[64,96,256]{2,1,0:T(8,128)(2,1)} %gather_fusion.2), calls=%async_computation.2 | async-start | bytes 6291456 | tf_op jit(solution)/shard_map/all_to_all | solution.py:236
  412.5 1.3 copy-start.1
  427.2 1.3 copy-start.3
  436.2 33.1 %copy-start.2 = (f32[4,160,768]{2,1,0:T(8,128)S(1)}, f32[4,160,768]{2,1,0:T(8,128)}, u32[]{:S(2)}) copy-start(f32[4,160,768]{2,1,0:T(8,128)} %copy-done.1) | copy-start | bytes 5898244

commit v11 on v10

--- a/solution.py
+++ b/solution.py
@@ -204,8 +204,6 @@
     packed = jnp.zeros((wide_count, 8, 128), jnp.int32).at[:, 0, :2 * most_slots].set(
         label_out.reshape(wide_count, 2 * most_slots)
     )
-    packed = swap_labels(packed, wide_count)
-    arrived_labels = packed[:, 0, :2 * most_slots].reshape(wide_count, most_slots, 2)
     grp_count = lax.axis_size("grp")
     pieces = [panel] + [
         lax.ppermute(panel, "grp", [(j, (j + shift) % grp_count) for j in range(grp_count)])
@@ -213,13 +211,7 @@
     ]
     gathered = jnp.concatenate(pieces, axis=0)
     panel_tiles = gathered.reshape(gathered.shape[0] // tile_side, tile_side, gathered.shape[1])
-    held = panel.shape[0] // tile_side
-    owner = arrived_labels[..., 1] // held
-    shift = lax.rem(lax.axis_index("grp") - owner + grp_count, grp_count)
-    arrived_labels = arrived_labels.at[..., 1].set(shift * held + arrived_labels[..., 1] % held)
     band = tile_side * 5 // 8
-    arrived_labels = arrived_labels.reshape(wide_count, most_slots, 2)
-    schedules = [slot_order(arrived_labels[:, rank, :], out_dev) for rank in range(most_slots)]
     picks = []
     for rank in range(most_slots):
         chunk_index = jnp.where(ranking == rank, target, wide_count)
@@ -229,8 +221,16 @@
     first = jnp.take(tiles, picks[0], axis=0, mode="clip")
     upper_out = jnp.take(tiles[:, :band, :], picks[1], axis=0, mode="clip")
     upper_out, packed = lax.optimization_barrier((upper_out, packed))
+    packed = swap_labels(packed, wide_count)
+    upper_out, packed = lax.optimization_barrier((upper_out, packed))
     arrived_labels = packed[:, 0, :2 * most_slots].reshape(wide_count, most_slots, 2)
+    held = panel.shape[0] // tile_side
+    owner = arrived_labels[..., 1] // held
+    shift = lax.rem(lax.axis_index("grp") - owner + grp_count, grp_count)
+    arrived_labels = arrived_labels.at[..., 1].set(shift * held + arrived_labels[..., 1] % held)
     lower_out = jnp.take(tiles[:, band:, :], picks[1], axis=0, mode="clip")
+
+    schedules = [slot_order(arrived_labels[:, rank, :], out_dev) for rank in range(most_slots)]
 
     def exchange(block):
         return lax.all_to_all(block, "wide", split_axis=0, concat_axis=0, tiled=True)

time: 474 us -> 472 us (level)
  waiting for transfers between devices: 86.5 us -> 78 us
  Pallas kernels: 301 us -> 309 us
    pallas_call x3, Pallas kernels: 36.9 us -> 51.2 us  [add_products(): pl.pallas_call(products_kernel, out_shape=jax.ShapeDtypeStruct(running.sh...]
    all_to_all x3, waiting for transfers between devices: 26.3 us -> 17.7 us  [exchange(): lax.all_to_all(block, 'wide', split_axis=0, concat_axis=0, tiled=True)]
    pallas_call x1, Pallas kernels: 187 us -> 181 us  [swap_labels(): pl.pallas_call(functools.partial(label_kernel, n), out_shape=jax.ShapeDty...]
  transfers between devices with their start and end apart: 6 -> 6, of which waited for: 4 -> 4; matrix products, arithmetic and copies ran while one was open for 7% -> 7% of each run, Pallas kernels for 55% -> 56%
where the time goes in v11:
time: 472 us; the launch traced here: 471 us
  Pallas kernels  309 us (65%)
  waiting for transfers between devices  78 us (17%)
  local copies, waits for them, and re-layouts  34.9 us (7%)
  starting transfers between devices  32.7 us (7%)
  other arithmetic  14.3 us (3%)
    pallas_call x1, Pallas kernels, swap_labels(): pl.pallas_call(functools.partial(label_kernel, n), out_shape=jax.ShapeDty...  181 us
    pallas_call x2, Pallas kernels, ring_sum(): pl.pallas_call(functools.partial(ring_sum_kernel, n), out_shape=jax.Shape...  76.8 us
    ppermute x3, waiting for transfers between devices, per_device(): lax.ppermute(panel, 'grp', [(j, (j + shift) % grp_count) for j in range(g...  60.3 us
    pallas_call x3, Pallas kernels, add_products(): pl.pallas_call(products_kernel, out_shape=jax.ShapeDtypeStruct(running.sh...  51.2 us
    all_to_all x3, starting transfers between devices, exchange(): lax.all_to_all(block, 'wide', split_axis=0, concat_axis=0, tiled=True)  26.8 us
    all_to_all x3, waiting for transfers between devices, exchange(): lax.all_to_all(block, 'wide', split_axis=0, concat_axis=0, tiled=True)  17.7 us
  transfers between devices with their start and end apart: 6, of which 4 were waited for; matrix products, arithmetic and copies ran while one was open for 7% of the time, Pallas kernels for 56%

profile of v11, /device:TPU:36, one launch (start us, length us, event | category | flops | bytes accessed | tf_op | source)
XLA Modules:
  0.0 470.5 jit_solution(17176256600123407673)
XLA Ops:
  0.0 0.9 select_reduce_fusion
  0.9 0.2 convert_reduce_fusion
  1.1 0.7 scatter_custom_fusion.2
  1.8 8.3 %gather_fusion.1 = bf16[64,256,256]{2,1,0:T(8,128)(2,1)} fusion(bf16[48,256,256]{2,1,0:T(8,128)(2,1)} %param.9, s32[1024]{0:T(1024)S(1)} %pad_clamp_fusion), kind=kCustom, calls=%fused_computation.1 | custom fusion | bytes 16777472 | tf_op jit(solution)/shard_map/jit(_take)/gather | solution.py:221
  10.1 11.7 %all-to-all-start.1 = ((bf16[64,256,256]{2,1,0:T(8,128)(2,1)}), bf16[64,256,256]{2,1,0:T(8,128)(2,1)}, u32[]{:S(2)}, u32[]{:S(2)}) async-start(bf16[64,256,256]{2,1,0:T(8,128)(2,1)} %gather_fusion.1), calls=%async_computation.1 | async-start | bytes 16777216 | tf_op jit(solution)/shard_map/all_to_all | solution.py:236
  21.8 0.0 copy-start.5
  21.8 0.0 copy-start.4
  21.9 4.3 slice.80
  26.2 0.0 copy-done.5
  26.2 0.1 copy.11
  26.3 0.0 copy-done.4
  26.3 0.8 scatter_fusion
  27.0 0.1 reshape.238
  27.1 0.7 scatter.33.lab_ref
  27.9 0.7 scatter_custom_fusion
  28.6 5.3 %gather_fusion = bf16[64,160,256]{2,1,0:T(8,128)(2,1)} fusion(bf16[48,160,256]{2,1,0:T(8,128)(2,1)} %slice.80, s32[1024]{0:T(1024)S(1)} %pad_clamp_fusion.1), kind=kCustom, calls=%fused_computation | custom fusion | bytes 10486016 | tf_op jit(solution)/shard_map/jit(_take)/gather | solution.py:222
  33.9 181.1 %shard_map.55 = s32[64,8,128]{2,1,0:T(8,128)} custom-call(s32[64,8,128]{2,1,0:T(8,128)} %scatter.33.lab_ref), custom_call_target="tpu_custom_call" | custom-call | tf_op jit(solution)/shard_map/pallas_call | solution.py:130
  215.0 0.0 all-to-all-done.1.arrived_ref
  215.0 8.8 %all-to-all-start = ((bf16[64,160,256]{2,1,0:T(8,128)(2,1)}), bf16[64,160,256]{2,1,0:T(8,128)(2,1)}, u32[]{:S(2)}, u32[]{:S(2)}) async-start(bf16[64,160,256]{2,1,0:T(8,128)(2,1)} %gather_fusion), calls=%async_computation | async-start | bytes 10485760 | tf_op jit(solution)/shard_map/all_to_all | solution.py:236
  223.9 0.0 slice-start
  223.9 1.7 collective-permute-start
  225.6 2.9 collective-permute-start.1
  228.4 1.4 collective-permute-start.2
  229.8 1.0 slice.81
  230.8 0.1 copy.13
  230.9 0.0 slice-done
  230.9 2.4 gather_fusion.2
  233.4 2.0 sort.32
  235.4 0.6 fusion.11
  236.6 25.4 %collective-permute-done = bf16[1024,768]{1,0:T(8,128)(2,1)} collective-permute-done((bf16[1024,768]{1,0:T(8,128)(2,1)}, bf16[1024,768]{1,0:T(8,128)(2,1)}, u32[]{:S(2)}, u32[]{:S(2)}) %collective-permute-start) | collective-permute-done | bytes 1572896 | tf_op jit(solution)/shard_map/ppermute | solution.py:209
  262.0 34.9 %collective-permute-done.1 = bf16[1024,768]{1,0:T(8,128)(2,1)} collective-permute-done((bf16[1024,768]{1,0:T(8,128)(2,1)}, bf16[1024,768]{1,0:T(8,128)(2,1)}, u32[]{:S(2)}, u32[]{:S(2)}) %collective-permute-start.1) | collective-permute-done | bytes 1572896 | tf_op jit(solution)/shard_map/ppermute | solution.py:209
  296.9 0.0 collective-permute-done.2
  296.9 6.6 %pad_maximum_fusion = bf16[4096,768]{1,0:T(8,128)(2,1)} fusion(bf16[1024,768]{1,0:T(8,128)(2,1)} %collective-permute-done.2, bf16[1024,768]{1,0:T(8,128)(2,1)} %collective-permute-done.1, bf16[1024,768]{1,0:T(8,128)(2,1)} %collective-permute-done, bf16[1024,768]{1,0:T(8,128)(2,1)} %param.13), kind=kLoop, calls=%fused_computation.6 | loop fusion | flops 25165824 | bytes 12582912 | tf_op jit(solution)/shard_map/concatenate | solution.py:212
  303.4 2.0 broadcast_in_dim.41.init_ref
  305.5 23.4 %shard_map.56 = f32[4,256,768]{2,1,0:T(8,128)S(1)} custom-call(s32[1]{0:T(128)} %bitcast.14.count_ref, s32[64]{0:T(128)S(1)} %get-tuple-element.42.order_ref, s32[64]{0:T(128)S(1)} %get-tuple-element.51.rows_ref, s32[64]{0:T(128)S(1)} %get-tuple-element.50.ks_ref, bf16[64,256,256]{2,1,0:T(8,128)(2,1)} %all-to-all-done.1.arrived_ref, ...), custom_call_target="tpu_custom_call" | custom-call | tf_op jit(solution)/shard_map/pallas_call | solution.py:182
  328.9 0.0 copy-start
  328.9 1.7 copy-done
  330.5 11.3 %all-to-all-done.arrived_ref = bf16[64,160,256]{2,1,0:T(8,128)(2,1)} async-done(((bf16[64,160,256]{2,1,0:T(8,128)(2,1)}), bf16[64,160,256]{2,1,0:T(8,128)(2,1)}, u32[]{:S(2)}, u32[]{:S(2)}) %all-to-all-start) | async-done | bytes 5242912 | tf_op jit(solution)/shard_map/all_to_all | solution.py:236
  341.8 6.3 %all-to-all-start.2 = ((bf16[64,96,256]{2,1,0:T(8,128)(2,1)}), bf16[64,96,256]{2,1,0:T(8,128)(2,1)S(1)}, u32[]{:S(2)}, u32[]{:S(2)}) async-start(bf16[64,96,256]{2,1,0:T(8,128)(2,1)} %gather_fusion.2), calls=%async_computation.2 | async-start | bytes 6291456 | tf_op jit(solution)/shard_map/all_to_all | solution.py:236
  348.6 2.1 sort.31
  350.7 1.7 slice.101.init_ref
  352.5 15.3 %shard_map.57.x_ref = f32[4,160,768]{2,1,0:T(8,128)S(1)} custom-call(s32[1]{0:T(128)} %bitcast.9.count_ref, s32[64]{0:T(128)S(1)} %get-tuple-element.40.order_ref, s32[64]{0:T(128)S(1)} %get-tuple-element.53.rows_ref, s32[64]{0:T(128)S(1)} %get-tuple-element.52.ks_ref, bf16[64,160,256]{2,1,0:T(8,128)(2,1)} %all-to-all-done.arrived_ref, ...), custom_call_target="tpu_custom_call" | custom-call | tf_op jit(solution)/shard_map/pallas_call | solution.py:182
  367.7 43.1 %shard_map.58 = f32[4,160,768]{2,1,0:T(8,128)S(1)} custom-call(f32[4,160,768]{2,1,0:T(8,128)S(1)} %shard_map.57.x_ref), custom_call_target="tpu_custom_call" | custom-call | tf_op jit(solution)/shard_map/pallas_call | solution.py:71
  410.8 0.0 copy-start.1
  410.8 1.3 copy-done.1
  412.1 2.4 slice.91.init_ref
  414.5 6.5 %all-to-all-done.2.arrived_ref = bf16[64,96,256]{2,1,0:T(8,128)(2,1)S(1)} async-done(((bf16[64,96,256]{2,1,0:T(8,128)(2,1)}), bf16[64,96,256]{2,1,0:T(8,128)(2,1)S(1)}, u32[]{:S(2)}, u32[]{:S(2)}) %all-to-all-start.2) | async-done | bytes 3145760 | tf_op jit(solution)/shard_map/all_to_all | solution.py:236
  421.0 0.0 copy-start.3
  421.0 1.3 copy-done.3
  422.2 12.6 %shard_map.59.x_ref = f32[4,96,768]{2,1,0:T(8,128)S(1)} custom-call(s32[1]{0:T(128)} %bitcast.9.count_ref, s32[64]{0:T(128)S(1)} %get-tuple-element.40.order_ref, s32[64]{0:T(128)S(1)} %get-tuple-element.53.rows_ref, s32[64]{0:T(128)S(1)} %get-tuple-element.52.ks_ref, bf16[64,96,256]{2,1,0:T(8,128)(2,1)S(1)} %all-to-all-done.2.arrived_ref, ...), custom_call_target="tpu_custom_call" | custom-call | tf_op jit(solution)/shard_map/pallas_call | solution.py:182
  434.8 0.0 copy-start.2
  434.8 33.7 %shard_map.60 = f32[4,96,768]{2,1,0:T(8,128)S(1)} custom-call(f32[4,96,768]{2,1,0:T(8,128)S(1)} %shard_map.59.x_ref), custom_call_target="tpu_custom_call" | custom-call | tf_op jit(solution)/shard_map/pallas_call | solution.py:71
  468.6 0.0 copy-done.2
  468.6 2.0 pad_maximum_fusion.1
  (15 shorter events, 0.1 us)
Async XLA Ops:
  10.1 204.9 %all-to-all-start.1 = ((bf16[64,256,256]{2,1,0:T(8,128)(2,1)}), bf16[64,256,256]{2,1,0:T(8,128)(2,1)}, u32[]{:S(2)}, u32[]{:S(2)}) async-start(bf16[64,256,256]{2,1,0:T(8,128)(2,1)} %gather_fusion.1), calls=%async_computation.1 | async-start | bytes 16777216 | tf_op jit(solution)/shard_map/all_to_all | solution.py:236
  21.8 4.3 copy-start.5
  21.8 4.4 copy-start.4
  215.0 126.8 %all-to-all-start = ((bf16[64,160,256]{2,1,0:T(8,128)(2,1)}), bf16[64,160,256]{2,1,0:T(8,128)(2,1)}, u32[]{:S(2)}, u32[]{:S(2)}) async-start(bf16[64,160,256]{2,1,0:T(8,128)(2,1)} %gather_fusion), calls=%async_computation | async-start | bytes 10485760 | tf_op jit(solution)/shard_map/all_to_all | solution.py:236
  223.9 7.0 %slice-start = ((bf16[48,256,256]{2,1,0:T(8,128)(2,1)}), bf16[48,96,256]{2,1,0:T(8,128)(2,1)S(1)}, s32[]{:S(2)}) async-start(bf16[48,256,256]{2,1,0:T(8,128)(2,1)} %param.9), calls=%async_computation.3 | async-start | bytes 4718592 | tf_op jit(solution)/shard_map/slice | solution.py:231
  223.9 38.1 %collective-permute-start = (bf16[1024,768]{1,0:T(8,128)(2,1)}, bf16[1024,768]{1,0:T(8,128)(2,1)}, u32[]{:S(2)}, u32[]{:S(2)}) collective-permute-start(bf16[1024,768]{1,0:T(8,128)(2,1)} %param.13), channel_id=1, source_target_pairs={{0,64},{64,128},{128,192},{192,0},{1,65},{65,129},{129,193},{193,1... | collective-permute-start | bytes 4718600 | tf_op jit(solution)/shard_map/ppermute | solution.py:209
  225.6 71.3 %collective-permute-start.1 = (bf16[1024,768]{1,0:T(8,128)(2,1)}, bf16[1024,768]{1,0:T(8,128)(2,1)}, u32[]{:S(2)}, u32[]{:S(2)}) collective-permute-start(bf16[1024,768]{1,0:T(8,128)(2,1)} %param.13), channel_id=1, source_target_pairs={{0,128},{64,192},{128,0},{192,64},{1,129},{65,193},{129,1},{193,65... | collective-permute-start | bytes 4718600 | tf_op jit(solution)/shard_map/ppermute | solution.py:209
  228.4 68.4 %collective-permute-start.2 = (bf16[1024,768]{1,0:T(8,128)(2,1)}, bf16[1024,768]{1,0:T(8,128)(2,1)}, u32[]{:S(2)}, u32[]{:S(2)}) collective-permute-start(bf16[1024,768]{1,0:T(8,128)(2,1)} %param.13), channel_id=1, source_target_pairs={{0,192},{64,0},{128,64},{192,128},{1,193},{65,1},{129,65},{193,129... | collective-permute-start | bytes 4718600 | tf_op jit(solution)/shard_map/ppermute | solution.py:209
  328.9 1.7 copy-start
  341.8 79.2 %all-to-all-start.2 = ((bf16[64,96,256]{2,1,0:T(8,128)(2,1)}), bf16[64,96,256]{2,1,0:T(8,128)(2,1)S(1)}, u32[]{:S(2)}, u32[]{:S(2)}) async-start(bf16[64,96,256]{2,1,0:T(8,128)(2,1)} %gather_fusion.2), calls=%async_computation.2 | async-start | bytes 6291456 | tf_op jit(solution)/shard_map/all_to_all | solution.py:236
  410.8 1.3 copy-start.1
  421.0 1.3 copy-start.3
  434.8 33.8 %copy-start.2 = (f32[4,160,768]{2,1,0:T(8,128)S(1)}, f32[4,160,768]{2,1,0:T(8,128)}, u32[]{:S(2)}) copy-start(f32[4,160,768]{2,1,0:T(8,128)} %copy-done.1) | copy-start | bytes 5898244

commit v12 on v11

--- a/solution.py
+++ b/solution.py
@@ -36,6 +36,7 @@
         copy.start()
         return copy
 
+    sent = []
     for step in range(n - 1):
         copies = []
         for way in range(2):
@@ -49,7 +50,8 @@
                 src = sbuf.at[way, step]
             copies.append(send(way, step, src, rbuf.at[way, step]))
         for copy in copies:
-            copy.wait()
+            copy.wait_recv()
+        sent.extend(copies)
 
     for way in range(2):
         rows = pl.ds(way * half, half)
@@ -63,7 +65,10 @@
             chunk = lax.rem(me - sign * step + 2 * n, n)
             copies.append(send(way, n - 1 + step, out_ref.at[chunk, rows], out_ref.at[chunk, rows]))
         for copy in copies:
-            copy.wait()
+            copy.wait_recv()
+        sent.extend(copies)
+    for copy in sent:
+        copy.wait_send()
 
 
 def ring_sum(x, n, ident):
@@ -211,7 +216,7 @@
     ]
     gathered = jnp.concatenate(pieces, axis=0)
     panel_tiles = gathered.reshape(gathered.shape[0] // tile_side, tile_side, gathered.shape[1])
-    band = tile_side * 5 // 8
+    band = tile_side * 11 // 16
     picks = []
     for rank in range(most_slots):
         chunk_index = jnp.where(ranking == rank, target, wide_count)

time: 472 us -> 475 us (level)
  waiting for transfers between devices: 78 us -> 84.7 us
    all_to_all x3, waiting for transfers between devices: 17.7 us -> 24.4 us  [exchange(): lax.all_to_all(block, 'wide', split_axis=0, concat_axis=0, tiled=True)]
  transfers between devices with their start and end apart: 6 -> 6, of which waited for: 4 -> 3; matrix products, arithmetic and copies ran while one was open for 7% -> 6% of each run, Pallas kernels for 56% -> 56%
where the time goes in v12:
time: 475 us; the launch traced here: 474 us
  Pallas kernels  310 us (65%)
  waiting for transfers between devices  84.7 us (18%)
  starting transfers between devices  32.9 us (7%)
  local copies, waits for them, and re-layouts  30.8 us (6%)
  other arithmetic  14.4 us (3%)
    pallas_call x1, Pallas kernels, swap_labels(): pl.pallas_call(functools.partial(label_kernel, n), out_shape=jax.ShapeDty...  180 us
    pallas_call x2, Pallas kernels, ring_sum(): pl.pallas_call(functools.partial(ring_sum_kernel, n), out_shape=jax.Shape...  79.2 us
    ppermute x3, waiting for transfers between devices, per_device(): lax.ppermute(panel, 'grp', [(j, (j + shift) % grp_count) for j in range(g...  60.3 us
    pallas_call x3, Pallas kernels, add_products(): pl.pallas_call(products_kernel, out_shape=jax.ShapeDtypeStruct(running.sh...  50.2 us
    all_to_all x3, starting transfers between devices, exchange(): lax.all_to_all(block, 'wide', split_axis=0, concat_axis=0, tiled=True)  27 us
    all_to_all x3, waiting for transfers between devices, exchange(): lax.all_to_all(block, 'wide', split_axis=0, concat_axis=0, tiled=True)  24.4 us
  transfers between devices with their start and end apart: 6, of which 3 were waited for; matrix products, arithmetic and copies ran while one was open for 6% of the time, Pallas kernels for 56%

profile of v12, /device:TPU:36, one launch (start us, length us, event | category | flops | bytes accessed | tf_op | source)
XLA Modules:
  0.0 474.3 jit_solution(15364342395347138808)
XLA Ops:
  0.0 0.9 select_reduce_fusion
  0.9 0.2 convert_reduce_fusion
  1.1 0.7 scatter_custom_fusion.2
  1.8 8.2 %gather_fusion.1 = bf16[64,256,256]{2,1,0:T(8,128)(2,1)} fusion(bf16[48,256,256]{2,1,0:T(8,128)(2,1)} %param.9, s32[1024]{0:T(1024)S(1)} %pad_clamp_fusion), kind=kCustom, calls=%fused_computation.1 | custom fusion | bytes 16777472 | tf_op jit(solution)/shard_map/jit(_take)/gather | solution.py:226
  10.1 11.7 %all-to-all-start.1 = ((bf16[64,256,256]{2,1,0:T(8,128)(2,1)}), bf16[64,256,256]{2,1,0:T(8,128)(2,1)}, u32[]{:S(2)}, u32[]{:S(2)}) async-start(bf16[64,256,256]{2,1,0:T(8,128)(2,1)} %gather_fusion.1), calls=%async_computation.1 | async-start | bytes 16777216 | tf_op jit(solution)/shard_map/all_to_all | solution.py:241
  21.8 0.0 copy-start.4
  21.8 0.0 copy-start.3
  21.8 4.7 slice.80
  26.5 0.0 copy-done.4
  26.5 0.1 copy.11
  26.6 0.0 copy-done.3
  26.6 0.8 scatter_fusion
  27.3 0.1 reshape.238
  27.4 0.7 scatter.33.lab_ref
  28.1 0.7 scatter_custom_fusion
  28.9 5.6 %gather_fusion = bf16[64,176,256]{2,1,0:T(8,128)(2,1)} fusion(bf16[48,176,256]{2,1,0:T(8,128)(2,1)} %slice.80, s32[1024]{0:T(1024)S(1)} %pad_clamp_fusion.1), kind=kCustom, calls=%fused_computation | custom fusion | bytes 11534592 | tf_op jit(solution)/shard_map/jit(_take)/gather | solution.py:227
  34.5 180.4 %shard_map.55 = s32[64,8,128]{2,1,0:T(8,128)} custom-call(s32[64,8,128]{2,1,0:T(8,128)} %scatter.33.lab_ref), custom_call_target="tpu_custom_call" | custom-call | tf_op jit(solution)/shard_map/pallas_call | solution.py:135
  215.0 0.0 all-to-all-done.1.arrived_ref
  215.0 8.9 %all-to-all-start = ((bf16[64,176,256]{2,1,0:T(8,128)(2,1)}), bf16[64,176,256]{2,1,0:T(8,128)(2,1)}, u32[]{:S(2)}, u32[]{:S(2)}) async-start(bf16[64,176,256]{2,1,0:T(8,128)(2,1)} %gather_fusion), calls=%async_computation | async-start | bytes 11534336 | tf_op jit(solution)/shard_map/all_to_all | solution.py:241
  223.8 0.0 slice-start
  223.9 1.7 collective-permute-start
  225.5 2.9 collective-permute-start.1
  228.4 1.4 collective-permute-start.2
  229.8 1.0 slice.81
  230.8 0.1 copy.13
  230.9 0.0 slice-done
  230.9 2.2 gather_fusion.2
  233.1 2.0 sort.32
  235.2 0.7 fusion.11
  236.5 25.5 %collective-permute-done = bf16[1024,768]{1,0:T(8,128)(2,1)} collective-permute-done((bf16[1024,768]{1,0:T(8,128)(2,1)}, bf16[1024,768]{1,0:T(8,128)(2,1)}, u32[]{:S(2)}, u32[]{:S(2)}) %collective-permute-start) | collective-permute-done | bytes 1572896 | tf_op jit(solution)/shard_map/ppermute | solution.py:214
  262.0 34.9 %collective-permute-done.1 = bf16[1024,768]{1,0:T(8,128)(2,1)} collective-permute-done((bf16[1024,768]{1,0:T(8,128)(2,1)}, bf16[1024,768]{1,0:T(8,128)(2,1)}, u32[]{:S(2)}, u32[]{:S(2)}) %collective-permute-start.1) | collective-permute-done | bytes 1572896 | tf_op jit(solution)/shard_map/ppermute | solution.py:214
  296.9 0.0 collective-permute-done.2
  296.9 6.6 %pad_maximum_fusion = bf16[4096,768]{1,0:T(8,128)(2,1)} fusion(bf16[1024,768]{1,0:T(8,128)(2,1)} %collective-permute-done.2, bf16[1024,768]{1,0:T(8,128)(2,1)} %collective-permute-done.1, bf16[1024,768]{1,0:T(8,128)(2,1)} %collective-permute-done, bf16[1024,768]{1,0:T(8,128)(2,1)} %param.13), kind=kLoop, calls=%fused_computation.6 | loop fusion | flops 25165824 | bytes 12582912 | tf_op jit(solution)/shard_map/concatenate | solution.py:217
  303.4 1.9 broadcast_in_dim.41.init_ref
  305.4 23.4 %shard_map.56 = f32[4,256,768]{2,1,0:T(8,128)S(1)} custom-call(s32[1]{0:T(128)} %bitcast.14.count_ref, s32[64]{0:T(128)S(1)} %get-tuple-element.42.order_ref, s32[64]{0:T(128)S(1)} %get-tuple-element.51.rows_ref, s32[64]{0:T(128)S(1)} %get-tuple-element.50.ks_ref, bf16[64,256,256]{2,1,0:T(8,128)(2,1)} %all-to-all-done.1.arrived_ref, ...), custom_call_target="tpu_custom_call" | custom-call | tf_op jit(solution)/shard_map/pallas_call | solution.py:187
  328.7 24.4 %all-to-all-done.arrived_ref = bf16[64,176,256]{2,1,0:T(8,128)(2,1)} async-done(((bf16[64,176,256]{2,1,0:T(8,128)(2,1)}), bf16[64,176,256]{2,1,0:T(8,128)(2,1)}, u32[]{:S(2)}, u32[]{:S(2)}) %all-to-all-start) | async-done | bytes 5767200 | tf_op jit(solution)/shard_map/all_to_all | solution.py:241
  353.1 6.4 %all-to-all-start.2 = ((bf16[64,80,256]{2,1,0:T(8,128)(2,1)}), bf16[64,80,256]{2,1,0:T(8,128)(2,1)}, u32[]{:S(2)}, u32[]{:S(2)}) async-start(bf16[64,80,256]{2,1,0:T(8,128)(2,1)} %gather_fusion.2), calls=%async_computation.2 | async-start | bytes 5242880 | tf_op jit(solution)/shard_map/all_to_all | solution.py:241
  360.2 2.0 sort.31
  362.3 0.2 slice.101.init_ref
  362.5 14.7 %shard_map.57.x_ref = f32[4,176,768]{2,1,0:T(8,128)S(1)} custom-call(s32[1]{0:T(128)} %bitcast.9.count_ref, s32[64]{0:T(128)S(1)} %get-tuple-element.40.order_ref, s32[64]{0:T(128)S(1)} %get-tuple-element.53.rows_ref, s32[64]{0:T(128)S(1)} %get-tuple-element.52.ks_ref, bf16[64,176,256]{2,1,0:T(8,128)(2,1)} %all-to-all-done.arrived_ref, ...), custom_call_target="tpu_custom_call" | custom-call | tf_op jit(solution)/shard_map/pallas_call | solution.py:187
  377.1 47.5 %shard_map.58 = f32[4,176,768]{2,1,0:T(8,128)S(1)} custom-call(f32[4,176,768]{2,1,0:T(8,128)S(1)} %shard_map.57.x_ref), custom_call_target="tpu_custom_call" | custom-call | tf_op jit(solution)/shard_map/pallas_call | solution.py:76
  424.6 0.0 copy-start
  424.6 1.3 copy-done
  426.0 1.0 slice.91.init_ref
  427.0 0.0 copy-start.1
  427.0 0.0 all-to-all-done.2.arrived_ref
  427.0 0.0 copy-start.2
  427.0 1.4 copy-done.2
  428.4 12.2 %shard_map.59.x_ref = f32[4,80,768]{2,1,0:T(8,128)S(1)} custom-call(s32[1]{0:T(128)} %bitcast.9.count_ref, s32[64]{0:T(128)S(1)} %get-tuple-element.40.order_ref, s32[64]{0:T(128)S(1)} %get-tuple-element.53.rows_ref, s32[64]{0:T(128)S(1)} %get-tuple-element.52.ks_ref, bf16[64,80,256]{2,1,0:T(8,128)(2,1)} %all-to-all-done.2.arrived_ref, ...), custom_call_target="tpu_custom_call" | custom-call | tf_op jit(solution)/shard_map/pallas_call | solution.py:187
  440.6 31.7 %shard_map.60 = f32[4,80,768]{2,1,0:T(8,128)S(1)} custom-call(f32[4,80,768]{2,1,0:T(8,128)S(1)} %shard_map.59.x_ref), custom_call_target="tpu_custom_call" | custom-call | tf_op jit(solution)/shard_map/pallas_call | solution.py:76
  472.3 0.0 copy-done.1
  472.3 2.0 pad_maximum_fusion.1
  (15 shorter events, 0.1 us)
Async XLA Ops:
  10.1 204.9 %all-to-all-start.1 = ((bf16[64,256,256]{2,1,0:T(8,128)(2,1)}), bf16[64,256,256]{2,1,0:T(8,128)(2,1)}, u32[]{:S(2)}, u32[]{:S(2)}) async-start(bf16[64,256,256]{2,1,0:T(8,128)(2,1)} %gather_fusion.1), calls=%async_computation.1 | async-start | bytes 16777216 | tf_op jit(solution)/shard_map/all_to_all | solution.py:241
  21.8 4.7 copy-start.4
  21.8 4.8 %copy-start.3 = (s32[128,2]{1,0:T(8,128)S(1)}, s32[128,2]{1,0:T(8,128)}, u32[]{:S(2)}) copy-start(s32[128,2]{1,0:T(8,128)} %constant.120.clone.1) | copy-start | bytes 3076
  215.0 138.1 %all-to-all-start = ((bf16[64,176,256]{2,1,0:T(8,128)(2,1)}), bf16[64,176,256]{2,1,0:T(8,128)(2,1)}, u32[]{:S(2)}, u32[]{:S(2)}) async-start(bf16[64,176,256]{2,1,0:T(8,128)(2,1)} %gather_fusion), calls=%async_computation | async-start | bytes 11534336 | tf_op jit(solution)/shard_map/all_to_all | solution.py:241
  223.8 7.0 %slice-start = ((bf16[48,256,256]{2,1,0:T(8,128)(2,1)}), bf16[48,80,256]{2,1,0:T(8,128)(2,1)S(1)}, s32[]{:S(2)}) async-start(bf16[48,256,256]{2,1,0:T(8,128)(2,1)} %param.9), calls=%async_computation.3 | async-start | bytes 3932160 | tf_op jit(solution)/shard_map/slice | solution.py:236
  223.9 38.1 %collective-permute-start = (bf16[1024,768]{1,0:T(8,128)(2,1)}, bf16[1024,768]{1,0:T(8,128)(2,1)}, u32[]{:S(2)}, u32[]{:S(2)}) collective-permute-start(bf16[1024,768]{1,0:T(8,128)(2,1)} %param.13), channel_id=1, source_target_pairs={{0,64},{64,128},{128,192},{192,0},{1,65},{65,129},{129,193},{193,1... | collective-permute-start | bytes 4718600 | tf_op jit(solution)/shard_map/ppermute | solution.py:214
  225.5 71.3 %collective-permute-start.1 = (bf16[1024,768]{1,0:T(8,128)(2,1)}, bf16[1024,768]{1,0:T(8,128)(2,1)}, u32[]{:S(2)}, u32[]{:S(2)}) collective-permute-start(bf16[1024,768]{1,0:T(8,128)(2,1)} %param.13), channel_id=1, source_target_pairs={{0,128},{64,192},{128,0},{192,64},{1,129},{65,193},{129,1},{193,65... | collective-permute-start | bytes 4718600 | tf_op jit(solution)/shard_map/ppermute | solution.py:214
  228.4 68.4 %collective-permute-start.2 = (bf16[1024,768]{1,0:T(8,128)(2,1)}, bf16[1024,768]{1,0:T(8,128)(2,1)}, u32[]{:S(2)}, u32[]{:S(2)}) collective-permute-start(bf16[1024,768]{1,0:T(8,128)(2,1)} %param.13), channel_id=1, source_target_pairs={{0,192},{64,0},{128,64},{192,128},{1,193},{65,1},{129,65},{193,129... | collective-permute-start | bytes 4718600 | tf_op jit(solution)/shard_map/ppermute | solution.py:214
  353.1 73.9 %all-to-all-start.2 = ((bf16[64,80,256]{2,1,0:T(8,128)(2,1)}), bf16[64,80,256]{2,1,0:T(8,128)(2,1)}, u32[]{:S(2)}, u32[]{:S(2)}) async-start(bf16[64,80,256]{2,1,0:T(8,128)(2,1)} %gather_fusion.2), calls=%async_computation.2 | async-start | bytes 5242880 | tf_op jit(solution)/shard_map/all_to_all | solution.py:241
  424.6 1.3 copy-start
  427.0 45.3 %copy-start.1 = (f32[4,176,768]{2,1,0:T(8,128)S(1)}, f32[4,176,768]{2,1,0:T(8,128)}, u32[]{:S(2)}) copy-start(f32[4,176,768]{2,1,0:T(8,128)} %copy-done) | copy-start | bytes 6488068
  427.0 1.4 copy-start.2

commit v13 on v12

--- a/solution.py
+++ b/solution.py
@@ -216,7 +216,7 @@
     ]
     gathered = jnp.concatenate(pieces, axis=0)
     panel_tiles = gathered.reshape(gathered.shape[0] // tile_side, tile_side, gathered.shape[1])
-    band = tile_side * 11 // 16
+    band = tile_side * 5 // 8
     picks = []
     for rank in range(most_slots):
         chunk_index = jnp.where(ranking == rank, target, wide_count)

time: 475 us -> 473 us (level); the launches traced: 474 us -> 465 us
  Pallas kernels: 310 us -> 297 us
    pallas_call x3, Pallas kernels: 50.2 us -> 37.8 us  [add_products(): pl.pallas_call(products_kernel, out_shape=jax.ShapeDtypeStruct(running.sh...]
  transfers between devices with their start and end apart: 6 -> 6, of which waited for: 3 -> 4; matrix products, arithmetic and copies ran while one was open for 6% -> 7% of each run, Pallas kernels for 56% -> 55%
where the time goes in v13:
time: 473 us; the launch traced here: 465 us
  Pallas kernels  297 us (63%)
  waiting for transfers between devices  85 us (18%)
  local copies, waits for them, and re-layouts  34.8 us (7%)
  starting transfers between devices  32.8 us (7%)
  other arithmetic  14.3 us (3%)
    pallas_call x1, Pallas kernels, swap_labels(): pl.pallas_call(functools.partial(label_kernel, n), out_shape=jax.ShapeDty...  181 us
    pallas_call x2, Pallas kernels, ring_sum(): pl.pallas_call(functools.partial(ring_sum_kernel, n), out_shape=jax.Shape...  77.7 us
    ppermute x3, waiting for transfers between devices, per_device(): lax.ppermute(panel, 'grp', [(j, (j + shift) % grp_count) for j in range(g...  60.3 us
    pallas_call x3, Pallas kernels, add_products(): pl.pallas_call(products_kernel, out_shape=jax.ShapeDtypeStruct(running.sh...  37.8 us
    all_to_all x3, starting transfers between devices, exchange(): lax.all_to_all(block, 'wide', split_axis=0, concat_axis=0, tiled=True)  26.8 us
    all_to_all x3, waiting for transfers between devices, exchange(): lax.all_to_all(block, 'wide', split_axis=0, concat_axis=0, tiled=True)  24.7 us
  transfers between devices with their start and end apart: 6, of which 4 were waited for; matrix products, arithmetic and copies ran while one was open for 7% of the time, Pallas kernels for 55%

profile of v13, /device:TPU:36, one launch (start us, length us, event | category | flops | bytes accessed | tf_op | source)
XLA Modules:
  0.0 465.1 jit_solution(9147634029095784595)
XLA Ops:
  0.0 0.9 select_reduce_fusion
  0.9 0.2 convert_reduce_fusion
  1.1 0.7 scatter_custom_fusion.2
  1.8 8.2 %gather_fusion.1 = bf16[64,256,256]{2,1,0:T(8,128)(2,1)} fusion(bf16[48,256,256]{2,1,0:T(8,128)(2,1)} %param.9, s32[1024]{0:T(1024)S(1)} %pad_clamp_fusion), kind=kCustom, calls=%fused_computation.1 | custom fusion | bytes 16777472 | tf_op jit(solution)/shard_map/jit(_take)/gather | solution.py:226
  10.1 11.7 %all-to-all-start.1 = ((bf16[64,256,256]{2,1,0:T(8,128)(2,1)}), bf16[64,256,256]{2,1,0:T(8,128)(2,1)}, u32[]{:S(2)}, u32[]{:S(2)}) async-start(bf16[64,256,256]{2,1,0:T(8,128)(2,1)} %gather_fusion.1), calls=%async_computation.1 | async-start | bytes 16777216 | tf_op jit(solution)/shard_map/all_to_all | solution.py:241
  21.8 0.0 copy-start.5
  21.8 0.0 copy-start.4
  21.8 4.3 slice.80
  26.1 0.0 copy-done.5
  26.1 0.1 copy.11
  26.2 0.0 copy-done.4
  26.2 0.8 scatter_fusion
  27.0 0.1 reshape.238
  27.1 0.7 scatter.33.lab_ref
  27.8 0.7 scatter_custom_fusion
  28.5 5.3 %gather_fusion = bf16[64,160,256]{2,1,0:T(8,128)(2,1)} fusion(bf16[48,160,256]{2,1,0:T(8,128)(2,1)} %slice.80, s32[1024]{0:T(1024)S(1)} %pad_clamp_fusion.1), kind=kCustom, calls=%fused_computation | custom fusion | bytes 10486016 | tf_op jit(solution)/shard_map/jit(_take)/gather | solution.py:227
  33.8 181.1 %shard_map.55 = s32[64,8,128]{2,1,0:T(8,128)} custom-call(s32[64,8,128]{2,1,0:T(8,128)} %scatter.33.lab_ref), custom_call_target="tpu_custom_call" | custom-call | tf_op jit(solution)/shard_map/pallas_call | solution.py:135
  215.0 0.0 all-to-all-done.1.arrived_ref
  215.0 8.8 %all-to-all-start = ((bf16[64,160,256]{2,1,0:T(8,128)(2,1)}), bf16[64,160,256]{2,1,0:T(8,128)(2,1)}, u32[]{:S(2)}, u32[]{:S(2)}) async-start(bf16[64,160,256]{2,1,0:T(8,128)(2,1)} %gather_fusion), calls=%async_computation | async-start | bytes 10485760 | tf_op jit(solution)/shard_map/all_to_all | solution.py:241
  223.8 0.0 slice-start
  223.8 1.7 collective-permute-start
  225.5 2.9 collective-permute-start.1
  228.4 1.4 collective-permute-start.2
  229.8 1.0 slice.81
  230.8 0.1 copy.13
  230.8 0.0 slice-done
  230.8 2.4 gather_fusion.2
  233.3 2.0 sort.32
  235.4 0.6 fusion.11
  236.6 25.4 %collective-permute-done = bf16[1024,768]{1,0:T(8,128)(2,1)} collective-permute-done((bf16[1024,768]{1,0:T(8,128)(2,1)}, bf16[1024,768]{1,0:T(8,128)(2,1)}, u32[]{:S(2)}, u32[]{:S(2)}) %collective-permute-start) | collective-permute-done | bytes 1572896 | tf_op jit(solution)/shard_map/ppermute | solution.py:214
  262.0 34.9 %collective-permute-done.1 = bf16[1024,768]{1,0:T(8,128)(2,1)} collective-permute-done((bf16[1024,768]{1,0:T(8,128)(2,1)}, bf16[1024,768]{1,0:T(8,128)(2,1)}, u32[]{:S(2)}, u32[]{:S(2)}) %collective-permute-start.1) | collective-permute-done | bytes 1572896 | tf_op jit(solution)/shard_map/ppermute | solution.py:214
  296.9 0.0 collective-permute-done.2
  296.9 6.6 %pad_maximum_fusion = bf16[4096,768]{1,0:T(8,128)(2,1)} fusion(bf16[1024,768]{1,0:T(8,128)(2,1)} %collective-permute-done.2, bf16[1024,768]{1,0:T(8,128)(2,1)} %collective-permute-done.1, bf16[1024,768]{1,0:T(8,128)(2,1)} %collective-permute-done, bf16[1024,768]{1,0:T(8,128)(2,1)} %param.13), kind=kLoop, calls=%fused_computation.6 | loop fusion | flops 25165824 | bytes 12582912 | tf_op jit(solution)/shard_map/concatenate | solution.py:217
  303.4 2.0 broadcast_in_dim.41.init_ref
  305.5 20.7 %shard_map.56 = f32[4,256,768]{2,1,0:T(8,128)S(1)} custom-call(s32[1]{0:T(128)} %bitcast.14.count_ref, s32[64]{0:T(128)S(1)} %get-tuple-element.42.order_ref, s32[64]{0:T(128)S(1)} %get-tuple-element.51.rows_ref, s32[64]{0:T(128)S(1)} %get-tuple-element.50.ks_ref, bf16[64,256,256]{2,1,0:T(8,128)(2,1)} %all-to-all-done.1.arrived_ref, ...), custom_call_target="tpu_custom_call" | custom-call | tf_op jit(solution)/shard_map/pallas_call | solution.py:187
  326.1 0.0 copy-start
  326.1 1.7 copy-done
  327.8 13.9 %all-to-all-done.arrived_ref = bf16[64,160,256]{2,1,0:T(8,128)(2,1)} async-done(((bf16[64,160,256]{2,1,0:T(8,128)(2,1)}), bf16[64,160,256]{2,1,0:T(8,128)(2,1)}, u32[]{:S(2)}, u32[]{:S(2)}) %all-to-all-start) | async-done | bytes 5242912 | tf_op jit(solution)/shard_map/all_to_all | solution.py:241
  341.7 6.3 %all-to-all-start.2 = ((bf16[64,96,256]{2,1,0:T(8,128)(2,1)}), bf16[64,96,256]{2,1,0:T(8,128)(2,1)S(1)}, u32[]{:S(2)}, u32[]{:S(2)}) async-start(bf16[64,96,256]{2,1,0:T(8,128)(2,1)} %gather_fusion.2), calls=%async_computation.2 | async-start | bytes 6291456 | tf_op jit(solution)/shard_map/all_to_all | solution.py:241
  348.6 2.1 sort.31
  350.7 1.7 slice.101.init_ref
  352.4 9.6 %shard_map.57.x_ref = f32[4,160,768]{2,1,0:T(8,128)S(1)} custom-call(s32[1]{0:T(128)} %bitcast.9.count_ref, s32[64]{0:T(128)S(1)} %get-tuple-element.40.order_ref, s32[64]{0:T(128)S(1)} %get-tuple-element.53.rows_ref, s32[64]{0:T(128)S(1)} %get-tuple-element.52.ks_ref, bf16[64,160,256]{2,1,0:T(8,128)(2,1)} %all-to-all-done.arrived_ref, ...), custom_call_target="tpu_custom_call" | custom-call | tf_op jit(solution)/shard_map/pallas_call | solution.py:187
  362.0 44.4 %shard_map.58 = f32[4,160,768]{2,1,0:T(8,128)S(1)} custom-call(f32[4,160,768]{2,1,0:T(8,128)S(1)} %shard_map.57.x_ref), custom_call_target="tpu_custom_call" | custom-call | tf_op jit(solution)/shard_map/pallas_call | solution.py:76
  406.4 0.0 copy-start.1
  406.4 1.3 copy-done.1
  407.7 2.4 slice.91.init_ref
  410.1 10.8 %all-to-all-done.2.arrived_ref = bf16[64,96,256]{2,1,0:T(8,128)(2,1)S(1)} async-done(((bf16[64,96,256]{2,1,0:T(8,128)(2,1)}), bf16[64,96,256]{2,1,0:T(8,128)(2,1)S(1)}, u32[]{:S(2)}, u32[]{:S(2)}) %all-to-all-start.2) | async-done | bytes 3145760 | tf_op jit(solution)/shard_map/all_to_all | solution.py:241
  420.9 0.0 copy-start.3
  420.9 1.3 copy-done.3
  422.2 7.5 %shard_map.59.x_ref = f32[4,96,768]{2,1,0:T(8,128)S(1)} custom-call(s32[1]{0:T(128)} %bitcast.9.count_ref, s32[64]{0:T(128)S(1)} %get-tuple-element.40.order_ref, s32[64]{0:T(128)S(1)} %get-tuple-element.53.rows_ref, s32[64]{0:T(128)S(1)} %get-tuple-element.52.ks_ref, bf16[64,96,256]{2,1,0:T(8,128)(2,1)S(1)} %all-to-all-done.2.arrived_ref, ...), custom_call_target="tpu_custom_call" | custom-call | tf_op jit(solution)/shard_map/pallas_call | solution.py:187
  429.7 0.0 copy-start.2
  429.7 33.4 %shard_map.60 = f32[4,96,768]{2,1,0:T(8,128)S(1)} custom-call(f32[4,96,768]{2,1,0:T(8,128)S(1)} %shard_map.59.x_ref), custom_call_target="tpu_custom_call" | custom-call | tf_op jit(solution)/shard_map/pallas_call | solution.py:76
  463.1 0.0 copy-done.2
  463.1 2.0 pad_maximum_fusion.1
  (15 shorter events, 0.1 us)
Async XLA Ops:
  10.1 204.9 %all-to-all-start.1 = ((bf16[64,256,256]{2,1,0:T(8,128)(2,1)}), bf16[64,256,256]{2,1,0:T(8,128)(2,1)}, u32[]{:S(2)}, u32[]{:S(2)}) async-start(bf16[64,256,256]{2,1,0:T(8,128)(2,1)} %gather_fusion.1), calls=%async_computation.1 | async-start | bytes 16777216 | tf_op jit(solution)/shard_map/all_to_all | solution.py:241
  21.8 4.3 copy-start.5
  21.8 4.4 copy-start.4
  215.0 126.8 %all-to-all-start = ((bf16[64,160,256]{2,1,0:T(8,128)(2,1)}), bf16[64,160,256]{2,1,0:T(8,128)(2,1)}, u32[]{:S(2)}, u32[]{:S(2)}) async-start(bf16[64,160,256]{2,1,0:T(8,128)(2,1)} %gather_fusion), calls=%async_computation | async-start | bytes 10485760 | tf_op jit(solution)/shard_map/all_to_all | solution.py:241
  223.8 7.0 %slice-start = ((bf16[48,256,256]{2,1,0:T(8,128)(2,1)}), bf16[48,96,256]{2,1,0:T(8,128)(2,1)S(1)}, s32[]{:S(2)}) async-start(bf16[48,256,256]{2,1,0:T(8,128)(2,1)} %param.9), calls=%async_computation.3 | async-start | bytes 4718592 | tf_op jit(solution)/shard_map/slice | solution.py:236
  223.8 38.2 %collective-permute-start = (bf16[1024,768]{1,0:T(8,128)(2,1)}, bf16[1024,768]{1,0:T(8,128)(2,1)}, u32[]{:S(2)}, u32[]{:S(2)}) collective-permute-start(bf16[1024,768]{1,0:T(8,128)(2,1)} %param.13), channel_id=1, source_target_pairs={{0,64},{64,128},{128,192},{192,0},{1,65},{65,129},{129,193},{193,1... | collective-permute-start | bytes 4718600 | tf_op jit(solution)/shard_map/ppermute | solution.py:214
  225.5 71.4 %collective-permute-start.1 = (bf16[1024,768]{1,0:T(8,128)(2,1)}, bf16[1024,768]{1,0:T(8,128)(2,1)}, u32[]{:S(2)}, u32[]{:S(2)}) collective-permute-start(bf16[1024,768]{1,0:T(8,128)(2,1)} %param.13), channel_id=1, source_target_pairs={{0,128},{64,192},{128,0},{192,64},{1,129},{65,193},{129,1},{193,65... | collective-permute-start | bytes 4718600 | tf_op jit(solution)/shard_map/ppermute | solution.py:214
  228.4 68.4 %collective-permute-start.2 = (bf16[1024,768]{1,0:T(8,128)(2,1)}, bf16[1024,768]{1,0:T(8,128)(2,1)}, u32[]{:S(2)}, u32[]{:S(2)}) collective-permute-start(bf16[1024,768]{1,0:T(8,128)(2,1)} %param.13), channel_id=1, source_target_pairs={{0,192},{64,0},{128,64},{192,128},{1,193},{65,1},{129,65},{193,129... | collective-permute-start | bytes 4718600 | tf_op jit(solution)/shard_map/ppermute | solution.py:214
  326.1 1.7 copy-start
  341.7 79.2 %all-to-all-start.2 = ((bf16[64,96,256]{2,1,0:T(8,128)(2,1)}), bf16[64,96,256]{2,1,0:T(8,128)(2,1)S(1)}, u32[]{:S(2)}, u32[]{:S(2)}) async-start(bf16[64,96,256]{2,1,0:T(8,128)(2,1)} %gather_fusion.2), calls=%async_computation.2 | async-start | bytes 6291456 | tf_op jit(solution)/shard_map/all_to_all | solution.py:241
  406.4 1.3 copy-start.1
  420.9 1.3 copy-start.3
  429.7 33.4 %copy-start.2 = (f32[4,160,768]{2,1,0:T(8,128)S(1)}, f32[4,160,768]{2,1,0:T(8,128)}, u32[]{:S(2)}) copy-start(f32[4,160,768]{2,1,0:T(8,128)} %copy-done.1) | copy-start | bytes 5898244

commit v14 on v11

--- a/solution.py
+++ b/solution.py
@@ -220,9 +220,8 @@
         ))
     first = jnp.take(tiles, picks[0], axis=0, mode="clip")
     upper_out = jnp.take(tiles[:, :band, :], picks[1], axis=0, mode="clip")
-    upper_out, packed = lax.optimization_barrier((upper_out, packed))
     packed = swap_labels(packed, wide_count)
-    upper_out, packed = lax.optimization_barrier((upper_out, packed))
+    first, packed = lax.optimization_barrier((first, packed))
     arrived_labels = packed[:, 0, :2 * most_slots].reshape(wide_count, most_slots, 2)
     held = panel.shape[0] // tile_side
     owner = arrived_labels[..., 1] // held

time: 472 us -> 483 us (1.023); the launches traced: 471 us -> 474 us
  waiting for transfers between devices: 78 us -> 262 us
  Pallas kernels: 309 us -> 131 us
    all_to_all x3, waiting for transfers between devices: 17.7 us -> 202 us  [exchange(): lax.all_to_all(block, 'wide', split_axis=0, concat_axis=0, tiled=True)]
    pallas_call x1, Pallas kernels: 181 us -> 19.4 us  [swap_labels(): pl.pallas_call(functools.partial(label_kernel, n), out_shape=jax.ShapeDty...]
    pallas_call x3, Pallas kernels: 51.2 us -> 29.8 us  [add_products(): pl.pallas_call(products_kernel, out_shape=jax.ShapeDtypeStruct(running.sh...]
  transfers between devices with their start and end apart: 6 -> 6, of which waited for: 4 -> 5; matrix products, arithmetic and copies ran while one was open for 7% -> 7% of each run, Pallas kernels for 56% -> 15%
where the time goes in v14:
time: 483 us; the launch traced here: 474 us
  waiting for transfers between devices  262 us (54%)
  Pallas kernels  131 us (27%)
  local copies, waits for them, and re-layouts  35.9 us (7%)
  starting transfers between devices  29 us (6%)
  other arithmetic  15 us (3%)
    all_to_all x3, waiting for transfers between devices, exchange(): lax.all_to_all(block, 'wide', split_axis=0, concat_axis=0, tiled=True)  202 us
    pallas_call x2, Pallas kernels, ring_sum(): pl.pallas_call(functools.partial(ring_sum_kernel, n), out_shape=jax.Shape...  81.4 us
    ppermute x3, waiting for transfers between devices, per_device(): lax.ppermute(panel, 'grp', [(j, (j + shift) % grp_count) for j in range(g...  60.2 us
    pallas_call x3, Pallas kernels, add_products(): pl.pallas_call(products_kernel, out_shape=jax.ShapeDtypeStruct(running.sh...  29.8 us
    all_to_all x3, starting transfers between devices, exchange(): lax.all_to_all(block, 'wide', split_axis=0, concat_axis=0, tiled=True)  23.2 us
    pallas_call x1, Pallas kernels, swap_labels(): pl.pallas_call(functools.partial(label_kernel, n), out_shape=jax.ShapeDty...  19.4 us
  transfers between devices with their start and end apart: 6, of which 5 were waited for; matrix products, arithmetic and copies ran while one was open for 7% of the time, Pallas kernels for 15%

profile of v14, /device:TPU:36, one launch (start us, length us, event | category | flops | bytes accessed | tf_op | source)
XLA Modules:
  0.0 474.3 jit_solution(8218858434411205015)
XLA Ops:
  0.0 0.9 select_reduce_fusion
  0.9 0.2 convert_reduce_fusion
  1.1 0.7 pad_add_fusion
  1.8 0.1 copy.11
  1.8 0.8 copy.17
  2.7 0.7 scatter_fusion
  3.4 0.1 reshape.238
  3.5 0.7 scatter.33.lab_ref
  4.2 19.4 %shard_map.55 = s32[64,8,128]{2,1,0:T(8,128)} custom-call(s32[64,8,128]{2,1,0:T(8,128)} %scatter.33.lab_ref), custom_call_target="tpu_custom_call" | custom-call | tf_op jit(solution)/shard_map/pallas_call | solution.py:130
  23.6 0.7 scatter_custom_fusion
  24.4 8.4 %gather_fusion = bf16[64,256,256]{2,1,0:T(8,128)(2,1)} fusion(bf16[48,256,256]{2,1,0:T(8,128)(2,1)} %param.9, s32[1024]{0:T(1024)S(1)} %pad_clamp_fusion.1), kind=kCustom, calls=%fused_computation | custom fusion | bytes 16777472 | tf_op jit(solution)/shard_map/jit(_take)/gather | solution.py:221
  32.8 10.0 %all-to-all-start.1 = ((bf16[64,256,256]{2,1,0:T(8,128)(2,1)}), bf16[64,256,256]{2,1,0:T(8,128)(2,1)}, u32[]{:S(2)}, u32[]{:S(2)}) async-start(bf16[64,256,256]{2,1,0:T(8,128)(2,1)} %gather_fusion), calls=%async_computation.1 | async-start | bytes 16777216 | tf_op jit(solution)/shard_map/all_to_all | solution.py:235
  42.8 4.3 slice.85
  47.0 0.7 scatter_custom_fusion.2
  47.8 5.3 %gather_fusion.1 = bf16[64,160,256]{2,1,0:T(8,128)(2,1)} fusion(bf16[48,160,256]{2,1,0:T(8,128)(2,1)} %slice.85, s32[1024]{0:T(1024)S(1)} %pad_clamp_fusion), kind=kCustom, calls=%fused_computation.1 | custom fusion | bytes 10486016 | tf_op jit(solution)/shard_map/jit(_take)/gather | solution.py:222
  53.1 175.8 %all-to-all-done.1.arrived_ref = bf16[64,256,256]{2,1,0:T(8,128)(2,1)} async-done(((bf16[64,256,256]{2,1,0:T(8,128)(2,1)}), bf16[64,256,256]{2,1,0:T(8,128)(2,1)}, u32[]{:S(2)}, u32[]{:S(2)}) %all-to-all-start.1) | async-done | bytes 8388640 | tf_op jit(solution)/shard_map/all_to_all | solution.py:235
  229.0 6.4 %all-to-all-start = ((bf16[64,160,256]{2,1,0:T(8,128)(2,1)}), bf16[64,160,256]{2,1,0:T(8,128)(2,1)}, u32[]{:S(2)}, u32[]{:S(2)}) async-start(bf16[64,160,256]{2,1,0:T(8,128)(2,1)} %gather_fusion.1), calls=%async_computation | async-start | bytes 10485760 | tf_op jit(solution)/shard_map/all_to_all | solution.py:235
  235.4 0.0 slice-start
  235.4 1.6 collective-permute-start
  237.0 2.9 collective-permute-start.1
  239.9 1.3 collective-permute-start.2
  241.3 1.0 slice.80
  242.2 0.1 copy.13
  242.3 0.0 slice-done
  242.3 2.4 gather_fusion.2
  244.8 2.1 sort.32
  246.9 0.7 fusion.11
  248.2 25.3 %collective-permute-done = bf16[1024,768]{1,0:T(8,128)(2,1)} collective-permute-done((bf16[1024,768]{1,0:T(8,128)(2,1)}, bf16[1024,768]{1,0:T(8,128)(2,1)}, u32[]{:S(2)}, u32[]{:S(2)}) %collective-permute-start) | collective-permute-done | bytes 1572896 | tf_op jit(solution)/shard_map/ppermute | solution.py:209
  273.5 34.9 %collective-permute-done.1 = bf16[1024,768]{1,0:T(8,128)(2,1)} collective-permute-done((bf16[1024,768]{1,0:T(8,128)(2,1)}, bf16[1024,768]{1,0:T(8,128)(2,1)}, u32[]{:S(2)}, u32[]{:S(2)}) %collective-permute-start.1) | collective-permute-done | bytes 1572896 | tf_op jit(solution)/shard_map/ppermute | solution.py:209
  308.4 0.0 collective-permute-done.2
  308.4 6.4 %pad_maximum_fusion = bf16[4096,768]{1,0:T(8,128)(2,1)} fusion(bf16[1024,768]{1,0:T(8,128)(2,1)} %collective-permute-done.2, bf16[1024,768]{1,0:T(8,128)(2,1)} %collective-permute-done.1, bf16[1024,768]{1,0:T(8,128)(2,1)} %collective-permute-done, bf16[1024,768]{1,0:T(8,128)(2,1)} %param.13), kind=kLoop, calls=%fused_computation.6 | loop fusion | flops 25165824 | bytes 12582912 | tf_op jit(solution)/shard_map/concatenate | solution.py:212
  314.8 2.0 broadcast_in_dim.41.init_ref
  316.9 18.0 %shard_map.56 = f32[4,256,768]{2,1,0:T(8,128)S(1)} custom-call(s32[1]{0:T(128)} %bitcast.15.count_ref, s32[64]{0:T(128)S(1)} %get-tuple-element.37.order_ref, s32[64]{0:T(128)S(1)} %get-tuple-element.44.rows_ref, s32[64]{0:T(128)S(1)} %get-tuple-element.43.ks_ref, bf16[64,256,256]{2,1,0:T(8,128)(2,1)} %all-to-all-done.1.arrived_ref, ...), custom_call_target="tpu_custom_call" | custom-call | tf_op jit(solution)/shard_map/pallas_call | solution.py:182
  334.8 0.0 copy-start
  334.8 1.7 copy-done
  336.6 16.2 %all-to-all-done.arrived_ref = bf16[64,160,256]{2,1,0:T(8,128)(2,1)} async-done(((bf16[64,160,256]{2,1,0:T(8,128)(2,1)}), bf16[64,160,256]{2,1,0:T(8,128)(2,1)}, u32[]{:S(2)}, u32[]{:S(2)}) %all-to-all-start) | async-done | bytes 5242912 | tf_op jit(solution)/shard_map/all_to_all | solution.py:235
  352.7 6.8 %all-to-all-start.2 = ((bf16[64,96,256]{2,1,0:T(8,128)(2,1)}), bf16[64,96,256]{2,1,0:T(8,128)(2,1)S(1)}, u32[]{:S(2)}, u32[]{:S(2)}) async-start(bf16[64,96,256]{2,1,0:T(8,128)(2,1)} %gather_fusion.2), calls=%async_computation.2 | async-start | bytes 6291456 | tf_op jit(solution)/shard_map/all_to_all | solution.py:235
  360.2 2.1 sort.31
  362.3 1.7 slice.101.init_ref
  364.0 6.8 %shard_map.57.x_ref = f32[4,160,768]{2,1,0:T(8,128)S(1)} custom-call(s32[1]{0:T(128)} %bitcast.9.count_ref, s32[64]{0:T(128)S(1)} %get-tuple-element.36.order_ref, s32[64]{0:T(128)S(1)} %get-tuple-element.49.rows_ref, s32[64]{0:T(128)S(1)} %get-tuple-element.48.ks_ref, bf16[64,160,256]{2,1,0:T(8,128)(2,1)} %all-to-all-done.arrived_ref, ...), custom_call_target="tpu_custom_call" | custom-call | tf_op jit(solution)/shard_map/pallas_call | solution.py:182
  370.8 47.8 %shard_map.58 = f32[4,160,768]{2,1,0:T(8,128)S(1)} custom-call(f32[4,160,768]{2,1,0:T(8,128)S(1)} %shard_map.57.x_ref), custom_call_target="tpu_custom_call" | custom-call | tf_op jit(solution)/shard_map/pallas_call | solution.py:71
  418.6 0.0 copy-start.1
  418.6 1.3 copy-done.1
  419.9 2.4 slice.91.init_ref
  422.3 10.1 %all-to-all-done.2.arrived_ref = bf16[64,96,256]{2,1,0:T(8,128)(2,1)S(1)} async-done(((bf16[64,96,256]{2,1,0:T(8,128)(2,1)}), bf16[64,96,256]{2,1,0:T(8,128)(2,1)S(1)}, u32[]{:S(2)}, u32[]{:S(2)}) %all-to-all-start.2) | async-done | bytes 3145760 | tf_op jit(solution)/shard_map/all_to_all | solution.py:235
  432.4 0.0 copy-start.3
  432.4 1.3 copy-done.3
  433.7 5.0 %shard_map.59.x_ref = f32[4,96,768]{2,1,0:T(8,128)S(1)} custom-call(s32[1]{0:T(128)} %bitcast.9.count_ref, s32[64]{0:T(128)S(1)} %get-tuple-element.36.order_ref, s32[64]{0:T(128)S(1)} %get-tuple-element.49.rows_ref, s32[64]{0:T(128)S(1)} %get-tuple-element.48.ks_ref, bf16[64,96,256]{2,1,0:T(8,128)(2,1)S(1)} %all-to-all-done.2.arrived_ref, ...), custom_call_target="tpu_custom_call" | custom-call | tf_op jit(solution)/shard_map/pallas_call | solution.py:182
  438.7 0.0 copy-start.2
  438.7 33.6 %shard_map.60 = f32[4,96,768]{2,1,0:T(8,128)S(1)} custom-call(f32[4,96,768]{2,1,0:T(8,128)S(1)} %shard_map.59.x_ref), custom_call_target="tpu_custom_call" | custom-call | tf_op jit(solution)/shard_map/pallas_call | solution.py:71
  472.3 0.0 copy-done.2
  472.3 2.0 pad_maximum_fusion.1
  (14 shorter events, 0.1 us)
Async XLA Ops:
  32.8 196.2 %all-to-all-start.1 = ((bf16[64,256,256]{2,1,0:T(8,128)(2,1)}), bf16[64,256,256]{2,1,0:T(8,128)(2,1)}, u32[]{:S(2)}, u32[]{:S(2)}) async-start(bf16[64,256,256]{2,1,0:T(8,128)(2,1)} %gather_fusion), calls=%async_computation.1 | async-start | bytes 16777216 | tf_op jit(solution)/shard_map/all_to_all | solution.py:235
  229.0 123.8 %all-to-all-start = ((bf16[64,160,256]{2,1,0:T(8,128)(2,1)}), bf16[64,160,256]{2,1,0:T(8,128)(2,1)}, u32[]{:S(2)}, u32[]{:S(2)}) async-start(bf16[64,160,256]{2,1,0:T(8,128)(2,1)} %gather_fusion.1), calls=%async_computation | async-start | bytes 10485760 | tf_op jit(solution)/shard_map/all_to_all | solution.py:235
  235.4 6.9 %slice-start = ((bf16[48,256,256]{2,1,0:T(8,128)(2,1)}), bf16[48,96,256]{2,1,0:T(8,128)(2,1)S(1)}, s32[]{:S(2)}) async-start(bf16[48,256,256]{2,1,0:T(8,128)(2,1)} %param.9), calls=%async_computation.3 | async-start | bytes 4718592 | tf_op jit(solution)/shard_map/slice | solution.py:230
  235.4 38.1 %collective-permute-start = (bf16[1024,768]{1,0:T(8,128)(2,1)}, bf16[1024,768]{1,0:T(8,128)(2,1)}, u32[]{:S(2)}, u32[]{:S(2)}) collective-permute-start(bf16[1024,768]{1,0:T(8,128)(2,1)} %param.13), channel_id=1, source_target_pairs={{0,64},{64,128},{128,192},{192,0},{1,65},{65,129},{129,193},{193,1... | collective-permute-start | bytes 4718600 | tf_op jit(solution)/shard_map/ppermute | solution.py:209
  237.0 71.3 %collective-permute-start.1 = (bf16[1024,768]{1,0:T(8,128)(2,1)}, bf16[1024,768]{1,0:T(8,128)(2,1)}, u32[]{:S(2)}, u32[]{:S(2)}) collective-permute-start(bf16[1024,768]{1,0:T(8,128)(2,1)} %param.13), channel_id=1, source_target_pairs={{0,128},{64,192},{128,0},{192,64},{1,129},{65,193},{129,1},{193,65... | collective-permute-start | bytes 4718600 | tf_op jit(solution)/shard_map/ppermute | solution.py:209
  239.9 68.4 %collective-permute-start.2 = (bf16[1024,768]{1,0:T(8,128)(2,1)}, bf16[1024,768]{1,0:T(8,128)(2,1)}, u32[]{:S(2)}, u32[]{:S(2)}) collective-permute-start(bf16[1024,768]{1,0:T(8,128)(2,1)} %param.13), channel_id=1, source_target_pairs={{0,192},{64,0},{128,64},{192,128},{1,193},{65,1},{129,65},{193,129... | collective-permute-start | bytes 4718600 | tf_op jit(solution)/shard_map/ppermute | solution.py:209
  334.8 1.8 copy-start
  352.7 79.7 %all-to-all-start.2 = ((bf16[64,96,256]{2,1,0:T(8,128)(2,1)}), bf16[64,96,256]{2,1,0:T(8,128)(2,1)S(1)}, u32[]{:S(2)}, u32[]{:S(2)}) async-start(bf16[64,96,256]{2,1,0:T(8,128)(2,1)} %gather_fusion.2), calls=%async_computation.2 | async-start | bytes 6291456 | tf_op jit(solution)/shard_map/all_to_all | solution.py:235
  418.6 1.3 copy-start.1
  432.4 1.3 copy-start.3
  438.7 33.6 %copy-start.2 = (f32[4,160,768]{2,1,0:T(8,128)S(1)}, f32[4,160,768]{2,1,0:T(8,128)}, u32[]{:S(2)}) copy-start(f32[4,160,768]{2,1,0:T(8,128)} %copy-done.1) | copy-start | bytes 5898244

commit v15 on v11

--- a/solution.py
+++ b/solution.py
@@ -148,7 +148,7 @@
 
 
 def products_kernel(count_ref, order_ref, rows_ref, ks_ref, arrived_ref, panel_ref, init_ref, out_ref):
-    out_ref[...] = init_ref[...]
+    del init_ref
     columns = panel_ref.shape[2]
     side = arrived_ref.shape[2]
 
@@ -184,6 +184,7 @@
         out_shape=jax.ShapeDtypeStruct(running.shape, jnp.float32),
         in_specs=[smem, smem, smem, smem, vmem, vmem, vmem],
         out_specs=vmem,
+        input_output_aliases={6: 0},
         compiler_params=pltpu.CompilerParams(vmem_limit_bytes=48 * 1024 * 1024),
     )(*schedule, arrived, panel_tiles, running)
 

time: 472 us -> 471 us (level)
  waiting for transfers between devices: 78 us -> 88.5 us
  local copies, waits for them, and re-layouts: 34.9 us -> 28.6 us
  Pallas kernels: 309 us -> 304 us
    all_to_all x3, waiting for transfers between devices: 17.7 us -> 28.2 us  [exchange(): lax.all_to_all(block, 'wide', split_axis=0, concat_axis=0, tiled=True)]
    pallas_call x3, Pallas kernels: 51.2 us -> 43.9 us  [add_products(): pl.pallas_call(products_kernel, out_shape=jax.ShapeDtypeStruct(running.sh...]
  transfers between devices with their start and end apart: 6 -> 6, of which waited for: 4 -> 4; matrix products, arithmetic and copies ran while one was open for 7% -> 6% of each run, Pallas kernels for 56% -> 55%
where the time goes in v15:
time: 471 us; the launch traced here: 469 us
  Pallas kernels  304 us (65%)
  waiting for transfers between devices  88.5 us (19%)
  starting transfers between devices  32.9 us (7%)
  local copies, waits for them, and re-layouts  28.6 us (6%)
  other arithmetic  14.3 us (3%)
    pallas_call x1, Pallas kernels, swap_labels(): pl.pallas_call(functools.partial(label_kernel, n), out_shape=jax.ShapeDty...  181 us
    pallas_call x2, Pallas kernels, ring_sum(): pl.pallas_call(functools.partial(ring_sum_kernel, n), out_shape=jax.Shape...  78.7 us
    ppermute x3, waiting for transfers between devices, per_device(): lax.ppermute(panel, 'grp', [(j, (j + shift) % grp_count) for j in range(g...  60.3 us
    pallas_call x3, Pallas kernels, add_products(): pl.pallas_call(products_kernel, out_shape=jax.ShapeDtypeStruct(running.sh...  43.9 us
    all_to_all x3, waiting for transfers between devices, exchange(): lax.all_to_all(block, 'wide', split_axis=0, concat_axis=0, tiled=True)  28.2 us
    all_to_all x3, starting transfers between devices, exchange(): lax.all_to_all(block, 'wide', split_axis=0, concat_axis=0, tiled=True)  27 us
  transfers between devices with their start and end apart: 6, of which 4 were waited for; matrix products, arithmetic and copies ran while one was open for 6% of the time, Pallas kernels for 55%

profile of v15, /device:TPU:36, one launch (start us, length us, event | category | flops | bytes accessed | tf_op | source)
XLA Modules:
  0.0 469.5 jit_solution(6663574066754247487)
XLA Ops:
  0.0 0.9 select_reduce_fusion
  0.9 0.2 convert_reduce_fusion
  1.1 0.7 scatter_custom_fusion.2
  1.8 8.3 %gather_fusion.1 = bf16[64,256,256]{2,1,0:T(8,128)(2,1)} fusion(bf16[48,256,256]{2,1,0:T(8,128)(2,1)} %param.9, s32[1024]{0:T(1024)S(1)} %pad_clamp_fusion), kind=kCustom, calls=%fused_computation.1 | custom fusion | bytes 16777472 | tf_op jit(solution)/shard_map/jit(_take)/gather | solution.py:222
  10.1 11.7 %all-to-all-start.1 = ((bf16[64,256,256]{2,1,0:T(8,128)(2,1)}), bf16[64,256,256]{2,1,0:T(8,128)(2,1)}, u32[]{:S(2)}, u32[]{:S(2)}) async-start(bf16[64,256,256]{2,1,0:T(8,128)(2,1)} %gather_fusion.1), calls=%async_computation.1 | async-start | bytes 16777216 | tf_op jit(solution)/shard_map/all_to_all | solution.py:237
  21.8 0.0 copy-start.4
  21.8 0.0 copy-start.3
  21.8 4.3 slice.80
  26.1 0.0 copy-done.4
  26.2 0.1 copy.14
  26.2 0.0 copy-done.3
  26.3 0.8 scatter_fusion
  27.0 0.1 reshape.238
  27.1 0.7 scatter.33.lab_ref
  27.8 0.7 scatter_custom_fusion
  28.6 5.3 %gather_fusion = bf16[64,160,256]{2,1,0:T(8,128)(2,1)} fusion(bf16[48,160,256]{2,1,0:T(8,128)(2,1)} %slice.80, s32[1024]{0:T(1024)S(1)} %pad_clamp_fusion.1), kind=kCustom, calls=%fused_computation | custom fusion | bytes 10486016 | tf_op jit(solution)/shard_map/jit(_take)/gather | solution.py:223
  33.8 181.1 %shard_map.55 = s32[64,8,128]{2,1,0:T(8,128)} custom-call(s32[64,8,128]{2,1,0:T(8,128)} %scatter.33.lab_ref), custom_call_target="tpu_custom_call" | custom-call | tf_op jit(solution)/shard_map/pallas_call | solution.py:130
  215.0 0.0 all-to-all-done.1.arrived_ref
  215.0 8.8 %all-to-all-start = ((bf16[64,160,256]{2,1,0:T(8,128)(2,1)}), bf16[64,160,256]{2,1,0:T(8,128)(2,1)}, u32[]{:S(2)}, u32[]{:S(2)}) async-start(bf16[64,160,256]{2,1,0:T(8,128)(2,1)} %gather_fusion), calls=%async_computation | async-start | bytes 10485760 | tf_op jit(solution)/shard_map/all_to_all | solution.py:237
  223.9 0.0 slice-start
  223.9 1.7 collective-permute-start
  225.5 2.9 collective-permute-start.1
  228.4 1.4 collective-permute-start.2
  229.8 1.0 slice.81
  230.8 0.1 copy.16
  230.9 0.0 slice-done
  230.9 2.4 gather_fusion.2
  233.4 2.0 sort.32
  235.4 0.6 fusion.11
  236.6 25.4 %collective-permute-done = bf16[1024,768]{1,0:T(8,128)(2,1)} collective-permute-done((bf16[1024,768]{1,0:T(8,128)(2,1)}, bf16[1024,768]{1,0:T(8,128)(2,1)}, u32[]{:S(2)}, u32[]{:S(2)}) %collective-permute-start) | collective-permute-done | bytes 1572896 | tf_op jit(solution)/shard_map/ppermute | solution.py:210
  262.0 34.9 %collective-permute-done.1 = bf16[1024,768]{1,0:T(8,128)(2,1)} collective-permute-done((bf16[1024,768]{1,0:T(8,128)(2,1)}, bf16[1024,768]{1,0:T(8,128)(2,1)}, u32[]{:S(2)}, u32[]{:S(2)}) %collective-permute-start.1) | collective-permute-done | bytes 1572896 | tf_op jit(solution)/shard_map/ppermute | solution.py:210
  296.9 0.0 collective-permute-done.2
  296.9 6.6 %pad_maximum_fusion = bf16[4096,768]{1,0:T(8,128)(2,1)} fusion(bf16[1024,768]{1,0:T(8,128)(2,1)} %collective-permute-done.2, bf16[1024,768]{1,0:T(8,128)(2,1)} %collective-permute-done.1, bf16[1024,768]{1,0:T(8,128)(2,1)} %collective-permute-done, bf16[1024,768]{1,0:T(8,128)(2,1)} %param.13), kind=kLoop, calls=%fused_computation.6 | loop fusion | flops 25165824 | bytes 12582912 | tf_op jit(solution)/shard_map/concatenate | solution.py:213
  303.4 0.2 broadcast_in_dim.41.init_ref
  303.7 20.6 %shard_map.56 = f32[4,256,768]{2,1,0:T(8,128)S(1)} custom-call(s32[1]{0:T(128)} %bitcast.14.count_ref, s32[64]{0:T(128)S(1)} %get-tuple-element.42.order_ref, s32[64]{0:T(128)S(1)} %get-tuple-element.51.rows_ref, s32[64]{0:T(128)S(1)} %get-tuple-element.50.ks_ref, bf16[64,256,256]{2,1,0:T(8,128)(2,1)} %all-to-all-done.1.arrived_ref, ...), custom_call_target="tpu_custom_call", output_to_operand_aliasing={{}: (6, {})} | custom-call | tf_op jit(solution)/shard_map/pallas_call | solution.py:182
  324.3 17.4 %all-to-all-done.arrived_ref = bf16[64,160,256]{2,1,0:T(8,128)(2,1)} async-done(((bf16[64,160,256]{2,1,0:T(8,128)(2,1)}), bf16[64,160,256]{2,1,0:T(8,128)(2,1)}, u32[]{:S(2)}, u32[]{:S(2)}) %all-to-all-start) | async-done | bytes 5242912 | tf_op jit(solution)/shard_map/all_to_all | solution.py:237
  341.8 6.4 %all-to-all-start.2 = ((bf16[64,96,256]{2,1,0:T(8,128)(2,1)}), bf16[64,96,256]{2,1,0:T(8,128)(2,1)}, u32[]{:S(2)}, u32[]{:S(2)}) async-start(bf16[64,96,256]{2,1,0:T(8,128)(2,1)} %gather_fusion.2), calls=%async_computation.2 | async-start | bytes 6291456 | tf_op jit(solution)/shard_map/all_to_all | solution.py:237
  348.8 2.1 sort.31
  350.9 0.2 slice.101.init_ref
  351.0 12.3 %shard_map.57.x_ref = f32[4,160,768]{2,1,0:T(8,128)S(1)} custom-call(s32[1]{0:T(128)} %bitcast.9.count_ref, s32[64]{0:T(128)S(1)} %get-tuple-element.40.order_ref, s32[64]{0:T(128)S(1)} %get-tuple-element.53.rows_ref, s32[64]{0:T(128)S(1)} %get-tuple-element.52.ks_ref, ...), custom_call_target="tpu_custom_call", output_to_operand_aliasing={{}: (6, {})} | custom-call | tf_op jit(solution)/shard_map/pallas_call | solution.py:182
  363.3 44.5 %shard_map.58 = f32[4,160,768]{2,1,0:T(8,128)S(1)} custom-call(f32[4,160,768]{2,1,0:T(8,128)S(1)} %shard_map.57.x_ref), custom_call_target="tpu_custom_call" | custom-call | tf_op jit(solution)/shard_map/pallas_call | solution.py:71
  407.8 0.0 copy-start.1
  407.8 1.3 copy-done.1
  409.1 1.1 slice.91.init_ref
  410.3 10.8 %all-to-all-done.2.arrived_ref = bf16[64,96,256]{2,1,0:T(8,128)(2,1)} async-done(((bf16[64,96,256]{2,1,0:T(8,128)(2,1)}), bf16[64,96,256]{2,1,0:T(8,128)(2,1)}, u32[]{:S(2)}, u32[]{:S(2)}) %all-to-all-start.2) | async-done | bytes 3145760 | tf_op jit(solution)/shard_map/all_to_all | solution.py:237
  421.0 0.0 copy-start
  421.1 1.3 copy-done
  422.3 10.9 %shard_map.59.x_ref = f32[4,96,768]{2,1,0:T(8,128)S(1)} custom-call(s32[1]{0:T(128)} %bitcast.9.count_ref, s32[64]{0:T(128)S(1)} %get-tuple-element.40.order_ref, s32[64]{0:T(128)S(1)} %get-tuple-element.53.rows_ref, s32[64]{0:T(128)S(1)} %get-tuple-element.52.ks_ref, ...), custom_call_target="tpu_custom_call", output_to_operand_aliasing={{}: (6, {})} | custom-call | tf_op jit(solution)/shard_map/pallas_call | solution.py:182
  433.2 0.0 copy-start.2
  433.3 34.3 %shard_map.60 = f32[4,96,768]{2,1,0:T(8,128)S(1)} custom-call(f32[4,96,768]{2,1,0:T(8,128)S(1)} %shard_map.59.x_ref), custom_call_target="tpu_custom_call" | custom-call | tf_op jit(solution)/shard_map/pallas_call | solution.py:71
  467.5 0.0 copy-done.2
  467.5 2.0 pad_maximum_fusion.1
  (15 shorter events, 0.1 us)
Async XLA Ops:
  10.1 204.9 %all-to-all-start.1 = ((bf16[64,256,256]{2,1,0:T(8,128)(2,1)}), bf16[64,256,256]{2,1,0:T(8,128)(2,1)}, u32[]{:S(2)}, u32[]{:S(2)}) async-start(bf16[64,256,256]{2,1,0:T(8,128)(2,1)} %gather_fusion.1), calls=%async_computation.1 | async-start | bytes 16777216 | tf_op jit(solution)/shard_map/all_to_all | solution.py:237
  21.8 4.3 copy-start.4
  21.8 4.4 copy-start.3
  215.0 126.8 %all-to-all-start = ((bf16[64,160,256]{2,1,0:T(8,128)(2,1)}), bf16[64,160,256]{2,1,0:T(8,128)(2,1)}, u32[]{:S(2)}, u32[]{:S(2)}) async-start(bf16[64,160,256]{2,1,0:T(8,128)(2,1)} %gather_fusion), calls=%async_computation | async-start | bytes 10485760 | tf_op jit(solution)/shard_map/all_to_all | solution.py:237
  223.9 7.0 %slice-start = ((bf16[48,256,256]{2,1,0:T(8,128)(2,1)}), bf16[48,96,256]{2,1,0:T(8,128)(2,1)S(1)}, s32[]{:S(2)}) async-start(bf16[48,256,256]{2,1,0:T(8,128)(2,1)} %param.9), calls=%async_computation.3 | async-start | bytes 4718592 | tf_op jit(solution)/shard_map/slice | solution.py:232
  223.9 38.1 %collective-permute-start = (bf16[1024,768]{1,0:T(8,128)(2,1)}, bf16[1024,768]{1,0:T(8,128)(2,1)}, u32[]{:S(2)}, u32[]{:S(2)}) collective-permute-start(bf16[1024,768]{1,0:T(8,128)(2,1)} %param.13), channel_id=1, source_target_pairs={{0,64},{64,128},{128,192},{192,0},{1,65},{65,129},{129,193},{193,1... | collective-permute-start | bytes 4718600 | tf_op jit(solution)/shard_map/ppermute | solution.py:210
  225.5 71.4 %collective-permute-start.1 = (bf16[1024,768]{1,0:T(8,128)(2,1)}, bf16[1024,768]{1,0:T(8,128)(2,1)}, u32[]{:S(2)}, u32[]{:S(2)}) collective-permute-start(bf16[1024,768]{1,0:T(8,128)(2,1)} %param.13), channel_id=1, source_target_pairs={{0,128},{64,192},{128,0},{192,64},{1,129},{65,193},{129,1},{193,65... | collective-permute-start | bytes 4718600 | tf_op jit(solution)/shard_map/ppermute | solution.py:210
  228.4 68.4 %collective-permute-start.2 = (bf16[1024,768]{1,0:T(8,128)(2,1)}, bf16[1024,768]{1,0:T(8,128)(2,1)}, u32[]{:S(2)}, u32[]{:S(2)}) collective-permute-start(bf16[1024,768]{1,0:T(8,128)(2,1)} %param.13), channel_id=1, source_target_pairs={{0,192},{64,0},{128,64},{192,128},{1,193},{65,1},{129,65},{193,129... | collective-permute-start | bytes 4718600 | tf_op jit(solution)/shard_map/ppermute | solution.py:210
  341.8 79.3 %all-to-all-start.2 = ((bf16[64,96,256]{2,1,0:T(8,128)(2,1)}), bf16[64,96,256]{2,1,0:T(8,128)(2,1)}, u32[]{:S(2)}, u32[]{:S(2)}) async-start(bf16[64,96,256]{2,1,0:T(8,128)(2,1)} %gather_fusion.2), calls=%async_computation.2 | async-start | bytes 6291456 | tf_op jit(solution)/shard_map/all_to_all | solution.py:237
  407.8 1.3 copy-start.1
  421.0 1.3 copy-start
  433.2 34.3 %copy-start.2 = (f32[4,160,768]{2,1,0:T(8,128)S(1)}, f32[4,160,768]{2,1,0:T(8,128)}, u32[]{:S(2)}) copy-start(f32[4,160,768]{2,1,0:T(8,128)} %copy-done.1) | copy-start | bytes 5898244
